TPU v7x, 32 devices: a whole 2x2x4 slice. The times are simulated.
32 devices in a mesh: row: 4 (over z), col: 8 (over y, x, core).
Axes of the slice: x: 2, y: 2, z: 4, core: 2. Of those that a mesh axis runs over, the one named last changes fastest.
Arguments:
- slab: float32 [4096, 8192], P('row', 'col'), may hold values from -6 to 6
- owner: int32 [2], replicated, may hold values from 0 to 7, as said below
- leaf_reflectors: float32 [2, 4096, 2048], P(None, 'row', 'col'), may hold values from -0.1875 to 0.1875
- leaf_factors: float32 [2, 1024, 2048], P(None, 'row', 'col'), as said below
- tree_reflectors: float32 [2, 2, 1024, 256], P(None, None, 'row'), may hold values from -0.25 to 0.25
- tree_mixers: float32 [2, 2, 1024, 256], P(None, None, 'row'), may hold values from -0.1875 to 0.1875
Outputs:
- updated: float32 [4096, 8192], P('row', 'col')
Inputs may be any that keep to these rules, and one draw needn't show every extreme that they name: `owner`: the 2 owners are distinct column blocks, and one of them is the last column block. Every 256 x 256 block of leaf_factors is upper triangular with diagonal entries from 1 to 2.
All inputs are finite; a program needn't handle non-finite values.
Results may differ from a plain program's by a relative error of at most 0.00015.
Values sent between devices are 32-bit elements; how exact they have to be, the bound alone decides.
No kernel may reach another device: no remote copies, remote signals or barrier semaphores. Data moves between devices by JAX's collectives and lax.ppermute only.
A program may use at most 64 MiB of HBM per device.

v0:
```python
import jax
import jax.numpy as jnp
from jax import lax
from jax.sharding import PartitionSpec as P

HIGH = lax.Precision.HIGHEST
LEADING = (((0,), (0,)), ((), ()))


def from_partner(shard, axis, apart):
    return lax.ppermute(shard, axis, [(i, i ^ 1 << apart) for i in range(lax.axis_size(axis))])


def apply_leaf(matrix, received, first_row, rows_dev):
    reflect_rows = received[first_row:rows_dev]
    factor_block = received[rows_dev:]
    lower = matrix[first_row:]
    projected = lax.dot_general(
        reflect_rows, lower, LEADING, precision=HIGH, preferred_element_type=jnp.float32
    )
    scaled = lax.dot_general(
        factor_block, projected, LEADING, precision=HIGH, preferred_element_type=jnp.float32
    )
    lower = lower - jnp.dot(
        reflect_rows, scaled, precision=HIGH, preferred_element_type=jnp.float32
    )
    return jnp.concatenate([matrix[:first_row], lower], axis=0)


def tree_step(matrix, halves, mixers, first_row, width, levels):
    top_rows = matrix[first_row : first_row + width]
    for level_no in range(levels):
        partial_sum = lax.dot_general(
            halves[level_no], top_rows, LEADING, precision=HIGH, preferred_element_type=jnp.float32
        )
        partner_sum = from_partner(partial_sum, "row", level_no)
        top_rows = top_rows - jnp.dot(
            mixers[level_no],
            partial_sum + partner_sum,
            precision=HIGH,
            preferred_element_type=jnp.float32,
        )
    return lax.dynamic_update_slice_in_dim(matrix, top_rows, first_row, 0)


def shards(slab, owner, leaf_reflectors, leaf_factors, tree_reflectors, tree_mixers):
    rows_dev = slab.shape[0]
    width = leaf_factors.shape[1]
    panels = owner.shape[0]
    levels = lax.axis_size("row").bit_length() - 1
    is_owner = (lax.axis_index("col") == owner).astype(jnp.float32)
    stacked = jnp.concatenate([leaf_reflectors, leaf_factors], axis=1) * is_owner[:, None, None]
    received = lax.psum(stacked, "col")
    panel_blocks = [received[panel_no] for panel_no in range(panels)]
    matrix = slab
    for panel_no in range(panels):
        matrix = apply_leaf(matrix, panel_blocks[panel_no], panel_no * width, rows_dev)
        matrix = tree_step(
            matrix,
            tree_reflectors[panel_no],
            tree_mixers[panel_no],
            panel_no * width,
            width,
            levels,
        )
    return matrix


def solution(mesh):
    return jax.shard_map(
        shards,
        mesh=mesh,
        in_specs=(
            P("row", "col"),
            P(),
            P(None, "row", "col"),
            P(None, "row", "col"),
            P(None, None, "row", None),
            P(None, None, "row", None),
        ),
        out_specs=P("row", "col"),
        check_vma=False,
    )
```

profile of v0, /device:TPU:0, one launch (start us, length us, event | category | flops | bytes accessed | tf_op | source)
XLA Modules:
  0.0 220.8 jit_solution(15570357751311416546)
XLA Ops:
  6.5 0.0 all-reduce.2.cloned.1.call-start
  6.5 0.7 compare_convert_fusion
  7.2 3.5 %maximum_multiply_fusion = f32[2,1280,256]{2,1,0:T(8,128)} fusion(f32[2,256,256]{2,1,0:T(8,128)} %param.9, f32[2,1024,256]{2,1,0:T(8,128)} %param.8, f32[2]{0:T(128)S(1)} %compare_convert_fusion), kind=kLoop, calls=%fused_computation.4 | loop fusion | flops 1310720 | bytes 5242888 | tf_op jit(solution)/shard_map/mul | solution.py:52
  10.7 0.0 all-reduce.2.cloned.1.call-update
  10.7 67.5 %all-reduce.2.cloned.1.call-done = f32[2,1280,256]{2,1,0:T(8,128)} async-done(((f32[2,1280,256]{2,1,0:T(8,128)}), f32[2,1280,256]{2,1,0:T(8,128)}) %all-reduce.2.cloned.1.call-update) | async-done | bytes 2621456 | tf_op jit(solution)/shard_map/psum | solution.py:53
  78.2 6.2 %fusion.11 = f32[256,1024]{1,0:T(8,128)S(1)} fusion(f32[1024,1024]{1,0:T(8,128)} %param.6, f32[2,1280,256]{2,1,0:T(8,128)} %all-reduce.2.cloned.1.call-done), kind=kOutput, calls=%fused_computation.24 | convolution fusion | flops 3221225472 | bytes 6291456 | tf_op jit(solution)/shard_map/dot_general | solution.py:18
  84.4 2.0 fusion.15
  86.4 0.0 copy-done
  86.4 0.0 copy-done.1
  86.4 0.0 copy-start.2
  86.4 3.8 %convolution_subtract_fusion = f32[1024,1024]{1,0:T(8,128)S(1)} fusion(f32[1024,1024]{1,0:T(8,128)S(1)} %copy-done, f32[256,1024]{1,0:T(8,128)S(1)} %fusion.15, f32[2,1280,256]{2,1,0:T(8,128)S(1)} %copy-done.1), kind=kOutput, calls=%fused_computation.5 | convolution fusion | flops 3222274048 | bytes 10485760 | tf_op jit(solution)/shard_map/dot_general | solution.py:24
  90.2 1.9 convolution_bitcast_fusion.7
  92.1 1.6 collective-permute-start
  93.7 2.7 %fusion = f32[256,1024]{1,0:T(8,128)S(1)} fusion(f32[1024,1024]{1,0:T(8,128)S(1)} %convolution_subtract_fusion, f32[2,1280,256]{2,1,0:T(8,128)S(1)} %copy-done.1), kind=kOutput, calls=%fused_computation.2 | convolution fusion | flops 2415919104 | bytes 4980736 | tf_op jit(solution)/shard_map/dot_general | solution.py:18
  96.4 1.0 fusion.14
  97.4 0.0 copy-start.3
  97.5 3.0 %slice_subtract_fusion = f32[768,1024]{1,0:T(8,128)S(1)} fusion(f32[1024,1024]{1,0:T(8,128)S(1)} %convolution_subtract_fusion, f32[256,1024]{1,0:T(8,128)S(1)} %fusion.14, f32[2,1280,256]{2,1,0:T(8,128)S(1)} %copy-done.1), kind=kOutput, calls=%fused_computation.1 | convolution fusion | flops 2416705536 | bytes 8126464 | tf_op jit(solution)/shard_map/dot_general | solution.py:24
  100.5 1.8 convolution_bitcast_fusion.3
  102.3 0.6 collective-permute-start.2
  102.9 15.4 %collective-permute-done = f32[256,1024]{0,1:T(8,128)S(1)} collective-permute-done((f32[256,1024]{0,1:T(8,128)S(1)}, f32[256,1024]{0,1:T(8,128)S(1)}, u32[]{:S(2)}, u32[]{:S(2)}) %collective-permute-start) | collective-permute-done | bytes 1048608 | tf_op jit(solution)/shard_map/ppermute | solution.py:11
  118.3 1.2 fusion.2
  119.4 1.9 convolution_bitcast_fusion.5
  121.3 2.5 %collective-permute-start.1 = (f32[256,1024]{0,1:T(8,128)S(1)}, f32[256,1024]{0,1:T(8,128)S(1)}, u32[]{:S(2)}, u32[]{:S(2)}) collective-permute-start(f32[256,1024]{0,1:T(8,128)S(1)} %convolution_bitcast_fusion.5), channel_id=1, source_target_pairs={{0,16},{8,24},{16,0},{24,8},{1,17},{9,25},{17,1},{25,9},{2,18},{10... | collective-permute-start | bytes 3145736 | tf_op jit(solution)/shard_map/ppermute | solution.py:11
  123.8 34.6 %collective-permute-done.2 = f32[256,1024]{0,1:T(8,128)S(1)} collective-permute-done((f32[256,1024]{0,1:T(8,128)S(1)}, f32[256,1024]{0,1:T(8,128)S(1)}, u32[]{:S(2)}, u32[]{:S(2)}) %collective-permute-start.2) | collective-permute-done | bytes 1048608 | tf_op jit(solution)/shard_map/ppermute | solution.py:11
  158.4 1.1 fusion.4
  159.5 1.8 convolution_bitcast_fusion.1
  161.3 0.1 collective-permute-start.3
  161.4 31.2 %collective-permute-done.1 = f32[256,1024]{0,1:T(8,128)S(1)} collective-permute-done((f32[256,1024]{0,1:T(8,128)S(1)}, f32[256,1024]{0,1:T(8,128)S(1)}, u32[]{:S(2)}, u32[]{:S(2)}) %collective-permute-start.1) | collective-permute-done | bytes 1048608 | tf_op jit(solution)/shard_map/ppermute | solution.py:11
  192.6 1.2 fusion.3
  193.8 2.6 %pad_maximum_fusion = f32[1024,1024]{1,0:T(8,128)} fusion(f32[768,1024]{1,0:T(8,128)S(1)} %slice_subtract_fusion, f32[256,1024]{1,0:T(8,128)S(1)} %fusion.3), kind=kLoop, calls=%fused_computation | loop fusion | flops 1048576 | bytes 8388608 | tf_op jit(solution)/shard_map/concatenate | solution.py:27
  196.4 15.4 %collective-permute-done.3 = f32[256,1024]{0,1:T(8,128)S(1)} collective-permute-done((f32[256,1024]{0,1:T(8,128)S(1)}, f32[256,1024]{0,1:T(8,128)S(1)}, u32[]{:S(2)}, u32[]{:S(2)}) %collective-permute-start.3) | collective-permute-done | bytes 1048608 | tf_op jit(solution)/shard_map/ppermute | solution.py:11
  211.9 2.1 fusion.6
  (4 shorter events, 0.0 us)
Async XLA Ops:
  6.5 71.7 %all-reduce.2.cloned.1.call-start = ((), (), s32[]{:S(2)}) async-start(), calls=%async_computation | async-start | bytes 5242880 | tf_op jit(solution)/shard_map/psum | solution.py:53
  78.2 8.2 %copy-start = (f32[1024,1024]{1,0:T(8,128)S(1)}, f32[1024,1024]{1,0:T(8,128)}, u32[]{:S(2)}) copy-start(f32[1024,1024]{1,0:T(8,128)} %param.6) | copy-start | bytes 12582916
  78.2 8.2 %copy-start.1 = (f32[2,1280,256]{2,1,0:T(8,128)S(1)}, f32[2,1280,256]{2,1,0:T(8,128)}, u32[]{:S(2)}) copy-start(f32[2,1280,256]{2,1,0:T(8,128)} %all-reduce.2.cloned.1.call-done) | copy-start | bytes 7864324
  86.4 3.8 %copy-start.2 = (f32[2,2,256,256]{3,2,1,0:T(8,128)S(1)}, f32[2,2,256,256]{3,2,1,0:T(8,128)}, u32[]{:S(2)}) copy-start(f32[2,2,256,256]{3,2,1,0:T(8,128)} %param.10) | copy-start | bytes 3145732
  92.1 26.2 %collective-permute-start = (f32[256,1024]{0,1:T(8,128)S(1)}, f32[256,1024]{0,1:T(8,128)S(1)}, u32[]{:S(2)}, u32[]{:S(2)}) collective-permute-start(f32[256,1024]{0,1:T(8,128)S(1)} %convolution_bitcast_fusion.7), channel_id=1, source_target_pairs={{0,8},{8,0},{16,24},{24,16},{1,9},{9,1},{17,25},{25,17},{2,10},{10... | collective-permute-start | bytes 3145736 | tf_op jit(solution)/shard_map/ppermute | solution.py:11
  97.4 20.8 %copy-start.3 = (f32[2,2,256,256]{3,2,1,0:T(8,128)S(1)}, f32[2,2,256,256]{3,2,1,0:T(8,128)}, u32[]{:S(2)}) copy-start(f32[2,2,256,256]{3,2,1,0:T(8,128)} %param.11) | copy-start | bytes 3145732
  102.3 56.1 %collective-permute-start.2 = (f32[256,1024]{0,1:T(8,128)S(1)}, f32[256,1024]{0,1:T(8,128)S(1)}, u32[]{:S(2)}, u32[]{:S(2)}) collective-permute-start(f32[256,1024]{0,1:T(8,128)S(1)} %convolution_bitcast_fusion.3), channel_id=1, source_target_pairs={{0,8},{8,0},{16,24},{24,16},{1,9},{9,1},{17,25},{25,17},{2,10},{10... | collective-permute-start | bytes 3145736 | tf_op jit(solution)/shard_map/ppermute | solution.py:11
  121.3 71.3 %collective-permute-start.1 = (f32[256,1024]{0,1:T(8,128)S(1)}, f32[256,1024]{0,1:T(8,128)S(1)}, u32[]{:S(2)}, u32[]{:S(2)}) collective-permute-start(f32[256,1024]{0,1:T(8,128)S(1)} %convolution_bitcast_fusion.5), channel_id=1, source_target_pairs={{0,16},{8,24},{16,0},{24,8},{1,17},{9,25},{17,1},{25,9},{2,18},{10... | collective-permute-start | bytes 3145736 | tf_op jit(solution)/shard_map/ppermute | solution.py:11
  161.3 50.5 %collective-permute-start.3 = (f32[256,1024]{0,1:T(8,128)S(1)}, f32[256,1024]{0,1:T(8,128)S(1)}, u32[]{:S(2)}, u32[]{:S(2)}) collective-permute-start(f32[256,1024]{0,1:T(8,128)S(1)} %convolution_bitcast_fusion.1), channel_id=1, source_target_pairs={{0,16},{8,24},{16,0},{24,8},{1,17},{9,25},{17,1},{25,9},{2,18},{10... | collective-permute-start | bytes 3145736 | tf_op jit(solution)/shard_map/ppermute | solution.py:11
Sparse Core Ops, SparseCore 0:
  10.8 67.3 all-reduce.1
where the time goes:
time: 221 us
  waiting for transfers between devices  164 us (74%)
  matrix products  31.7 us (14%)
  between operations  13.5 us (6%)
  other arithmetic  6.76 us (3%)
  starting transfers between devices  4.7 us (2%)
    ppermute x4, waiting for transfers between devices, from_partner(): lax.ppermute(shard, axis, [(i, i ^ 1 << apart) for i in range(lax.axis_si...  96.6 us
    psum x1, waiting for transfers between devices, shards(): received = lax.psum(stacked, 'col')  67.5 us
    dot_general x2, matrix products, apply_leaf(): lax.dot_general(reflect_rows, lower, LEADING, precision=HIGH, preferred_e...  8.91 us
    dot_general x4, matrix products, tree_step(): lax.dot_general(halves[level_no], top_rows, LEADING, precision=HIGH, pref...  7.35 us
    dot_general x2, matrix products, apply_leaf(): jnp.dot(reflect_rows, scaled, precision=HIGH, preferred_element_type=jnp....  6.81 us
    dot_general x4, matrix products, tree_step(): jnp.dot(mixers[level_no], partial_sum + partner_sum, precision=HIGH, pref...  5.55 us
    ppermute x4, starting transfers between devices, from_partner(): lax.ppermute(shard, axis, [(i, i ^ 1 << apart) for i in range(lax.axis_si...  4.69 us
  transfers between devices with their start and end apart: 5, of which 5 were waited for; matrix products, arithmetic and copies ran while one was open for 8% of the time, Pallas kernels for 0%

commit v1 on v0

v1 whole, which is shorter than its diff:
```python
import jax
import jax.numpy as jnp
from jax import lax
from jax.sharding import PartitionSpec as P

PRECISION = lax.Precision.HIGH
LEADING = (((0,), (0,)), ((), ()))
CHUNKS = 4


def dot(a, b):
    return jnp.dot(a, b, precision=PRECISION, preferred_element_type=jnp.float32)


def dot_t(a, b):
    return lax.dot_general(a, b, LEADING, precision=PRECISION, preferred_element_type=jnp.float32)


def from_partner(shard, apart):
    return lax.ppermute(shard, "row", [(i, i ^ 1 << apart) for i in range(lax.axis_size("row"))])


def swap_cores(shard):
    return lax.ppermute(shard, "col", [(i, i ^ 1) for i in range(lax.axis_size("col"))])


def broadcast_halves(half_0, half_1, owner):
    size = lax.axis_size("col")
    me = lax.axis_index("col")
    first = me % 2 == 0
    arrived = swap_cores(jnp.where(first, half_1, half_0))
    current = jnp.where(me % 2 == owner % 2, jnp.where(first, half_0, half_1), arrived)
    bits = [1 << k for k in range(1, size.bit_length() - 1)]
    turned = bits[len(bits) // 2 :] + bits[: len(bits) // 2]
    for even_bit, odd_bit in zip(bits, turned):
        pairs = [(i, i ^ (odd_bit if i % 2 else even_bit)) for i in range(size)]
        arrived = lax.ppermute(current, "col", pairs)
        bit = jnp.where(first, even_bit, odd_bit)
        current = jnp.where((me ^ owner) & bit == 0, current, arrived)
    other = swap_cores(current)
    return jnp.where(first, current, other), jnp.where(first, other, current)


def broadcast_panel(reflectors, factors, owner, first_row):
    rows = reflectors.shape[0] - first_row
    width = factors.shape[0]
    middle = first_row + rows // 2
    half_0 = jnp.concatenate([reflectors[first_row:middle], factors[: width // 2]], axis=0)
    half_1 = jnp.concatenate([reflectors[middle:], factors[width // 2 :]], axis=0)
    half_0, half_1 = broadcast_halves(half_0, half_1, owner)
    block = jnp.concatenate([half_0[: rows // 2], half_1[: rows // 2]], axis=0)
    factor = jnp.concatenate([half_0[rows // 2 :], half_1[rows // 2 :]], axis=0)
    return block, factor


def shards(slab, owner, leaf_reflectors, leaf_factors, tree_reflectors, tree_mixers):
    rows_dev, columns = slab.shape
    width = leaf_factors.shape[1]
    panels = owner.shape[0]
    levels = lax.axis_size("row").bit_length() - 1
    step = columns // CHUNKS
    lower = slab
    finished = []
    for panel_no in range(panels):
        reflect_rows, factor = broadcast_panel(
            leaf_reflectors[panel_no], leaf_factors[panel_no], owner[panel_no], panel_no * width
        )
        scaled = dot_t(factor, dot_t(reflect_rows, lower))
        top = lower[:width] - dot(reflect_rows[:width], scaled)
        lower = lower[width:] - dot(reflect_rows[width:], scaled)
        pieces = []
        for chunk in range(CHUNKS):
            piece = top[:, chunk * step : (chunk + 1) * step]
            for level_no in range(levels):
                partial_sum = dot_t(tree_reflectors[panel_no, level_no], piece)
                both = partial_sum + from_partner(partial_sum, level_no)
                piece = piece - dot(tree_mixers[panel_no, level_no], both)
            pieces.append(piece)
        finished.append(jnp.concatenate(pieces, axis=1))
    return jnp.concatenate(finished + [lower], axis=0)


def solution(mesh):
    return jax.shard_map(
        shards,
        mesh=mesh,
        in_specs=(
            P("row", "col"),
            P(),
            P(None, "row", "col"),
            P(None, "row", "col"),
            P(None, None, "row", None),
            P(None, None, "row", None),
        ),
        out_specs=P("row", "col"),
        check_vma=False,
    )
```

time: 221 us -> 186 us (0.84)
  waiting for transfers between devices: 164 us -> 118 us
  starting transfers between devices: 4.7 us -> 32.4 us
  matrix products: 31.7 us -> 20.8 us
  between operations: 13.5 us -> 5.39 us
  local copies, waits for them, and re-layouts: 0.02 us -> 3.29 us
    psum x1 -> x0, waiting for transfers between devices: 67.5 us -> none  [shards(): received = lax.psum(stacked, 'col')]
    ppermute x4 -> x24, starting transfers between devices: 4.69 us -> 32.4 us  [the longest x16 22.9 us: from_partner(): lax.ppermute(shard, 'row', [(i, i ^ 1 << apart) for i in range(lax.axis_s...]
    ppermute x4 -> x24, waiting for transfers between devices: 96.6 us -> 118 us  [the longest x16 96.7 us: from_partner(): lax.ppermute(shard, 'row', [(i, i ^ 1 << apart) for i in range(lax.axis_s...]
    dot_general x14 -> x40, matrix products: 31.7 us -> 20.8 us  [the longest x20 11.4 us: dot_t(): lax.dot_general(a, b, LEADING, precision=PRECISION, preferred_element_typ...]
    mul x1 -> x0, other arithmetic: 3.5 us -> none  [shards(): jnp.concatenate([leaf_reflectors, leaf_factors], axis=1)]
    slice x0 -> x12, local copies, waits for them, and re-layouts: none -> 3.27 us  [the longest x1 1.28 us: broadcast_panel(): factors[:width // 2]]
    select_n x0 -> x10, other arithmetic: none -> 2.98 us  [the longest x4 1.34 us: broadcast_halves(): current = jnp.where((me ^ owner) & bit == 0, current, arrived)]
  transfers between devices with their start and end apart: 5 -> 24, of which waited for: 5 -> 18; matrix products, arithmetic and copies ran while one was open for 8% -> 7% of each run, Pallas kernels for 0% -> 0%
where the time goes in v1:
time: 186 us
  waiting for transfers between devices  118 us (63%)
  starting transfers between devices  32.4 us (17%)
  matrix products  20.8 us (11%)
  other arithmetic  5.58 us (3%)
  between operations  5.39 us (3%)
  local copies, waits for them, and re-layouts  3.29 us (2%)
    ppermute x16, waiting for transfers between devices, from_partner(): lax.ppermute(shard, 'row', [(i, i ^ 1 << apart) for i in range(lax.axis_s...  96.7 us
    ppermute x16, starting transfers between devices, from_partner(): lax.ppermute(shard, 'row', [(i, i ^ 1 << apart) for i in range(lax.axis_s...  22.9 us
    ppermute x4, waiting for transfers between devices, broadcast_halves(): arrived = lax.ppermute(current, 'col', pairs)  19.5 us
    dot_general x20, matrix products, dot_t(): lax.dot_general(a, b, LEADING, precision=PRECISION, preferred_element_typ...  11.4 us
    dot_general x20, matrix products, dot(): jnp.dot(a, b, precision=PRECISION, preferred_element_type=jnp.float32)  9.4 us
    ppermute x4, starting transfers between devices, broadcast_halves(): arrived = lax.ppermute(current, 'col', pairs)  8.66 us
  transfers between devices with their start and end apart: 24, of which 18 were waited for; matrix products, arithmetic and copies ran while one was open for 7% of the time, Pallas kernels for 0%

profile of v1, /device:TPU:0, one launch (start us, length us, event | category | flops | bytes accessed | tf_op | source)
XLA Modules:
  0.0 185.6 jit_solution(10432024117414062979)
XLA Ops:
  7.7 3.0 %collective-permute-start.13 = (f32[512,256]{1,0:T(8,128)S(1)}, f32[512,256]{1,0:T(8,128)}, u32[]{:S(2)}, u32[]{:S(2)}) collective-permute-start(f32[512,256]{1,0:T(8,128)S(1)} %select_select_fusion.1), channel_id=1, source_target_pairs={{0,2},{1,5},{2,0},{3,7},{4,6},{5,1},{6,4},{7,3},{8,10},{9,13},{10,... | collective-permute-start | bytes 1572872 | tf_op jit(solution)/shard_map/ppermute | solution.py:37
  13.2 4.7 %collective-permute-done.13 = f32[512,256]{1,0:T(8,128)} collective-permute-done((f32[512,256]{1,0:T(8,128)S(1)}, f32[512,256]{1,0:T(8,128)}, u32[]{:S(2)}, u32[]{:S(2)}) %collective-permute-start.13) | collective-permute-done | bytes 524320 | tf_op jit(solution)/shard_map/ppermute | solution.py:37
  19.1 2.1 %collective-permute-start.14 = (f32[512,256]{1,0:T(8,128)S(1)}, f32[512,256]{1,0:T(8,128)S(1)}, u32[]{:S(2)}, u32[]{:S(2)}) collective-permute-start(f32[512,256]{1,0:T(8,128)S(1)} %broadcast_select_fusion.4), channel_id=1, source_target_pairs={{0,4},{1,3},{2,6},{3,1},{4,0},{5,7},{6,2},{7,5},{8,12},{9,11},{10,... | collective-permute-start | bytes 1572872 | tf_op jit(solution)/shard_map/ppermute | solution.py:37
  21.2 6.4 %collective-permute-done.1 = f32[640,256]{1,0:T(8,128)S(1)} collective-permute-done((f32[640,256]{1,0:T(8,128)S(1)}, f32[640,256]{1,0:T(8,128)S(1)}, u32[]{:S(2)}, u32[]{:S(2)}) %collective-permute-start.1) | collective-permute-done | bytes 655392 | tf_op jit(solution)/shard_map/ppermute | solution.py:37
  27.6 3.4 %collective-permute-start.2 = (f32[640,256]{1,0:T(8,128)S(1)}, f32[640,256]{1,0:T(8,128)S(1)}, u32[]{:S(2)}, u32[]{:S(2)}) collective-permute-start(f32[640,256]{1,0:T(8,128)S(1)} %broadcast_select_fusion), channel_id=1, source_target_pairs={{0,4},{1,3},{2,6},{3,1},{4,0},{5,7},{6,2},{7,5},{8,12},{9,11},{10,... | collective-permute-start | bytes 1966088 | tf_op jit(solution)/shard_map/ppermute | solution.py:37
  31.2 8.4 %collective-permute-done.2 = f32[640,256]{1,0:T(8,128)S(1)} collective-permute-done((f32[640,256]{1,0:T(8,128)S(1)}, f32[640,256]{1,0:T(8,128)S(1)}, u32[]{:S(2)}, u32[]{:S(2)}) %collective-permute-start.2) | collective-permute-done | bytes 655392 | tf_op jit(solution)/shard_map/ppermute | solution.py:37
  40.0 1.9 %collective-permute-done.3 = f32[640,256]{1,0:T(8,128)S(1)} collective-permute-done((f32[640,256]{1,0:T(8,128)S(1)}, f32[640,256]{1,0:T(8,128)S(1)}, u32[]{:S(2)}, u32[]{:S(2)}) %collective-permute-start.3) | collective-permute-done | bytes 655392 | tf_op jit(solution)/shard_map/ppermute | solution.py:24
  42.1 2.1 %fusion.16 = f32[256,1024]{1,0:T(8,128)S(1)} fusion(f32[1024,1024]{1,0:T(8,128)S(1)} %copy-done.2, f32[512,256]{1,0:T(8,128)S(1)} %slice.242, f32[512,256]{1,0:T(8,128)S(1)} %slice.241), kind=kOutput, calls=%fused_computation.53 | convolution fusion | flops 1610874880 | bytes 6291456 | tf_op jit(solution)/shard_map/dot_general | solution.py:16
  48.7 1.7 fusion.23
  53.9 1.6 collective-permute-start.4
  56.9 1.6 collective-permute-start.8
  60.5 2.6 %collective-permute-done.4 = f32[256,256]{0,1:T(8,128)S(1)} collective-permute-done((f32[256,256]{0,1:T(8,128)S(1)}, f32[256,256]{0,1:T(8,128)S(1)}, u32[]{:S(2)}, u32[]{:S(2)}) %collective-permute-start.4) | collective-permute-done | bytes 262176 | tf_op jit(solution)/shard_map/ppermute | solution.py:20
  65.0 3.7 %collective-permute-done.6 = f32[256,256]{0,1:T(8,128)S(1)} collective-permute-done((f32[256,256]{0,1:T(8,128)S(1)}, f32[256,256]{0,1:T(8,128)S(1)}, u32[]{:S(2)}, u32[]{:S(2)}) %collective-permute-start.6) | collective-permute-done | bytes 262176 | tf_op jit(solution)/shard_map/ppermute | solution.py:20
  71.4 2.9 %collective-permute-done.8 = f32[256,256]{0,1:T(8,128)S(1)} collective-permute-done((f32[256,256]{0,1:T(8,128)S(1)}, f32[256,256]{0,1:T(8,128)S(1)}, u32[]{:S(2)}, u32[]{:S(2)}) %collective-permute-start.8) | collective-permute-done | bytes 262176 | tf_op jit(solution)/shard_map/ppermute | solution.py:20
  76.2 3.7 %collective-permute-done.10 = f32[256,256]{0,1:T(8,128)S(1)} collective-permute-done((f32[256,256]{0,1:T(8,128)S(1)}, f32[256,256]{0,1:T(8,128)S(1)}, u32[]{:S(2)}, u32[]{:S(2)}) %collective-permute-start.10) | collective-permute-done | bytes 262176 | tf_op jit(solution)/shard_map/ppermute | solution.py:20
  79.9 2.6 %collective-permute-start.5 = (f32[256,256]{0,1:T(8,128)S(1)}, f32[256,256]{0,1:T(8,128)S(1)}, u32[]{:S(2)}, u32[]{:S(2)}) collective-permute-start(f32[256,256]{0,1:T(8,128)S(1)} %convolution_bitcast_fusion.29), channel_id=1, source_target_pairs={{0,16},{8,24},{16,0},{24,8},{1,17},{9,25},{17,1},{25,9},{2,18},{10... | collective-permute-start | bytes 786440 | tf_op jit(solution)/shard_map/ppermute | solution.py:20
  83.7 7.5 %collective-permute-done.16 = f32[256,256]{0,1:T(8,128)S(1)} collective-permute-done((f32[256,256]{0,1:T(8,128)S(1)}, f32[256,256]{0,1:T(8,128)S(1)}, u32[]{:S(2)}, u32[]{:S(2)}) %collective-permute-start.16) | collective-permute-done | bytes 262176 | tf_op jit(solution)/shard_map/ppermute | solution.py:20
  91.2 1.7 collective-permute-start.7
  93.2 9.2 %collective-permute-done.18 = f32[256,256]{0,1:T(8,128)S(1)} collective-permute-done((f32[256,256]{0,1:T(8,128)S(1)}, f32[256,256]{0,1:T(8,128)S(1)}, u32[]{:S(2)}, u32[]{:S(2)}) %collective-permute-start.18) | collective-permute-done | bytes 262176 | tf_op jit(solution)/shard_map/ppermute | solution.py:20
  102.4 1.7 collective-permute-start.9
  105.2 2.9 %collective-permute-done.20 = f32[256,256]{0,1:T(8,128)S(1)} collective-permute-done((f32[256,256]{0,1:T(8,128)S(1)}, f32[256,256]{0,1:T(8,128)S(1)}, u32[]{:S(2)}, u32[]{:S(2)}) %collective-permute-start.20) | collective-permute-done | bytes 262176 | tf_op jit(solution)/shard_map/ppermute | solution.py:20
  108.1 1.7 collective-permute-start.11
  110.1 3.2 %collective-permute-done.22 = f32[256,256]{0,1:T(8,128)S(1)} collective-permute-done((f32[256,256]{0,1:T(8,128)S(1)}, f32[256,256]{0,1:T(8,128)S(1)}, u32[]{:S(2)}, u32[]{:S(2)}) %collective-permute-start.22) | collective-permute-done | bytes 262176 | tf_op jit(solution)/shard_map/ppermute | solution.py:20
  113.3 1.7 collective-permute-start.17
  117.8 1.8 collective-permute-start.21
  119.9 29.2 %collective-permute-done.9 = f32[256,256]{0,1:T(8,128)S(1)} collective-permute-done((f32[256,256]{0,1:T(8,128)S(1)}, f32[256,256]{0,1:T(8,128)S(1)}, u32[]{:S(2)}, u32[]{:S(2)}) %collective-permute-start.9) | collective-permute-done | bytes 262176 | tf_op jit(solution)/shard_map/ppermute | solution.py:20
  149.4 10.9 %collective-permute-done.11 = f32[256,256]{0,1:T(8,128)S(1)} collective-permute-done((f32[256,256]{0,1:T(8,128)S(1)}, f32[256,256]{0,1:T(8,128)S(1)}, u32[]{:S(2)}, u32[]{:S(2)}) %collective-permute-start.11) | collective-permute-done | bytes 262176 | tf_op jit(solution)/shard_map/ppermute | solution.py:20
  160.6 5.3 %collective-permute-done.17 = f32[256,256]{0,1:T(8,128)S(1)} collective-permute-done((f32[256,256]{0,1:T(8,128)S(1)}, f32[256,256]{0,1:T(8,128)S(1)}, u32[]{:S(2)}, u32[]{:S(2)}) %collective-permute-start.17) | collective-permute-done | bytes 262176 | tf_op jit(solution)/shard_map/ppermute | solution.py:20
  166.2 5.3 %collective-permute-done.19 = f32[256,256]{0,1:T(8,128)S(1)} collective-permute-done((f32[256,256]{0,1:T(8,128)S(1)}, f32[256,256]{0,1:T(8,128)S(1)}, u32[]{:S(2)}, u32[]{:S(2)}) %collective-permute-start.19) | collective-permute-done | bytes 262176 | tf_op jit(solution)/shard_map/ppermute | solution.py:20
  171.8 5.3 %collective-permute-done.21 = f32[256,256]{0,1:T(8,128)S(1)} collective-permute-done((f32[256,256]{0,1:T(8,128)S(1)}, f32[256,256]{0,1:T(8,128)S(1)}, u32[]{:S(2)}, u32[]{:S(2)}) %collective-permute-start.21) | collective-permute-done | bytes 262176 | tf_op jit(solution)/shard_map/ppermute | solution.py:20
  177.4 5.2 %collective-permute-done.23 = f32[256,256]{0,1:T(8,128)S(1)} collective-permute-done((f32[256,256]{0,1:T(8,128)S(1)}, f32[256,256]{0,1:T(8,128)S(1)}, u32[]{:S(2)}, u32[]{:S(2)}) %collective-permute-start.23) | collective-permute-done | bytes 262176 | tf_op jit(solution)/shard_map/ppermute | solution.py:20
  183.0 2.6 %pad_maximum_fusion = f32[1024,1024]{1,0:T(8,128)} fusion(f32[512,1024]{1,0:T(8,128)S(1)} %slice_subtract_fusion.1, f32[256,256]{1,0:T(8,128)S(1)} %fusion, f32[256,256]{1,0:T(8,128)S(1)} %fusion.2, f32[256,256]{1,0:T(8,128)S(1)} %fusion.4, f32[256,256]{1,0:T(8,128)S(1)} %fusion.6, f32[256,256]{1,0:T(8,128)S(1)} %fusion.8, f32[256,256]{1,0:T(8,128)S(1)} %fusion.10, ...), kind=kLoop, calls=%fused_computation | loop fusion | flops 8388608 | bytes 8388608 | tf_op jit(solution)/shard_map/concatenate | solution.py:80
  (89 shorter events, 32.8 us)
Async XLA Ops:
  0.0 3.3 %copy-start.4 = (s32[2]{0:T(128)S(1)}, s32[2]{0:T(128)}, u32[]{:S(2)}) copy-start(s32[2]{0:T(128)} %param.7) | copy-start | bytes 28
  0.0 3.1 %copy-start.3 = (f32[2,1024,256]{2,1,0:T(8,128)S(1)}, f32[2,1024,256]{2,1,0:T(8,128)}, u32[]{:S(2)}) copy-start(f32[2,1024,256]{2,1,0:T(8,128)} %param.8) | copy-start | bytes 6291460
  2.5 5.0 %collective-permute-start.12 = (f32[512,256]{1,0:T(8,128)S(1)}, f32[512,256]{1,0:T(8,128)}, u32[]{:S(2)}, u32[]{:S(2)}) collective-permute-start(f32[512,256]{1,0:T(8,128)S(1)} %fusion.31), channel_id=1, source_target_pairs={{0,1},{1,0},{2,3},{3,2},{4,5},{5,4},{6,7},{7,6},{8,9},{9,8},{10,11... | collective-permute-start | bytes 1572872 | tf_op jit(solution)/shard_map/ppermute | solution.py:24
  3.2 7.5 %collective-permute-start = (f32[640,256]{1,0:T(8,128)S(1)}, f32[640,256]{1,0:T(8,128)}, u32[]{:S(2)}, u32[]{:S(2)}) collective-permute-start(f32[640,256]{1,0:T(8,128)S(1)} %fusion.27), channel_id=1, source_target_pairs={{0,1},{1,0},{2,3},{3,2},{4,5},{5,4},{6,7},{7,6},{8,9},{9,8},{10,11... | collective-permute-start | bytes 1966088 | tf_op jit(solution)/shard_map/ppermute | solution.py:24
  7.7 10.3 %collective-permute-start.13 = (f32[512,256]{1,0:T(8,128)S(1)}, f32[512,256]{1,0:T(8,128)}, u32[]{:S(2)}, u32[]{:S(2)}) collective-permute-start(f32[512,256]{1,0:T(8,128)S(1)} %select_select_fusion.1), channel_id=1, source_target_pairs={{0,2},{1,5},{2,0},{3,7},{4,6},{5,1},{6,4},{7,3},{8,10},{9,13},{10,... | collective-permute-start | bytes 1572872 | tf_op jit(solution)/shard_map/ppermute | solution.py:37
  11.9 15.6 %collective-permute-start.1 = (f32[640,256]{1,0:T(8,128)S(1)}, f32[640,256]{1,0:T(8,128)S(1)}, u32[]{:S(2)}, u32[]{:S(2)}) collective-permute-start(f32[640,256]{1,0:T(8,128)S(1)} %select_select_fusion), channel_id=1, source_target_pairs={{0,2},{1,5},{2,0},{3,7},{4,6},{5,1},{6,4},{7,3},{8,10},{9,13},{10,... | collective-permute-start | bytes 1966088 | tf_op jit(solution)/shard_map/ppermute | solution.py:37
  19.1 12.0 %collective-permute-start.14 = (f32[512,256]{1,0:T(8,128)S(1)}, f32[512,256]{1,0:T(8,128)S(1)}, u32[]{:S(2)}, u32[]{:S(2)}) collective-permute-start(f32[512,256]{1,0:T(8,128)S(1)} %broadcast_select_fusion.4), channel_id=1, source_target_pairs={{0,4},{1,3},{2,6},{3,1},{4,0},{5,7},{6,2},{7,5},{8,12},{9,11},{10,... | collective-permute-start | bytes 1572872 | tf_op jit(solution)/shard_map/ppermute | solution.py:37
  27.6 12.0 %collective-permute-start.2 = (f32[640,256]{1,0:T(8,128)S(1)}, f32[640,256]{1,0:T(8,128)S(1)}, u32[]{:S(2)}, u32[]{:S(2)}) collective-permute-start(f32[640,256]{1,0:T(8,128)S(1)} %broadcast_select_fusion), channel_id=1, source_target_pairs={{0,4},{1,3},{2,6},{3,1},{4,0},{5,7},{6,2},{7,5},{8,12},{9,11},{10,... | collective-permute-start | bytes 1966088 | tf_op jit(solution)/shard_map/ppermute | solution.py:37
  31.1 8.7 %collective-permute-start.15 = (f32[512,256]{1,0:T(8,128)S(1)}, f32[512,256]{1,0:T(8,128)S(1)}, u32[]{:S(2)}, u32[]{:S(2)}) collective-permute-start(f32[512,256]{1,0:T(8,128)S(1)} %broadcast_select_fusion.5), channel_id=1, source_target_pairs={{0,1},{1,0},{2,3},{3,2},{4,5},{5,4},{6,7},{7,6},{8,9},{9,8},{10,11... | collective-permute-start | bytes 1572872 | tf_op jit(solution)/shard_map/ppermute | solution.py:24
  39.7 2.2 %collective-permute-start.3 = (f32[640,256]{1,0:T(8,128)S(1)}, f32[640,256]{1,0:T(8,128)S(1)}, u32[]{:S(2)}, u32[]{:S(2)}) collective-permute-start(f32[640,256]{1,0:T(8,128)S(1)} %broadcast_select_fusion.1), channel_id=1, source_target_pairs={{0,1},{1,0},{2,3},{3,2},{4,5},{5,4},{6,7},{7,6},{8,9},{9,8},{10,11... | collective-permute-start | bytes 1966088 | tf_op jit(solution)/shard_map/ppermute | solution.py:24
  39.9 2.2 %copy-start.2 = (f32[1024,1024]{1,0:T(8,128)S(1)}, f32[1024,1024]{1,0:T(8,128)}, u32[]{:S(2)}) copy-start(f32[1024,1024]{1,0:T(8,128)} %param.6) | copy-start | bytes 12582916
  44.3 1.4 copy-start
  51.8 12.9 %copy-start.1 = (f32[2,2,256,256]{3,2,1,0:T(8,128)S(1)}, f32[2,2,256,256]{3,2,1,0:T(8,128)}, u32[]{:S(2)}) copy-start(f32[2,2,256,256]{3,2,1,0:T(8,128)} %param.11) | copy-start | bytes 3145732
  53.9 9.2 %collective-permute-start.4 = (f32[256,256]{0,1:T(8,128)S(1)}, f32[256,256]{0,1:T(8,128)S(1)}, u32[]{:S(2)}, u32[]{:S(2)}) collective-permute-start(f32[256,256]{0,1:T(8,128)S(1)} %convolution_bitcast_fusion.31), channel_id=1, source_target_pairs={{0,8},{8,0},{16,24},{24,16},{1,9},{9,1},{17,25},{25,17},{2,10},{10... | collective-permute-start | bytes 786440 | tf_op jit(solution)/shard_map/ppermute | solution.py:20
  55.9 12.8 %collective-permute-start.6 = (f32[256,256]{0,1:T(8,128)S(1)}, f32[256,256]{0,1:T(8,128)S(1)}, u32[]{:S(2)}, u32[]{:S(2)}) collective-permute-start(f32[256,256]{0,1:T(8,128)S(1)} %convolution_bitcast_fusion.27), channel_id=1, source_target_pairs={{0,8},{8,0},{16,24},{24,16},{1,9},{9,1},{17,25},{25,17},{2,10},{10... | collective-permute-start | bytes 786440 | tf_op jit(solution)/shard_map/ppermute | solution.py:20
  56.9 17.4 %collective-permute-start.8 = (f32[256,256]{0,1:T(8,128)S(1)}, f32[256,256]{0,1:T(8,128)S(1)}, u32[]{:S(2)}, u32[]{:S(2)}) collective-permute-start(f32[256,256]{0,1:T(8,128)S(1)} %convolution_bitcast_fusion.23), channel_id=1, source_target_pairs={{0,8},{8,0},{16,24},{24,16},{1,9},{9,1},{17,25},{25,17},{2,10},{10... | collective-permute-start | bytes 786440 | tf_op jit(solution)/shard_map/ppermute | solution.py:20
  58.5 21.4 %collective-permute-start.10 = (f32[256,256]{0,1:T(8,128)S(1)}, f32[256,256]{0,1:T(8,128)S(1)}, u32[]{:S(2)}, u32[]{:S(2)}) collective-permute-start(f32[256,256]{0,1:T(8,128)S(1)} %convolution_bitcast_fusion.19), channel_id=1, source_target_pairs={{0,8},{8,0},{16,24},{24,16},{1,9},{9,1},{17,25},{25,17},{2,10},{10... | collective-permute-start | bytes 786440 | tf_op jit(solution)/shard_map/ppermute | solution.py:20
  59.0 32.2 %collective-permute-start.16 = (f32[256,256]{0,1:T(8,128)S(1)}, f32[256,256]{0,1:T(8,128)S(1)}, u32[]{:S(2)}, u32[]{:S(2)}) collective-permute-start(f32[256,256]{0,1:T(8,128)S(1)} %convolution_bitcast_fusion.15), channel_id=1, source_target_pairs={{0,8},{8,0},{16,24},{24,16},{1,9},{9,1},{17,25},{25,17},{2,10},{10... | collective-permute-start | bytes 786440 | tf_op jit(solution)/shard_map/ppermute | solution.py:20
  63.1 39.3 %collective-permute-start.18 = (f32[256,256]{0,1:T(8,128)S(1)}, f32[256,256]{0,1:T(8,128)S(1)}, u32[]{:S(2)}, u32[]{:S(2)}) collective-permute-start(f32[256,256]{0,1:T(8,128)S(1)} %convolution_bitcast_fusion.11), channel_id=1, source_target_pairs={{0,8},{8,0},{16,24},{24,16},{1,9},{9,1},{17,25},{25,17},{2,10},{10... | collective-permute-start | bytes 786440 | tf_op jit(solution)/shard_map/ppermute | solution.py:20
  68.7 39.4 %collective-permute-start.20 = (f32[256,256]{0,1:T(8,128)S(1)}, f32[256,256]{0,1:T(8,128)S(1)}, u32[]{:S(2)}, u32[]{:S(2)}) collective-permute-start(f32[256,256]{0,1:T(8,128)S(1)} %convolution_bitcast_fusion.7), channel_id=1, source_target_pairs={{0,8},{8,0},{16,24},{24,16},{1,9},{9,1},{17,25},{25,17},{2,10},{10... | collective-permute-start | bytes 786440 | tf_op jit(solution)/shard_map/ppermute | solution.py:20
  74.3 39.0 %collective-permute-start.22 = (f32[256,256]{0,1:T(8,128)S(1)}, f32[256,256]{0,1:T(8,128)S(1)}, u32[]{:S(2)}, u32[]{:S(2)}) collective-permute-start(f32[256,256]{0,1:T(8,128)S(1)} %convolution_bitcast_fusion.3), channel_id=1, source_target_pairs={{0,8},{8,0},{16,24},{24,16},{1,9},{9,1},{17,25},{25,17},{2,10},{10... | collective-permute-start | bytes 786440 | tf_op jit(solution)/shard_map/ppermute | solution.py:20
  79.9 36.2 %collective-permute-start.5 = (f32[256,256]{0,1:T(8,128)S(1)}, f32[256,256]{0,1:T(8,128)S(1)}, u32[]{:S(2)}, u32[]{:S(2)}) collective-permute-start(f32[256,256]{0,1:T(8,128)S(1)} %convolution_bitcast_fusion.29), channel_id=1, source_target_pairs={{0,16},{8,24},{16,0},{24,8},{1,17},{9,25},{17,1},{25,9},{2,18},{10... | collective-permute-start | bytes 786440 | tf_op jit(solution)/shard_map/ppermute | solution.py:20
  91.2 26.6 %collective-permute-start.7 = (f32[256,256]{0,1:T(8,128)S(1)}, f32[256,256]{0,1:T(8,128)S(1)}, u32[]{:S(2)}, u32[]{:S(2)}) collective-permute-start(f32[256,256]{0,1:T(8,128)S(1)} %convolution_bitcast_fusion.25), channel_id=1, source_target_pairs={{0,16},{8,24},{16,0},{24,8},{1,17},{9,25},{17,1},{25,9},{2,18},{10... | collective-permute-start | bytes 786440 | tf_op jit(solution)/shard_map/ppermute | solution.py:20
  102.4 46.6 %collective-permute-start.9 = (f32[256,256]{0,1:T(8,128)S(1)}, f32[256,256]{0,1:T(8,128)S(1)}, u32[]{:S(2)}, u32[]{:S(2)}) collective-permute-start(f32[256,256]{0,1:T(8,128)S(1)} %convolution_bitcast_fusion.21), channel_id=1, source_target_pairs={{0,16},{8,24},{16,0},{24,8},{1,17},{9,25},{17,1},{25,9},{2,18},{10... | collective-permute-start | bytes 786440 | tf_op jit(solution)/shard_map/ppermute | solution.py:20
  108.1 52.1 %collective-permute-start.11 = (f32[256,256]{0,1:T(8,128)S(1)}, f32[256,256]{0,1:T(8,128)S(1)}, u32[]{:S(2)}, u32[]{:S(2)}) collective-permute-start(f32[256,256]{0,1:T(8,128)S(1)} %convolution_bitcast_fusion.17), channel_id=1, source_target_pairs={{0,16},{8,24},{16,0},{24,8},{1,17},{9,25},{17,1},{25,9},{2,18},{10... | collective-permute-start | bytes 786440 | tf_op jit(solution)/shard_map/ppermute | solution.py:20
  113.3 52.6 %collective-permute-start.17 = (f32[256,256]{0,1:T(8,128)S(1)}, f32[256,256]{0,1:T(8,128)S(1)}, u32[]{:S(2)}, u32[]{:S(2)}) collective-permute-start(f32[256,256]{0,1:T(8,128)S(1)} %convolution_bitcast_fusion.13), channel_id=1, source_target_pairs={{0,16},{8,24},{16,0},{24,8},{1,17},{9,25},{17,1},{25,9},{2,18},{10... | collective-permute-start | bytes 786440 | tf_op jit(solution)/shard_map/ppermute | solution.py:20
  116.1 55.4 %collective-permute-start.19 = (f32[256,256]{0,1:T(8,128)S(1)}, f32[256,256]{0,1:T(8,128)S(1)}, u32[]{:S(2)}, u32[]{:S(2)}) collective-permute-start(f32[256,256]{0,1:T(8,128)S(1)} %convolution_bitcast_fusion.9), channel_id=1, source_target_pairs={{0,16},{8,24},{16,0},{24,8},{1,17},{9,25},{17,1},{25,9},{2,18},{10... | collective-permute-start | bytes 786440 | tf_op jit(solution)/shard_map/ppermute | solution.py:20
  117.8 59.3 %collective-permute-start.21 = (f32[256,256]{0,1:T(8,128)S(1)}, f32[256,256]{0,1:T(8,128)S(1)}, u32[]{:S(2)}, u32[]{:S(2)}) collective-permute-start(f32[256,256]{0,1:T(8,128)S(1)} %convolution_bitcast_fusion.5), channel_id=1, source_target_pairs={{0,16},{8,24},{16,0},{24,8},{1,17},{9,25},{17,1},{25,9},{2,18},{10... | collective-permute-start | bytes 786440 | tf_op jit(solution)/shard_map/ppermute | solution.py:20
  149.0 33.6 %collective-permute-start.23 = (f32[256,256]{0,1:T(8,128)S(1)}, f32[256,256]{0,1:T(8,128)S(1)}, u32[]{:S(2)}, u32[]{:S(2)}) collective-permute-start(f32[256,256]{0,1:T(8,128)S(1)} %convolution_bitcast_fusion.1), channel_id=1, source_target_pairs={{0,16},{8,24},{16,0},{24,8},{1,17},{9,25},{17,1},{25,9},{2,18},{10... | collective-permute-start | bytes 786440 | tf_op jit(solution)/shard_map/ppermute | solution.py:20

commit v2 on v1

--- a/solution.py
+++ b/solution.py
@@ -5,7 +5,7 @@
 
 PRECISION = lax.Precision.HIGH
 LEADING = (((0,), (0,)), ((), ()))
-CHUNKS = 4
+CUTS = ((1, 1), (1, 1))
 
 
 def dot(a, b):
@@ -24,11 +24,15 @@
     return lax.ppermute(shard, "col", [(i, i ^ 1) for i in range(lax.axis_size("col"))])
 
 
-def broadcast_halves(half_0, half_1, owner):
+def broadcast_halves(half_0, half_1, owner, held):
     size = lax.axis_size("col")
     me = lax.axis_index("col")
     first = me % 2 == 0
     arrived = swap_cores(jnp.where(first, half_1, half_0))
+    if held is not None:
+        first_value = held[0, 0]
+        owner = owner + (first_value != first_value).astype(owner.dtype)
+    marks = [arrived]
     current = jnp.where(me % 2 == owner % 2, jnp.where(first, half_0, half_1), arrived)
     bits = [1 << k for k in range(1, size.bit_length() - 1)]
     turned = bits[len(bits) // 2 :] + bits[: len(bits) // 2]
@@ -37,20 +41,22 @@
         arrived = lax.ppermute(current, "col", pairs)
         bit = jnp.where(first, even_bit, odd_bit)
         current = jnp.where((me ^ owner) & bit == 0, current, arrived)
+        marks.append(arrived)
     other = swap_cores(current)
-    return jnp.where(first, current, other), jnp.where(first, other, current)
+    marks.append(other)
+    return jnp.where(first, current, other), jnp.where(first, other, current), marks
 
 
-def broadcast_panel(reflectors, factors, owner, first_row):
+def broadcast_panel(reflectors, factors, owner, first_row, held):
     rows = reflectors.shape[0] - first_row
     width = factors.shape[0]
     middle = first_row + rows // 2
     half_0 = jnp.concatenate([reflectors[first_row:middle], factors[: width // 2]], axis=0)
     half_1 = jnp.concatenate([reflectors[middle:], factors[width // 2 :]], axis=0)
-    half_0, half_1 = broadcast_halves(half_0, half_1, owner)
+    half_0, half_1, marks = broadcast_halves(half_0, half_1, owner, held)
     block = jnp.concatenate([half_0[: rows // 2], half_1[: rows // 2]], axis=0)
     factor = jnp.concatenate([half_0[rows // 2 :], half_1[rows // 2 :]], axis=0)
-    return block, factor
+    return block, factor, marks
 
 
 def shards(slab, owner, leaf_reflectors, leaf_factors, tree_reflectors, tree_mixers):
@@ -58,19 +64,24 @@
     width = leaf_factors.shape[1]
     panels = owner.shape[0]
     levels = lax.axis_size("row").bit_length() - 1
-    step = columns // CHUNKS
+    held = None
     lower = slab
     finished = []
     for panel_no in range(panels):
-        reflect_rows, factor = broadcast_panel(
-            leaf_reflectors[panel_no], leaf_factors[panel_no], owner[panel_no], panel_no * width
+        reflect_rows, factor, marks = broadcast_panel(
+            leaf_reflectors[panel_no], leaf_factors[panel_no], owner[panel_no], panel_no * width, held
         )
+        held = marks[-2]
         scaled = dot_t(factor, dot_t(reflect_rows, lower))
         top = lower[:width] - dot(reflect_rows[:width], scaled)
         lower = lower[width:] - dot(reflect_rows[width:], scaled)
         pieces = []
-        for chunk in range(CHUNKS):
-            piece = top[:, chunk * step : (chunk + 1) * step]
+        parts = CUTS[min(panel_no, len(CUTS) - 1)]
+        start = 0
+        for part in parts:
+            step = columns * part // sum(parts)
+            piece = top[:, start : start + step]
+            start += step
             for level_no in range(levels):
                 partial_sum = dot_t(tree_reflectors[panel_no, level_no], piece)
                 both = partial_sum + from_partner(partial_sum, level_no)

time: 186 us -> 161 us (0.87)
  starting transfers between devices: 32.4 us -> 17.7 us
  waiting for transfers between devices: 118 us -> 112 us
  matrix products: 20.8 us -> 17.6 us
  other arithmetic: 5.58 us -> 3.37 us
    ppermute x16 -> x8, starting transfers between devices: 22.9 us -> 8.1 us  [from_partner(): lax.ppermute(shard, 'row', [(i, i ^ 1 << apart) for i in range(lax.axis_s...]
    ppermute x16 -> x8, waiting for transfers between devices: 96.7 us -> 89.8 us  [from_partner(): lax.ppermute(shard, 'row', [(i, i ^ 1 << apart) for i in range(lax.axis_s...]
    ppermute x4, waiting for transfers between devices: 19.5 us -> 22.1 us  [broadcast_halves(): arrived = lax.ppermute(current, 'col', pairs)]
    dot_general x20 -> x12, matrix products: 9.4 us -> 7.31 us  [dot(): jnp.dot(a, b, precision=PRECISION, preferred_element_type=jnp.float32)]
    ppermute x4, waiting for transfers between devices: 1.88 us -> 0.01 us  [swap_cores(): lax.ppermute(shard, 'col', [(i, i ^ 1) for i in range(lax.axis_size('col'...]
    dot_general x20 -> x12, matrix products: 11.4 us -> 10.3 us  [dot_t(): lax.dot_general(a, b, LEADING, precision=PRECISION, preferred_element_typ...]
  transfers between devices with their start and end apart: 24 -> 16, of which waited for: 18 -> 10; matrix products, arithmetic and copies ran while one was open for 7% -> 13% of each run, Pallas kernels for 0% -> 0%
where the time goes in v2:
time: 161 us
  waiting for transfers between devices  112 us (70%)
  starting transfers between devices  17.7 us (11%)
  matrix products  17.6 us (11%)
  between operations  5.3 us (3%)
  local copies, waits for them, and re-layouts  4.96 us (3%)
  other arithmetic  3.37 us (2%)
    ppermute x8, waiting for transfers between devices, from_partner(): lax.ppermute(shard, 'row', [(i, i ^ 1 << apart) for i in range(lax.axis_s...  89.8 us
    ppermute x4, waiting for transfers between devices, broadcast_halves(): arrived = lax.ppermute(current, 'col', pairs)  22.1 us
    dot_general x12, matrix products, dot_t(): lax.dot_general(a, b, LEADING, precision=PRECISION, preferred_element_typ...  10.3 us
    ppermute x4, starting transfers between devices, broadcast_halves(): arrived = lax.ppermute(current, 'col', pairs)  8.83 us
    ppermute x8, starting transfers between devices, from_partner(): lax.ppermute(shard, 'row', [(i, i ^ 1 << apart) for i in range(lax.axis_s...  8.1 us
    dot_general x12, matrix products, dot(): jnp.dot(a, b, precision=PRECISION, preferred_element_type=jnp.float32)  7.31 us
  transfers between devices with their start and end apart: 16, of which 10 were waited for; matrix products, arithmetic and copies ran while one was open for 13% of the time, Pallas kernels for 0%

profile of v2, /device:TPU:0, one launch (start us, length us, event | category | flops | bytes accessed | tf_op | source)
XLA Modules:
  0.0 160.8 jit_solution(17123911957004764708)
XLA Ops:
  0.0 1.1 slice_bitcast_fusion.5
  1.1 1.3 slice_bitcast_fusion.1
  5.9 2.6 %collective-permute-start.1 = (f32[640,256]{1,0:T(8,128)S(1)}, f32[640,256]{1,0:T(8,128)S(1)}, u32[]{:S(2)}, u32[]{:S(2)}) collective-permute-start(f32[640,256]{1,0:T(8,128)S(1)} %select_select_fusion), channel_id=1, source_target_pairs={{0,2},{1,5},{2,0},{3,7},{4,6},{5,1},{6,4},{7,3},{8,10},{9,13},{10,... | collective-permute-start | bytes 1966088 | tf_op jit(solution)/shard_map/ppermute | solution.py:41
  9.1 7.9 %collective-permute-done.1 = f32[640,256]{1,0:T(8,128)S(1)} collective-permute-done((f32[640,256]{1,0:T(8,128)S(1)}, f32[640,256]{1,0:T(8,128)S(1)}, u32[]{:S(2)}, u32[]{:S(2)}) %collective-permute-start.1) | collective-permute-done | bytes 655392 | tf_op jit(solution)/shard_map/ppermute | solution.py:41
  17.1 2.1 %collective-permute-start.2 = (f32[640,256]{1,0:T(8,128)S(1)}, f32[640,256]{1,0:T(8,128)S(1)}, u32[]{:S(2)}, u32[]{:S(2)}) collective-permute-start(f32[640,256]{1,0:T(8,128)S(1)} %broadcast_select_fusion), channel_id=1, source_target_pairs={{0,4},{1,3},{2,6},{3,1},{4,0},{5,7},{6,2},{7,5},{8,12},{9,11},{10,... | collective-permute-start | bytes 1966088 | tf_op jit(solution)/shard_map/ppermute | solution.py:41
  19.2 1.2 slice_bitcast_fusion.3
  20.5 7.2 %collective-permute-done.2 = f32[640,256]{1,0:T(8,128)S(1)} collective-permute-done((f32[640,256]{1,0:T(8,128)S(1)}, f32[640,256]{1,0:T(8,128)S(1)}, u32[]{:S(2)}, u32[]{:S(2)}) %collective-permute-start.2) | collective-permute-done | bytes 655392 | tf_op jit(solution)/shard_map/ppermute | solution.py:41
  30.5 2.1 %collective-permute-start.9 = (f32[512,256]{1,0:T(8,128)S(1)}, f32[512,256]{1,0:T(8,128)S(1)}, u32[]{:S(2)}, u32[]{:S(2)}) collective-permute-start(f32[512,256]{1,0:T(8,128)S(1)} %select_select_fusion.1), channel_id=1, source_target_pairs={{0,2},{1,5},{2,0},{3,7},{4,6},{5,1},{6,4},{7,3},{8,10},{9,13},{10,... | collective-permute-start | bytes 1572872 | tf_op jit(solution)/shard_map/ppermute | solution.py:41
  32.8 7.0 %collective-permute-done.9 = f32[512,256]{1,0:T(8,128)S(1)} collective-permute-done((f32[512,256]{1,0:T(8,128)S(1)}, f32[512,256]{1,0:T(8,128)S(1)}, u32[]{:S(2)}, u32[]{:S(2)}) %collective-permute-start.9) | collective-permute-done | bytes 524320 | tf_op jit(solution)/shard_map/ppermute | solution.py:41
  39.9 2.1 %collective-permute-start.10 = (f32[512,256]{1,0:T(8,128)S(1)}, f32[512,256]{1,0:T(8,128)S(1)}, u32[]{:S(2)}, u32[]{:S(2)}) collective-permute-start(f32[512,256]{1,0:T(8,128)S(1)} %broadcast_select_fusion.4), channel_id=1, source_target_pairs={{0,4},{1,3},{2,6},{3,1},{4,0},{5,7},{6,2},{7,5},{8,12},{9,11},{10,... | collective-permute-start | bytes 1572872 | tf_op jit(solution)/shard_map/ppermute | solution.py:41
  42.2 2.1 %fusion.8 = f32[256,1024]{1,0:T(8,128)S(1)} fusion(f32[1024,1024]{1,0:T(8,128)S(1)} %copy-done, f32[512,256]{1,0:T(8,128)S(1)} %slice.214, f32[512,256]{1,0:T(8,128)S(1)} %slice.213), kind=kOutput, calls=%fused_computation.29 | convolution fusion | flops 1610874880 | bytes 6291456 | tf_op jit(solution)/shard_map/dot_general | solution.py:16
  44.3 0.7 fusion.38
  45.0 0.6 convolution_subtract_fusion.1
  46.9 1.6 %collective-permute-start.4 = (f32[256,512]{0,1:T(8,128)S(1)}, f32[256,512]{0,1:T(8,128)S(1)}, u32[]{:S(2)}, u32[]{:S(2)}) collective-permute-start(f32[256,512]{0,1:T(8,128)S(1)} %convolution_bitcast_fusion.15), channel_id=1, source_target_pairs={{0,8},{8,0},{16,24},{24,16},{1,9},{9,1},{17,25},{25,17},{2,10},{10... | collective-permute-start | bytes 1572872 | tf_op jit(solution)/shard_map/ppermute | solution.py:20
  49.0 1.5 slice_subtract_fusion
  50.7 16.8 %collective-permute-done.4 = f32[256,512]{0,1:T(8,128)S(1)} collective-permute-done((f32[256,512]{0,1:T(8,128)S(1)}, f32[256,512]{0,1:T(8,128)S(1)}, u32[]{:S(2)}, u32[]{:S(2)}) %collective-permute-start.4) | collective-permute-done | bytes 524320 | tf_op jit(solution)/shard_map/ppermute | solution.py:20
  68.6 1.8 %collective-permute-start.5 = (f32[256,512]{0,1:T(8,128)S(1)}, f32[256,512]{0,1:T(8,128)S(1)}, u32[]{:S(2)}, u32[]{:S(2)}) collective-permute-start(f32[256,512]{0,1:T(8,128)S(1)} %convolution_bitcast_fusion.13), channel_id=1, source_target_pairs={{0,16},{8,24},{16,0},{24,8},{1,17},{9,25},{17,1},{25,9},{2,18},{10... | collective-permute-start | bytes 1572872 | tf_op jit(solution)/shard_map/ppermute | solution.py:20
  70.3 6.1 %collective-permute-done.6 = f32[256,512]{0,1:T(8,128)S(1)} collective-permute-done((f32[256,512]{0,1:T(8,128)S(1)}, f32[256,512]{0,1:T(8,128)S(1)}, u32[]{:S(2)}, u32[]{:S(2)}) %collective-permute-start.6) | collective-permute-done | bytes 524320 | tf_op jit(solution)/shard_map/ppermute | solution.py:20
  76.9 0.6 convolution_bitcast_fusion.9
  77.5 0.7 collective-permute-start.7
  78.4 1.6 %fusion.15 = f32[256,1024]{1,0:T(8,128)S(1)} fusion(f32[768,1024]{1,0:T(8,128)S(1)} %slice_subtract_fusion, f32[384,256]{1,0:T(8,128)S(1)} %slice.223, f32[384,256]{1,0:T(8,128)S(1)} %slice.222), kind=kOutput, calls=%fused_computation.36 | convolution fusion | flops 1208156160 | bytes 4980736 | tf_op jit(solution)/shard_map/dot_general | solution.py:16
  80.1 0.9 fusion.42
  81.0 0.7 convolution_subtract_fusion
  82.3 2.6 %collective-permute-start.12 = (f32[256,512]{0,1:T(8,128)S(1)}, f32[256,512]{0,1:T(8,128)S(1)}, u32[]{:S(2)}, u32[]{:S(2)}) collective-permute-start(f32[256,512]{0,1:T(8,128)S(1)} %convolution_bitcast_fusion.7), channel_id=1, source_target_pairs={{0,8},{8,0},{16,24},{24,16},{1,9},{9,1},{17,25},{25,17},{2,10},{10... | collective-permute-start | bytes 1572872 | tf_op jit(solution)/shard_map/ppermute | solution.py:20
  85.5 1.1 slice_subtract_fusion.1
  86.7 16.6 %collective-permute-done.5 = f32[256,512]{0,1:T(8,128)S(1)} collective-permute-done((f32[256,512]{0,1:T(8,128)S(1)}, f32[256,512]{0,1:T(8,128)S(1)}, u32[]{:S(2)}, u32[]{:S(2)}) %collective-permute-start.5) | collective-permute-done | bytes 524320 | tf_op jit(solution)/shard_map/ppermute | solution.py:20
  103.7 15.3 %collective-permute-done.12 = f32[256,512]{0,1:T(8,128)S(1)} collective-permute-done((f32[256,512]{0,1:T(8,128)S(1)}, f32[256,512]{0,1:T(8,128)S(1)}, u32[]{:S(2)}, u32[]{:S(2)}) %collective-permute-start.12) | collective-permute-done | bytes 524320 | tf_op jit(solution)/shard_map/ppermute | solution.py:20
  120.3 5.6 %collective-permute-done.14 = f32[256,512]{0,1:T(8,128)S(1)} collective-permute-done((f32[256,512]{0,1:T(8,128)S(1)}, f32[256,512]{0,1:T(8,128)S(1)}, u32[]{:S(2)}, u32[]{:S(2)}) %collective-permute-start.14) | collective-permute-done | bytes 524320 | tf_op jit(solution)/shard_map/ppermute | solution.py:20
  127.0 0.7 collective-permute-start.15
  128.1 24.1 %collective-permute-done.13 = f32[256,512]{0,1:T(8,128)S(1)} collective-permute-done((f32[256,512]{0,1:T(8,128)S(1)}, f32[256,512]{0,1:T(8,128)S(1)}, u32[]{:S(2)}, u32[]{:S(2)}) %collective-permute-start.13) | collective-permute-done | bytes 524320 | tf_op jit(solution)/shard_map/ppermute | solution.py:20
  152.6 5.3 %collective-permute-done.15 = f32[256,512]{0,1:T(8,128)S(1)} collective-permute-done((f32[256,512]{0,1:T(8,128)S(1)}, f32[256,512]{0,1:T(8,128)S(1)}, u32[]{:S(2)}, u32[]{:S(2)}) %collective-permute-start.15) | collective-permute-done | bytes 524320 | tf_op jit(solution)/shard_map/ppermute | solution.py:20
  158.3 2.5 %pad_maximum_fusion = f32[1024,1024]{1,0:T(8,128)} fusion(f32[512,1024]{1,0:T(8,128)S(1)} %slice_subtract_fusion.1, f32[256,512]{1,0:T(8,128)S(1)} %fusion.7, f32[256,512]{1,0:T(8,128)S(1)} %fusion.5, f32[256,512]{1,0:T(8,128)S(1)} %fusion.3, f32[256,512]{1,0:T(8,128)S(1)} %fusion.1), kind=kLoop, calls=%fused_computation | loop fusion | flops 4194304 | bytes 8388608 | tf_op jit(solution)/shard_map/concatenate | solution.py:91
  (56 shorter events, 11.4 us)
Async XLA Ops:
  0.0 3.0 %copy-start.3 = (s32[2]{0:T(128)S(1)}, s32[2]{0:T(128)}, u32[]{:S(2)}) copy-start(s32[2]{0:T(128)} %param.7) | copy-start | bytes 28
  2.5 3.2 %collective-permute-start = (f32[640,256]{1,0:T(8,128)S(1)}, f32[640,256]{1,0:T(8,128)S(1)}, u32[]{:S(2)}, u32[]{:S(2)}) collective-permute-start(f32[640,256]{1,0:T(8,128)S(1)} %fusion.19), channel_id=1, source_target_pairs={{0,1},{1,0},{2,3},{3,2},{4,5},{5,4},{6,7},{7,6},{8,9},{9,8},{10,11... | collective-permute-start | bytes 1966088 | tf_op jit(solution)/shard_map/ppermute | solution.py:24
  5.9 11.1 %collective-permute-start.1 = (f32[640,256]{1,0:T(8,128)S(1)}, f32[640,256]{1,0:T(8,128)S(1)}, u32[]{:S(2)}, u32[]{:S(2)}) collective-permute-start(f32[640,256]{1,0:T(8,128)S(1)} %select_select_fusion), channel_id=1, source_target_pairs={{0,2},{1,5},{2,0},{3,7},{4,6},{5,1},{6,4},{7,3},{8,10},{9,13},{10,... | collective-permute-start | bytes 1966088 | tf_op jit(solution)/shard_map/ppermute | solution.py:41
  17.1 10.7 %collective-permute-start.2 = (f32[640,256]{1,0:T(8,128)S(1)}, f32[640,256]{1,0:T(8,128)S(1)}, u32[]{:S(2)}, u32[]{:S(2)}) collective-permute-start(f32[640,256]{1,0:T(8,128)S(1)} %broadcast_select_fusion), channel_id=1, source_target_pairs={{0,4},{1,3},{2,6},{3,1},{4,0},{5,7},{6,2},{7,5},{8,12},{9,11},{10,... | collective-permute-start | bytes 1966088 | tf_op jit(solution)/shard_map/ppermute | solution.py:41
  20.5 10.0 %collective-permute-start.8 = (f32[512,256]{1,0:T(8,128)S(1)}, f32[512,256]{1,0:T(8,128)S(1)}, u32[]{:S(2)}, u32[]{:S(2)}) collective-permute-start(f32[512,256]{1,0:T(8,128)S(1)} %fusion.35), channel_id=1, source_target_pairs={{0,1},{1,0},{2,3},{3,2},{4,5},{5,4},{6,7},{7,6},{8,9},{9,8},{10,11... | collective-permute-start | bytes 1572872 | tf_op jit(solution)/shard_map/ppermute | solution.py:24
  30.5 9.2 %collective-permute-start.9 = (f32[512,256]{1,0:T(8,128)S(1)}, f32[512,256]{1,0:T(8,128)S(1)}, u32[]{:S(2)}, u32[]{:S(2)}) collective-permute-start(f32[512,256]{1,0:T(8,128)S(1)} %select_select_fusion.1), channel_id=1, source_target_pairs={{0,2},{1,5},{2,0},{3,7},{4,6},{5,1},{6,4},{7,3},{8,10},{9,13},{10,... | collective-permute-start | bytes 1572872 | tf_op jit(solution)/shard_map/ppermute | solution.py:41
  32.7 9.3 %collective-permute-start.3 = (f32[640,256]{1,0:T(8,128)S(1)}, f32[640,256]{1,0:T(8,128)S(1)}, u32[]{:S(2)}, u32[]{:S(2)}) collective-permute-start(f32[640,256]{1,0:T(8,128)S(1)} %broadcast_select_fusion.1), channel_id=1, source_target_pairs={{0,1},{1,0},{2,3},{3,2},{4,5},{5,4},{6,7},{7,6},{8,9},{9,8},{10,11... | collective-permute-start | bytes 1966088 | tf_op jit(solution)/shard_map/ppermute | solution.py:24
  32.8 9.4 %copy-start = (f32[1024,1024]{1,0:T(8,128)S(1)}, f32[1024,1024]{1,0:T(8,128)}, u32[]{:S(2)}) copy-start(f32[1024,1024]{1,0:T(8,128)} %param.6) | copy-start | bytes 12582916
  39.9 10.7 %collective-permute-start.10 = (f32[512,256]{1,0:T(8,128)S(1)}, f32[512,256]{1,0:T(8,128)S(1)}, u32[]{:S(2)}, u32[]{:S(2)}) collective-permute-start(f32[512,256]{1,0:T(8,128)S(1)} %broadcast_select_fusion.4), channel_id=1, source_target_pairs={{0,4},{1,3},{2,6},{3,1},{4,0},{5,7},{6,2},{7,5},{8,12},{9,11},{10,... | collective-permute-start | bytes 1572872 | tf_op jit(solution)/shard_map/ppermute | solution.py:41
  44.3 1.4 copy-start.1
  46.9 20.6 %copy-start.2 = (f32[2,2,256,256]{3,2,1,0:T(8,128)S(1)}, f32[2,2,256,256]{3,2,1,0:T(8,128)}, u32[]{:S(2)}) copy-start(f32[2,2,256,256]{3,2,1,0:T(8,128)} %param.11) | copy-start | bytes 3145732
  46.9 20.5 %collective-permute-start.4 = (f32[256,512]{0,1:T(8,128)S(1)}, f32[256,512]{0,1:T(8,128)S(1)}, u32[]{:S(2)}, u32[]{:S(2)}) collective-permute-start(f32[256,512]{0,1:T(8,128)S(1)} %convolution_bitcast_fusion.15), channel_id=1, source_target_pairs={{0,8},{8,0},{16,24},{24,16},{1,9},{9,1},{17,25},{25,17},{2,10},{10... | collective-permute-start | bytes 1572872 | tf_op jit(solution)/shard_map/ppermute | solution.py:20
  48.6 27.8 %collective-permute-start.6 = (f32[256,512]{0,1:T(8,128)S(1)}, f32[256,512]{0,1:T(8,128)S(1)}, u32[]{:S(2)}, u32[]{:S(2)}) collective-permute-start(f32[256,512]{0,1:T(8,128)S(1)} %convolution_bitcast_fusion.11), channel_id=1, source_target_pairs={{0,8},{8,0},{16,24},{24,16},{1,9},{9,1},{17,25},{25,17},{2,10},{10... | collective-permute-start | bytes 1572872 | tf_op jit(solution)/shard_map/ppermute | solution.py:20
  50.6 27.6 %collective-permute-start.11 = (f32[512,256]{1,0:T(8,128)S(1)}, f32[512,256]{1,0:T(8,128)S(1)}, u32[]{:S(2)}, u32[]{:S(2)}) collective-permute-start(f32[512,256]{1,0:T(8,128)S(1)} %broadcast_select_fusion.5), channel_id=1, source_target_pairs={{0,1},{1,0},{2,3},{3,2},{4,5},{5,4},{6,7},{7,6},{8,9},{9,8},{10,11... | collective-permute-start | bytes 1572872 | tf_op jit(solution)/shard_map/ppermute | solution.py:24
  68.6 34.8 %collective-permute-start.5 = (f32[256,512]{0,1:T(8,128)S(1)}, f32[256,512]{0,1:T(8,128)S(1)}, u32[]{:S(2)}, u32[]{:S(2)}) collective-permute-start(f32[256,512]{0,1:T(8,128)S(1)} %convolution_bitcast_fusion.13), channel_id=1, source_target_pairs={{0,16},{8,24},{16,0},{24,8},{1,17},{9,25},{17,1},{25,9},{2,18},{10... | collective-permute-start | bytes 1572872 | tf_op jit(solution)/shard_map/ppermute | solution.py:20
  77.5 50.2 %collective-permute-start.7 = (f32[256,512]{0,1:T(8,128)S(1)}, f32[256,512]{0,1:T(8,128)S(1)}, u32[]{:S(2)}, u32[]{:S(2)}) collective-permute-start(f32[256,512]{0,1:T(8,128)S(1)} %convolution_bitcast_fusion.9), channel_id=1, source_target_pairs={{0,16},{8,24},{16,0},{24,8},{1,17},{9,25},{17,1},{25,9},{2,18},{10... | collective-permute-start | bytes 1572872 | tf_op jit(solution)/shard_map/ppermute | solution.py:20
  82.3 36.7 %collective-permute-start.12 = (f32[256,512]{0,1:T(8,128)S(1)}, f32[256,512]{0,1:T(8,128)S(1)}, u32[]{:S(2)}, u32[]{:S(2)}) collective-permute-start(f32[256,512]{0,1:T(8,128)S(1)} %convolution_bitcast_fusion.7), channel_id=1, source_target_pairs={{0,8},{8,0},{16,24},{24,16},{1,9},{9,1},{17,25},{25,17},{2,10},{10... | collective-permute-start | bytes 1572872 | tf_op jit(solution)/shard_map/ppermute | solution.py:20
  85.5 40.5 %collective-permute-start.14 = (f32[256,512]{0,1:T(8,128)S(1)}, f32[256,512]{0,1:T(8,128)S(1)}, u32[]{:S(2)}, u32[]{:S(2)}) collective-permute-start(f32[256,512]{0,1:T(8,128)S(1)} %convolution_bitcast_fusion.3), channel_id=1, source_target_pairs={{0,8},{8,0},{16,24},{24,16},{1,9},{9,1},{17,25},{25,17},{2,10},{10... | collective-permute-start | bytes 1572872 | tf_op jit(solution)/shard_map/ppermute | solution.py:20
  120.1 32.1 %collective-permute-start.13 = (f32[256,512]{0,1:T(8,128)S(1)}, f32[256,512]{0,1:T(8,128)S(1)}, u32[]{:S(2)}, u32[]{:S(2)}) collective-permute-start(f32[256,512]{0,1:T(8,128)S(1)} %convolution_bitcast_fusion.5), channel_id=1, source_target_pairs={{0,16},{8,24},{16,0},{24,8},{1,17},{9,25},{17,1},{25,9},{2,18},{10... | collective-permute-start | bytes 1572872 | tf_op jit(solution)/shard_map/ppermute | solution.py:20
  127.0 30.9 %collective-permute-start.15 = (f32[256,512]{0,1:T(8,128)S(1)}, f32[256,512]{0,1:T(8,128)S(1)}, u32[]{:S(2)}, u32[]{:S(2)}) collective-permute-start(f32[256,512]{0,1:T(8,128)S(1)} %convolution_bitcast_fusion.1), channel_id=1, source_target_pairs={{0,16},{8,24},{16,0},{24,8},{1,17},{9,25},{17,1},{25,9},{2,18},{10... | collective-permute-start | bytes 1572872 | tf_op jit(solution)/shard_map/ppermute | solution.py:20

commit v3 on v1

v3 whole, which is shorter than its diff:
```python
import jax
import jax.numpy as jnp
from jax import lax
from jax.sharding import PartitionSpec as P

PRECISION = lax.Precision.HIGH
LEADING = (((0,), (0,)), ((), ()))
CUTS = ((1, 1), (1, 1))
STREAMS = 1
GATE_0 = "none"
GATE_1 = "arrived"
GATE_2 = "own"
GATE_3 = "own"
FIRST_AFTER = False
ALONE = False
UPDATE = True


def dot(a, b):
    return jnp.dot(a, b, precision=PRECISION, preferred_element_type=jnp.float32)


def dot_t(a, b):
    return lax.dot_general(a, b, LEADING, precision=PRECISION, preferred_element_type=jnp.float32)


def from_partner(shard, apart):
    return lax.ppermute(shard, "row", [(i, i ^ 1 << apart) for i in range(lax.axis_size("row"))])


def swap_cores(shard):
    return lax.ppermute(shard, "col", [(i, i ^ 1) for i in range(lax.axis_size("col"))])


def never(held, columns):
    row = held[:1, :columns]
    return row != row


def after(value, held):
    if held is None:
        return value
    return jnp.where(never(held, value.shape[1]), -value, value)


class Broadcast:
    def __init__(self, reflectors, factors, owner, first_row, streams):
        size = lax.axis_size("col")
        self.me = lax.axis_index("col")
        self.first = self.me % 2 == 0
        self.owner = owner
        self.rows = reflectors.shape[0] - first_row
        self.width = factors.shape[0]
        middle = first_row + self.rows // 2
        block_0 = jnp.concatenate([reflectors[first_row:middle], factors[: self.width // 2]], axis=0)
        block_1 = jnp.concatenate([reflectors[middle:], factors[self.width // 2 :]], axis=0)
        part = block_0.shape[0] // streams
        cut = [slice(s * part, (s + 1) * part) for s in range(streams)]
        self.halves = [(block_0[c], block_1[c]) for c in cut]
        bits = [1 << k for k in range(1, size.bit_length() - 1)]
        turned = bits[len(bits) // 2 :] + bits[: len(bits) // 2]
        self.exchanges = [
            (
                [(i, i ^ (odd if i % 2 else even)) for i in range(size)],
                jnp.where(self.first, even, odd),
            )
            for even, odd in zip(bits, turned)
        ]
        self.bit = 1

    def begin(self, held=None):
        sent = [after(jnp.where(self.first, h1, h0), held) for h0, h1 in self.halves]
        self.arrived = [swap_cores(s) for s in sent]
        self.current = [jnp.where(self.first, h0, h1) for h0, h1 in self.halves]

    def select(self, held):
        keep = (self.me ^ self.owner) & self.bit == 0
        result = []
        for current, arrived in zip(self.current, self.arrived):
            if held is not None:
                keep = jnp.logical_or(keep, never(held, current.shape[1]))
            result.append(jnp.where(keep, current, arrived))
        self.current = result

    def exchange(self, number, held=None):
        self.select(held)
        pairs, self.bit = self.exchanges[number]
        self.arrived = [lax.ppermute(c, "col", pairs) for c in self.current]

    def end(self, held=None):
        self.select(held)
        other = [swap_cores(c) for c in self.current]
        self.arrived = other
        side_0 = jnp.concatenate([jnp.where(self.first, c, o) for c, o in zip(self.current, other)], axis=0)
        side_1 = jnp.concatenate([jnp.where(self.first, o, c) for c, o in zip(self.current, other)], axis=0)
        half = self.rows // 2
        block = jnp.concatenate([side_0[:half], side_1[:half]], axis=0)
        return block, jnp.concatenate([side_0[half:], side_1[half:]], axis=0)


def shards(slab, owner, leaf_reflectors, leaf_factors, tree_reflectors, tree_mixers):
    rows_dev, columns = slab.shape
    width = leaf_factors.shape[1]
    panels = owner.shape[0]
    levels = lax.axis_size("row").bit_length() - 1

    def bounds(panel_no):
        parts = CUTS[min(panel_no, len(CUTS) - 1)]
        edges = [0]
        for part in parts:
            edges.append(edges[-1] + columns * part // sum(parts))
        return list(zip(edges[:-1], edges[1:]))

    casts = [
        Broadcast(
            leaf_reflectors[p], leaf_factors[p], owner[p], p * width, 1 if p else STREAMS
        )
        for p in range(panels)
    ]
    lower = slab
    tops, chunks = [], []
    marks = {"none": None}
    for panel_no, cast in enumerate(casts):
        later = panel_no > 0
        cast.begin(marks[GATE_0] if later else None)
        for number in range(len(cast.exchanges)):
            cast.exchange(number, (marks[GATE_1] if number == 0 else marks[GATE_2]) if later else None)
            if number == len(cast.exchanges) - 1:
                marks["arrived"] = cast.arrived[-1]
            if number == 0:
                marks["arrived_first"] = cast.arrived[-1]
        block, factor = cast.end(marks[GATE_3] if later else None)
        marks["other"] = cast.arrived[-1]
        scaled = dot_t(factor, dot_t(block, lower))
        top = lower[:width] - dot(block[:width], scaled)
        lower = lower[width:] - dot(block[width:], scaled)
        tops.append(top)
        row = []
        for start, stop in bounds(panel_no):
            piece = top[:, start:stop]
            own = dot_t(tree_reflectors[panel_no, 0], piece)
            if ALONE and row:
                own = after(own, row[0][2])
            row.append([piece, own, from_partner(own, 0)])
        chunks.append(row)
        marks["own"] = row[0][1]
        marks["theirs"] = row[0][2]
    for panel_no in range(panels):
        for level_no in range(levels - 1):
            for chunk in chunks[panel_no]:
                piece, own, theirs = chunk
                both = own + theirs
                if FIRST_AFTER and panel_no == 0:
                    both = after(both, chunks[1][0][1])
                piece = piece - dot(tree_mixers[panel_no, level_no], both)
                own = dot_t(tree_reflectors[panel_no, level_no + 1], piece)
                chunk[:] = [piece, own, from_partner(own, level_no + 1)]
    if UPDATE:
        result = jnp.concatenate(tops + [lower], axis=0)
    else:
        rows_out = []
    for panel_no in range(panels):
        pieces = []
        for (start, stop), (piece, own, theirs) in zip(bounds(panel_no), chunks[panel_no]):
            piece = piece - dot(tree_mixers[panel_no, levels - 1], own + theirs)
            if UPDATE:
                result = lax.dynamic_update_slice(result, piece, (panel_no * width, start))
            pieces.append(piece)
        if not UPDATE:
            rows_out.append(jnp.concatenate(pieces, axis=1))
    if not UPDATE:
        result = jnp.concatenate(rows_out + [lower], axis=0)
    return result


def solution(mesh):
    return jax.shard_map(
        shards,
        mesh=mesh,
        in_specs=(
            P("row", "col"),
            P(),
            P(None, "row", "col"),
            P(None, "row", "col"),
            P(None, None, "row", None),
            P(None, None, "row", None),
        ),
        out_specs=P("row", "col"),
        check_vma=False,
    )
```

time: 186 us -> 153 us (0.82)
  waiting for transfers between devices: 118 us -> 104 us
  starting transfers between devices: 32.4 us -> 21.7 us
  between operations: 5.39 us -> 1.79 us
  other arithmetic: 5.58 us -> 2.65 us
  matrix products: 20.8 us -> 18 us
    ppermute x16 -> x8, waiting for transfers between devices: 96.7 us -> 82.8 us  [from_partner(): lax.ppermute(shard, 'row', [(i, i ^ 1 << apart) for i in range(lax.axis_s...]
    ppermute x16 -> x8, starting transfers between devices: 22.9 us -> 11.8 us  [from_partner(): lax.ppermute(shard, 'row', [(i, i ^ 1 << apart) for i in range(lax.axis_s...]
    concatenate x1, other arithmetic: 2.59 us -> 0.57 us  [shards(): result = jnp.concatenate(tops + [lower], axis=0)]
    dot_general x20 -> x12, matrix products: 9.4 us -> 7.95 us  [dot(): jnp.dot(a, b, precision=PRECISION, preferred_element_type=jnp.float32)]
    dot_general x20 -> x12, matrix products: 11.4 us -> 10.1 us  [dot_t(): lax.dot_general(a, b, LEADING, precision=PRECISION, preferred_element_typ...]
  transfers between devices with their start and end apart: 24 -> 16, of which waited for: 18 -> 12; matrix products, arithmetic and copies ran while one was open for 7% -> 14% of each run, Pallas kernels for 0% -> 0%
where the time goes in v3:
time: 153 us; the launch traced here: 152 us
  waiting for transfers between devices  104 us (68%)
  starting transfers between devices  21.7 us (14%)
  matrix products  18 us (12%)
  local copies, waits for them, and re-layouts  4.36 us (3%)
  other arithmetic  2.65 us (2%)
  between operations  1.79 us (1%)
    ppermute x8, waiting for transfers between devices, from_partner(): lax.ppermute(shard, 'row', [(i, i ^ 1 << apart) for i in range(lax.axis_s...  82.8 us
    ppermute x4, waiting for transfers between devices, exchange(): self.arrived = [lax.ppermute(c, 'col', pairs) for c in self.current]  20.5 us
    ppermute x8, starting transfers between devices, from_partner(): lax.ppermute(shard, 'row', [(i, i ^ 1 << apart) for i in range(lax.axis_s...  11.8 us
    dot_general x12, matrix products, dot_t(): lax.dot_general(a, b, LEADING, precision=PRECISION, preferred_element_typ...  10.1 us
    ppermute x4, starting transfers between devices, exchange(): self.arrived = [lax.ppermute(c, 'col', pairs) for c in self.current]  9.18 us
    dot_general x12, matrix products, dot(): jnp.dot(a, b, precision=PRECISION, preferred_element_type=jnp.float32)  7.95 us
  transfers between devices with their start and end apart: 16, of which 12 were waited for; matrix products, arithmetic and copies ran while one was open for 14% of the time, Pallas kernels for 0%

profile of v3, /device:TPU:0, one launch (start us, length us, event | category | flops | bytes accessed | tf_op | source)
XLA Modules:
  0.0 152.4 jit_solution(17172900362502322963)
XLA Ops:
  0.0 1.1 slice_bitcast_fusion.5
  1.1 1.3 slice_bitcast_fusion.1
  5.0 2.9 %collective-permute-start.1 = (f32[640,256]{1,0:T(8,128)S(1)}, f32[640,256]{1,0:T(8,128)S(1)}, u32[]{:S(2)}, u32[]{:S(2)}) collective-permute-start(f32[640,256]{1,0:T(8,128)S(1)} %select_select_fusion), channel_id=1, source_target_pairs={{0,2},{1,5},{2,0},{3,7},{4,6},{5,1},{6,4},{7,3},{8,10},{9,13},{10,... | collective-permute-start | bytes 1966088 | tf_op jit(solution)/shard_map/ppermute | solution.py:88
  8.0 8.6 %collective-permute-done.1 = f32[640,256]{1,0:T(8,128)S(1)} collective-permute-done((f32[640,256]{1,0:T(8,128)S(1)}, f32[640,256]{1,0:T(8,128)S(1)}, u32[]{:S(2)}, u32[]{:S(2)}) %collective-permute-start.1) | collective-permute-done | bytes 655392 | tf_op jit(solution)/shard_map/ppermute | solution.py:88
  16.6 2.1 %collective-permute-start.2 = (f32[640,256]{1,0:T(8,128)S(1)}, f32[640,256]{1,0:T(8,128)S(1)}, u32[]{:S(2)}, u32[]{:S(2)}) collective-permute-start(f32[640,256]{1,0:T(8,128)S(1)} %broadcast_select_fusion), channel_id=1, source_target_pairs={{0,4},{1,3},{2,6},{3,1},{4,0},{5,7},{6,2},{7,5},{8,12},{9,11},{10,... | collective-permute-start | bytes 1966088 | tf_op jit(solution)/shard_map/ppermute | solution.py:88
  18.7 1.2 slice_bitcast_fusion.3
  20.1 7.2 %collective-permute-done.2 = f32[640,256]{1,0:T(8,128)S(1)} collective-permute-done((f32[640,256]{1,0:T(8,128)S(1)}, f32[640,256]{1,0:T(8,128)S(1)}, u32[]{:S(2)}, u32[]{:S(2)}) %collective-permute-start.2) | collective-permute-done | bytes 655392 | tf_op jit(solution)/shard_map/ppermute | solution.py:88
  28.2 1.3 select_select_fusion.1
  29.5 2.1 %collective-permute-start.5 = (f32[512,256]{1,0:T(8,128)S(1)}, f32[512,256]{1,0:T(8,128)S(1)}, u32[]{:S(2)}, u32[]{:S(2)}) collective-permute-start(f32[512,256]{1,0:T(8,128)S(1)} %select_select_fusion.1), channel_id=1, source_target_pairs={{0,2},{1,5},{2,0},{3,7},{4,6},{5,1},{6,4},{7,3},{8,10},{9,13},{10,... | collective-permute-start | bytes 1572872 | tf_op jit(solution)/shard_map/ppermute | solution.py:88
  31.7 2.1 %fusion.12 = f32[256,1024]{1,0:T(8,128)S(1)} fusion(f32[1024,1024]{1,0:T(8,128)S(1)} %copy-done, f32[512,256]{1,0:T(8,128)S(1)} %slice.219, f32[512,256]{1,0:T(8,128)S(1)} %slice.218), kind=kOutput, calls=%fused_computation.33 | convolution fusion | flops 1610874880 | bytes 6291456 | tf_op jit(solution)/shard_map/dot_general | solution.py:24
  33.9 0.7 fusion.42
  35.7 1.6 %collective-permute-start.8 = (f32[256,512]{1,0:T(8,128)S(1)}, f32[256,512]{1,0:T(8,128)S(1)}, u32[]{:S(2)}, u32[]{:S(2)}) collective-permute-start(f32[256,512]{1,0:T(8,128)S(1)} %convolution_bitcast_fusion.15), channel_id=1, source_target_pairs={{0,8},{8,0},{16,24},{24,16},{1,9},{9,1},{17,25},{25,17},{2,10},{10... | collective-permute-start | bytes 1572872 | tf_op jit(solution)/shard_map/ppermute | solution.py:28
  37.4 1.3 collective-permute-done.5
  38.8 2.1 %collective-permute-start.6 = (f32[512,256]{1,0:T(8,128)S(1)}, f32[512,256]{1,0:T(8,128)S(1)}, u32[]{:S(2)}, u32[]{:S(2)}) collective-permute-start(f32[512,256]{1,0:T(8,128)S(1)} %broadcast_select_fusion.4), channel_id=1, source_target_pairs={{0,4},{1,3},{2,6},{3,1},{4,0},{5,7},{6,2},{7,5},{8,12},{9,11},{10,... | collective-permute-start | bytes 1572872 | tf_op jit(solution)/shard_map/ppermute | solution.py:88
  41.5 1.6 %collective-permute-start.10 = (f32[256,512]{0,1:T(8,128)S(1)}, f32[256,512]{0,1:T(8,128)S(1)}, u32[]{:S(2)}, u32[]{:S(2)}) collective-permute-start(f32[256,512]{0,1:T(8,128)S(1)} %convolution_bitcast_fusion.11), channel_id=1, source_target_pairs={{0,8},{8,0},{16,24},{24,16},{1,9},{9,1},{17,25},{25,17},{2,10},{10... | collective-permute-start | bytes 1572872 | tf_op jit(solution)/shard_map/ppermute | solution.py:28
  43.1 1.5 slice_subtract_fusion
  44.6 3.4 %collective-permute-done.6 = f32[512,256]{1,0:T(8,128)S(1)} collective-permute-done((f32[512,256]{1,0:T(8,128)S(1)}, f32[512,256]{1,0:T(8,128)S(1)}, u32[]{:S(2)}, u32[]{:S(2)}) %collective-permute-start.6) | collective-permute-done | bytes 524320 | tf_op jit(solution)/shard_map/ppermute | solution.py:88
  48.2 2.4 %collective-permute-done.8 = f32[256,512]{1,0:T(8,128)S(1)} collective-permute-done((f32[256,512]{1,0:T(8,128)S(1)}, f32[256,512]{1,0:T(8,128)S(1)}, u32[]{:S(2)}, u32[]{:S(2)}) %collective-permute-start.8) | collective-permute-done | bytes 524320 | tf_op jit(solution)/shard_map/ppermute | solution.py:28
  51.6 2.6 %collective-permute-start.9 = (f32[256,512]{0,1:T(8,128)S(1)}, f32[256,512]{0,1:T(8,128)S(1)}, u32[]{:S(2)}, u32[]{:S(2)}) collective-permute-start(f32[256,512]{0,1:T(8,128)S(1)} %convolution_bitcast_fusion.13), channel_id=1, source_target_pairs={{0,16},{8,24},{16,0},{24,8},{1,17},{9,25},{17,1},{25,9},{2,18},{10... | collective-permute-start | bytes 1572872 | tf_op jit(solution)/shard_map/ppermute | solution.py:28
  54.2 16.2 %collective-permute-done.10 = f32[256,512]{0,1:T(8,128)S(1)} collective-permute-done((f32[256,512]{0,1:T(8,128)S(1)}, f32[256,512]{0,1:T(8,128)S(1)}, u32[]{:S(2)}, u32[]{:S(2)}) %collective-permute-start.10) | collective-permute-done | bytes 524320 | tf_op jit(solution)/shard_map/ppermute | solution.py:28
  71.7 1.6 %fusion.19 = f32[256,1024]{1,0:T(8,128)S(1)} fusion(f32[768,1024]{1,0:T(8,128)S(1)} %slice_subtract_fusion, f32[384,256]{1,0:T(8,128)S(1)} %slice.228, f32[384,256]{1,0:T(8,128)S(1)} %slice.227), kind=kOutput, calls=%fused_computation.40 | convolution fusion | flops 1208156160 | bytes 4980736 | tf_op jit(solution)/shard_map/dot_general | solution.py:24
  73.3 0.9 fusion.46
  74.2 1.1 slice_subtract_fusion.1
  76.5 1.9 %collective-permute-start.12 = (f32[256,512]{0,1:T(8,128)S(1)}, f32[256,512]{0,1:T(8,128)S(1)}, u32[]{:S(2)}, u32[]{:S(2)}) collective-permute-start(f32[256,512]{0,1:T(8,128)S(1)} %convolution_bitcast_fusion.7), channel_id=1, source_target_pairs={{0,8},{8,0},{16,24},{24,16},{1,9},{9,1},{17,25},{25,17},{2,10},{10... | collective-permute-start | bytes 1572872 | tf_op jit(solution)/shard_map/ppermute | solution.py:28
  79.9 9.7 %collective-permute-done.9 = f32[256,512]{0,1:T(8,128)S(1)} collective-permute-done((f32[256,512]{0,1:T(8,128)S(1)}, f32[256,512]{0,1:T(8,128)S(1)}, u32[]{:S(2)}, u32[]{:S(2)}) %collective-permute-start.9) | collective-permute-done | bytes 524320 | tf_op jit(solution)/shard_map/ppermute | solution.py:28
  90.0 14.6 %collective-permute-done.12 = f32[256,512]{0,1:T(8,128)S(1)} collective-permute-done((f32[256,512]{0,1:T(8,128)S(1)}, f32[256,512]{0,1:T(8,128)S(1)}, u32[]{:S(2)}, u32[]{:S(2)}) %collective-permute-start.12) | collective-permute-done | bytes 524320 | tf_op jit(solution)/shard_map/ppermute | solution.py:28
  105.7 2.8 %collective-permute-start.13 = (f32[256,512]{0,1:T(8,128)S(1)}, f32[256,512]{0,1:T(8,128)S(1)}, u32[]{:S(2)}, u32[]{:S(2)}) collective-permute-start(f32[256,512]{0,1:T(8,128)S(1)} %convolution_bitcast_fusion.5), channel_id=1, source_target_pairs={{0,16},{8,24},{16,0},{24,8},{1,17},{9,25},{17,1},{25,9},{2,18},{10... | collective-permute-start | bytes 1572872 | tf_op jit(solution)/shard_map/ppermute | solution.py:28
  108.4 7.8 %collective-permute-done.14 = f32[256,512]{0,1:T(8,128)S(1)} collective-permute-done((f32[256,512]{0,1:T(8,128)S(1)}, f32[256,512]{0,1:T(8,128)S(1)}, u32[]{:S(2)}, u32[]{:S(2)}) %collective-permute-start.14) | collective-permute-done | bytes 524320 | tf_op jit(solution)/shard_map/ppermute | solution.py:28
  117.3 0.9 collective-permute-start.15
  118.6 23.4 %collective-permute-done.13 = f32[256,512]{0,1:T(8,128)S(1)} collective-permute-done((f32[256,512]{0,1:T(8,128)S(1)}, f32[256,512]{0,1:T(8,128)S(1)}, u32[]{:S(2)}, u32[]{:S(2)}) %collective-permute-start.13) | collective-permute-done | bytes 524320 | tf_op jit(solution)/shard_map/ppermute | solution.py:28
  142.4 8.8 %collective-permute-done.15 = f32[256,512]{0,1:T(8,128)S(1)} collective-permute-done((f32[256,512]{0,1:T(8,128)S(1)}, f32[256,512]{0,1:T(8,128)S(1)}, u32[]{:S(2)}, u32[]{:S(2)}) %collective-permute-start.15) | collective-permute-done | bytes 524320 | tf_op jit(solution)/shard_map/ppermute | solution.py:28
  151.2 1.2 fusion.11
  (59 shorter events, 12.6 us)
Async XLA Ops:
  0.0 3.0 %copy-start.4 = (s32[2]{0:T(128)S(1)}, s32[2]{0:T(128)}, u32[]{:S(2)}) copy-start(s32[2]{0:T(128)} %param.7) | copy-start | bytes 28
  2.5 2.4 %collective-permute-start = (f32[640,256]{1,0:T(8,128)S(1)}, f32[640,256]{1,0:T(8,128)}, u32[]{:S(2)}, u32[]{:S(2)}) collective-permute-start(f32[640,256]{1,0:T(8,128)S(1)} %fusion.23), channel_id=1, source_target_pairs={{0,1},{1,0},{2,3},{3,2},{4,5},{5,4},{6,7},{7,6},{8,9},{9,8},{10,11... | collective-permute-start | bytes 1966088 | tf_op jit(solution)/shard_map/ppermute | solution.py:32
  5.0 11.5 %collective-permute-start.1 = (f32[640,256]{1,0:T(8,128)S(1)}, f32[640,256]{1,0:T(8,128)S(1)}, u32[]{:S(2)}, u32[]{:S(2)}) collective-permute-start(f32[640,256]{1,0:T(8,128)S(1)} %select_select_fusion), channel_id=1, source_target_pairs={{0,2},{1,5},{2,0},{3,7},{4,6},{5,1},{6,4},{7,3},{8,10},{9,13},{10,... | collective-permute-start | bytes 1966088 | tf_op jit(solution)/shard_map/ppermute | solution.py:88
  16.6 10.7 %collective-permute-start.2 = (f32[640,256]{1,0:T(8,128)S(1)}, f32[640,256]{1,0:T(8,128)S(1)}, u32[]{:S(2)}, u32[]{:S(2)}) collective-permute-start(f32[640,256]{1,0:T(8,128)S(1)} %broadcast_select_fusion), channel_id=1, source_target_pairs={{0,4},{1,3},{2,6},{3,1},{4,0},{5,7},{6,2},{7,5},{8,12},{9,11},{10,... | collective-permute-start | bytes 1966088 | tf_op jit(solution)/shard_map/ppermute | solution.py:88
  20.0 8.2 %collective-permute-start.4 = (f32[512,256]{1,0:T(8,128)S(1)}, f32[512,256]{1,0:T(8,128)}, u32[]{:S(2)}, u32[]{:S(2)}) collective-permute-start(f32[512,256]{1,0:T(8,128)S(1)} %fusion.39), channel_id=1, source_target_pairs={{0,1},{1,0},{2,3},{3,2},{4,5},{5,4},{6,7},{7,6},{8,9},{9,8},{10,11... | collective-permute-start | bytes 1572872 | tf_op jit(solution)/shard_map/ppermute | solution.py:32
  27.4 4.1 %collective-permute-start.3 = (f32[640,256]{1,0:T(8,128)S(1)}, f32[640,256]{1,0:T(8,128)S(1)}, u32[]{:S(2)}, u32[]{:S(2)}) collective-permute-start(f32[640,256]{1,0:T(8,128)S(1)} %broadcast_select_fusion.1), channel_id=1, source_target_pairs={{0,1},{1,0},{2,3},{3,2},{4,5},{5,4},{6,7},{7,6},{8,9},{9,8},{10,11... | collective-permute-start | bytes 1966088 | tf_op jit(solution)/shard_map/ppermute | solution.py:32
  28.1 3.6 %copy-start = (f32[1024,1024]{1,0:T(8,128)S(1)}, f32[1024,1024]{1,0:T(8,128)}, u32[]{:S(2)}) copy-start(f32[1024,1024]{1,0:T(8,128)} %param.6) | copy-start | bytes 12582916
  29.5 9.2 %collective-permute-start.5 = (f32[512,256]{1,0:T(8,128)S(1)}, f32[512,256]{1,0:T(8,128)S(1)}, u32[]{:S(2)}, u32[]{:S(2)}) collective-permute-start(f32[512,256]{1,0:T(8,128)S(1)} %select_select_fusion.1), channel_id=1, source_target_pairs={{0,2},{1,5},{2,0},{3,7},{4,6},{5,1},{6,4},{7,3},{8,10},{9,13},{10,... | collective-permute-start | bytes 1572872 | tf_op jit(solution)/shard_map/ppermute | solution.py:88
  33.9 1.4 copy-start.1
  35.7 14.8 %collective-permute-start.8 = (f32[256,512]{1,0:T(8,128)S(1)}, f32[256,512]{1,0:T(8,128)S(1)}, u32[]{:S(2)}, u32[]{:S(2)}) collective-permute-start(f32[256,512]{1,0:T(8,128)S(1)} %convolution_bitcast_fusion.15), channel_id=1, source_target_pairs={{0,8},{8,0},{16,24},{24,16},{1,9},{9,1},{17,25},{25,17},{2,10},{10... | collective-permute-start | bytes 1572872 | tf_op jit(solution)/shard_map/ppermute | solution.py:28
  38.8 9.2 %collective-permute-start.6 = (f32[512,256]{1,0:T(8,128)S(1)}, f32[512,256]{1,0:T(8,128)S(1)}, u32[]{:S(2)}, u32[]{:S(2)}) collective-permute-start(f32[512,256]{1,0:T(8,128)S(1)} %broadcast_select_fusion.4), channel_id=1, source_target_pairs={{0,4},{1,3},{2,6},{3,1},{4,0},{5,7},{6,2},{7,5},{8,12},{9,11},{10,... | collective-permute-start | bytes 1572872 | tf_op jit(solution)/shard_map/ppermute | solution.py:88
  41.5 9.0 %copy-start.2 = (f32[2,2,256,256]{3,2,1,0:T(8,128)S(1)}, f32[2,2,256,256]{3,2,1,0:T(8,128)}, u32[]{:S(2)}) copy-start(f32[2,2,256,256]{3,2,1,0:T(8,128)} %param.11) | copy-start | bytes 3145732
  41.5 28.9 %collective-permute-start.10 = (f32[256,512]{0,1:T(8,128)S(1)}, f32[256,512]{0,1:T(8,128)S(1)}, u32[]{:S(2)}, u32[]{:S(2)}) collective-permute-start(f32[256,512]{0,1:T(8,128)S(1)} %convolution_bitcast_fusion.11), channel_id=1, source_target_pairs={{0,8},{8,0},{16,24},{24,16},{1,9},{9,1},{17,25},{25,17},{2,10},{10... | collective-permute-start | bytes 1572872 | tf_op jit(solution)/shard_map/ppermute | solution.py:28
  48.1 23.4 %collective-permute-start.7 = (f32[512,256]{1,0:T(8,128)S(1)}, f32[512,256]{1,0:T(8,128)S(1)}, u32[]{:S(2)}, u32[]{:S(2)}) collective-permute-start(f32[512,256]{1,0:T(8,128)S(1)} %broadcast_select_fusion.5), channel_id=1, source_target_pairs={{0,1},{1,0},{2,3},{3,2},{4,5},{5,4},{6,7},{7,6},{8,9},{9,8},{10,11... | collective-permute-start | bytes 1572872 | tf_op jit(solution)/shard_map/ppermute | solution.py:32
  51.6 38.0 %collective-permute-start.9 = (f32[256,512]{0,1:T(8,128)S(1)}, f32[256,512]{0,1:T(8,128)S(1)}, u32[]{:S(2)}, u32[]{:S(2)}) collective-permute-start(f32[256,512]{0,1:T(8,128)S(1)} %convolution_bitcast_fusion.13), channel_id=1, source_target_pairs={{0,16},{8,24},{16,0},{24,8},{1,17},{9,25},{17,1},{25,9},{2,18},{10... | collective-permute-start | bytes 1572872 | tf_op jit(solution)/shard_map/ppermute | solution.py:28
  71.4 46.8 %collective-permute-start.11 = (f32[256,512]{0,1:T(8,128)S(1)}, f32[256,512]{0,1:T(8,128)S(1)}, u32[]{:S(2)}, u32[]{:S(2)}) collective-permute-start(f32[256,512]{0,1:T(8,128)S(1)} %convolution_bitcast_fusion.9), channel_id=1, source_target_pairs={{0,16},{8,24},{16,0},{24,8},{1,17},{9,25},{17,1},{25,9},{2,18},{10... | collective-permute-start | bytes 1572872 | tf_op jit(solution)/shard_map/ppermute | solution.py:28
  76.5 28.1 %collective-permute-start.12 = (f32[256,512]{0,1:T(8,128)S(1)}, f32[256,512]{0,1:T(8,128)S(1)}, u32[]{:S(2)}, u32[]{:S(2)}) collective-permute-start(f32[256,512]{0,1:T(8,128)S(1)} %convolution_bitcast_fusion.7), channel_id=1, source_target_pairs={{0,8},{8,0},{16,24},{24,16},{1,9},{9,1},{17,25},{25,17},{2,10},{10... | collective-permute-start | bytes 1572872 | tf_op jit(solution)/shard_map/ppermute | solution.py:28
  79.1 37.1 %collective-permute-start.14 = (f32[256,512]{0,1:T(8,128)S(1)}, f32[256,512]{0,1:T(8,128)S(1)}, u32[]{:S(2)}, u32[]{:S(2)}) collective-permute-start(f32[256,512]{0,1:T(8,128)S(1)} %convolution_bitcast_fusion.3), channel_id=1, source_target_pairs={{0,8},{8,0},{16,24},{24,16},{1,9},{9,1},{17,25},{25,17},{2,10},{10... | collective-permute-start | bytes 1572872 | tf_op jit(solution)/shard_map/ppermute | solution.py:28
  105.7 36.3 %collective-permute-start.13 = (f32[256,512]{0,1:T(8,128)S(1)}, f32[256,512]{0,1:T(8,128)S(1)}, u32[]{:S(2)}, u32[]{:S(2)}) collective-permute-start(f32[256,512]{0,1:T(8,128)S(1)} %convolution_bitcast_fusion.5), channel_id=1, source_target_pairs={{0,16},{8,24},{16,0},{24,8},{1,17},{9,25},{17,1},{25,9},{2,18},{10... | collective-permute-start | bytes 1572872 | tf_op jit(solution)/shard_map/ppermute | solution.py:28
  117.3 33.9 %collective-permute-start.15 = (f32[256,512]{0,1:T(8,128)S(1)}, f32[256,512]{0,1:T(8,128)S(1)}, u32[]{:S(2)}, u32[]{:S(2)}) collective-permute-start(f32[256,512]{0,1:T(8,128)S(1)} %convolution_bitcast_fusion.1), channel_id=1, source_target_pairs={{0,16},{8,24},{16,0},{24,8},{1,17},{9,25},{17,1},{25,9},{2,18},{10... | collective-permute-start | bytes 1572872 | tf_op jit(solution)/shard_map/ppermute | solution.py:28
  142.4 8.8 %copy-start.3 = (f32[1024,1024]{1,0:T(8,128)}, f32[1024,1024]{1,0:T(8,128)S(1)}, u32[]{:S(2)}) copy-start(f32[1024,1024]{1,0:T(8,128)S(1)} %fusion.8) | copy-start | bytes 12582916

commit v4 on v3

v4 whole, which is shorter than its diff:
```python
import jax
import jax.numpy as jnp
from jax import lax
from jax.sharding import PartitionSpec as P

PRECISION = lax.Precision.HIGH
LEADING = (((0,), (0,)), ((), ()))
CUTS = ((1, 1, 1, 1), (1, 1))
STREAMS = 1
DYNAMIC = True
PLAN = (
    ("begin0", ""),
    ("move0.0", ""),
    ("move0.1", ""),
    ("end0", ""),
    ("send0.0", ""),
    ("leaf0", ""),
    ("send0.1", ""),
    ("send0.2", "got0.0"),
    ("send0.3", "got0.0"),
    ("begin1", ""),
    ("move1.0", "own0.0"),
    ("move1.1", ""),
    ("end1", ""),
    ("leaf1", ""),
    ("send1.0", ""),
    ("send1.1", "got1.0"),
    ("tree0.0", ""),
    ("tree0.1", "own0.3"),
    ("tree0.2", ""),
    ("tree0.3", "own1.0"),
    ("tree1.0", ""),
    ("tree1.1", ""),
    ("last0.0", ""),
    ("last0.1", ""),
    ("last0.2", ""),
    ("last0.3", ""),
    ("last1.0", ""),
    ("last1.1", ""),
)


def dot(a, b):
    return jnp.dot(a, b, precision=PRECISION, preferred_element_type=jnp.float32)


def dot_t(a, b):
    return lax.dot_general(a, b, LEADING, precision=PRECISION, preferred_element_type=jnp.float32)


def from_partner(shard, apart):
    return lax.ppermute(shard, "row", [(i, i ^ 1 << apart) for i in range(lax.axis_size("row"))])


def swap_cores(shard):
    return lax.ppermute(shard, "col", [(i, i ^ 1) for i in range(lax.axis_size("col"))])


def never(held, columns):
    row = held[:1, : min(columns, held.shape[1])]
    if columns > row.shape[1]:
        row = jnp.tile(row, (1, columns // row.shape[1]))
    return row != row


def after(value, held):
    if held is None:
        return value
    return jnp.where(never(held, value.shape[1]), -value, value)


class Broadcast:
    def __init__(self, reflectors, factors, owner, first_row, streams):
        size = lax.axis_size("col")
        self.me = lax.axis_index("col")
        self.first = self.me % 2 == 0
        self.owner = owner
        self.rows = reflectors.shape[0] - first_row
        self.width = factors.shape[0]
        middle = first_row + self.rows // 2
        part = (self.rows + self.width) // 2 // streams
        cut = [slice(k * part, (k + 1) * part) for k in range(streams)]
        if DYNAMIC:

            def half(number):
                rows = lax.dynamic_slice_in_dim(
                    reflectors, first_row + number * (self.rows // 2), self.rows // 2, 0
                )
                factor = lax.dynamic_slice_in_dim(factors, number * (self.width // 2), self.width // 2, 0)
                return jnp.concatenate([rows, factor], axis=0)

            mine = half(self.me % 2)
            other = half(1 - self.me % 2)
        else:
            block_0 = jnp.concatenate([reflectors[first_row:middle], factors[: self.width // 2]], axis=0)
            block_1 = jnp.concatenate([reflectors[middle:], factors[self.width // 2 :]], axis=0)
            mine = jnp.where(self.first, block_0, block_1)
            other = jnp.where(self.first, block_1, block_0)
        self.mine, self.sent = [mine[c] for c in cut], [other[c] for c in cut]
        bits = [1 << k for k in range(1, size.bit_length() - 1)]
        turned = bits[len(bits) // 2 :] + bits[: len(bits) // 2]
        self.exchanges = [
            (
                [(i, i ^ (odd if i % 2 else even)) for i in range(size)],
                jnp.where(self.first, even, odd),
            )
            for even, odd in zip(bits, turned)
        ]
        self.bit = 1

    def begin(self, held=None):
        self.arrived = [swap_cores(after(s, held)) for s in self.sent]
        self.current = self.mine

    def select(self, held):
        keep = (self.me ^ self.owner) & self.bit == 0
        result = []
        for current, arrived in zip(self.current, self.arrived):
            if held is not None:
                keep = jnp.logical_or(keep, never(held, current.shape[1]))
            result.append(jnp.where(keep, current, arrived))
        self.current = result

    def exchange(self, number, held=None):
        self.select(held)
        pairs, self.bit = self.exchanges[number]
        self.arrived = [lax.ppermute(c, "col", pairs) for c in self.current]

    def end(self, held=None):
        self.select(held)
        other = [swap_cores(c) for c in self.current]
        self.arrived = other
        side_0 = jnp.concatenate([jnp.where(self.first, c, o) for c, o in zip(self.current, other)], axis=0)
        side_1 = jnp.concatenate([jnp.where(self.first, o, c) for c, o in zip(self.current, other)], axis=0)
        half = self.rows // 2
        block = jnp.concatenate([side_0[:half], side_1[:half]], axis=0)
        return block, jnp.concatenate([side_0[half:], side_1[half:]], axis=0)


def shards(slab, owner, leaf_reflectors, leaf_factors, tree_reflectors, tree_mixers):
    rows_dev, columns = slab.shape
    width = leaf_factors.shape[1]
    panels = owner.shape[0]
    levels = lax.axis_size("row").bit_length() - 1

    def bounds(panel_no):
        parts = CUTS[min(panel_no, len(CUTS) - 1)]
        edges = [0]
        for part in parts:
            edges.append(edges[-1] + columns * part // sum(parts))
        return list(zip(edges[:-1], edges[1:]))

    casts = [
        Broadcast(
            leaf_reflectors[p], leaf_factors[p], owner[p], p * width, 1 if p else STREAMS
        )
        for p in range(panels)
    ]
    blocks = [None] * panels
    tops = [None] * panels
    chunks = [{} for _ in range(panels)]
    edges = [bounds(p) for p in range(panels)]
    marks = {}
    lower = [slab]
    result = None

    def leaf(panel_no):
        block, factor = blocks[panel_no]
        matrix = lower[-1]
        scaled = dot_t(factor, dot_t(block, matrix))
        tops[panel_no] = matrix[:width] - dot(block[:width], scaled)
        lower.append(matrix[width:] - dot(block[width:], scaled))

    def head(panel_no, chunk):
        block, factor = blocks[panel_no]
        start, stop = edges[panel_no][chunk]
        part = lower[-1][:, start:stop]
        scaled = dot_t(factor, dot_t(block, part))
        return part[:width] - dot(block[:width], scaled)

    def send(panel_no, chunk, held):
        start, stop = edges[panel_no][chunk]
        piece = head(panel_no, chunk) if tops[panel_no] is None else tops[panel_no][:, start:stop]
        own = after(dot_t(tree_reflectors[panel_no, 0], piece), held)
        theirs = from_partner(own, 0)
        chunks[panel_no][chunk] = [piece, own, theirs, 0]
        marks[f"own{panel_no}.{chunk}"] = own
        marks[f"got{panel_no}.{chunk}"] = theirs

    def tree(panel_no, chunk, held):
        piece, own, theirs, level_no = chunks[panel_no][chunk]
        piece = piece - dot(tree_mixers[panel_no, level_no], after(own + theirs, held))
        own = dot_t(tree_reflectors[panel_no, level_no + 1], piece)
        theirs = from_partner(own, level_no + 1)
        chunks[panel_no][chunk] = [piece, own, theirs, level_no + 1]
        marks[f"up{panel_no}.{chunk}"] = own
        marks[f"gup{panel_no}.{chunk}"] = theirs

    def last(panel_no, chunk, held):
        nonlocal result
        if result is None:
            result = jnp.concatenate(tops + lower[-1:], axis=0)
        piece, own, theirs, level_no = chunks[panel_no][chunk]
        piece = piece - dot(tree_mixers[panel_no, level_no], after(own + theirs, held))
        marks[f"end{panel_no}.{chunk}"] = piece
        result = lax.dynamic_update_slice(result, piece, (panel_no * width, edges[panel_no][chunk][0]))

    for text, mark in PLAN:
        held = marks[mark] if mark else None
        name, numbers = text.rstrip("0123456789."), text[len(text.rstrip("0123456789.")) :].split(".")
        panel_no = int(numbers[0])
        if panel_no >= panels:
            continue
        if name == "begin":
            casts[panel_no].begin(held)
        elif name == "move":
            if int(numbers[1]) == 0:
                casts[panel_no].exchange(0, held)
                marks[f"arr{panel_no}.0"] = casts[panel_no].arrived[-1]
            else:
                for number in range(1, len(casts[panel_no].exchanges)):
                    casts[panel_no].exchange(number, held)
                marks[f"arr{panel_no}.1"] = casts[panel_no].arrived[-1]
        elif name == "end":
            blocks[panel_no] = casts[panel_no].end(held)
            marks[f"arr{panel_no}.2"] = casts[panel_no].arrived[-1]
        elif name == "leaf":
            leaf(panel_no)
        elif name == "send":
            send(panel_no, int(numbers[1]), held)
        elif name == "tree":
            for _ in range(levels - 1):
                tree(panel_no, int(numbers[1]), held)
        else:
            last(panel_no, int(numbers[1]), held)
    return result


def solution(mesh):
    return jax.shard_map(
        shards,
        mesh=mesh,
        in_specs=(
            P("row", "col"),
            P(),
            P(None, "row", "col"),
            P(None, "row", "col"),
            P(None, None, "row", None),
            P(None, None, "row", None),
        ),
        out_specs=P("row", "col"),
        check_vma=False,
    )
```

time: 153 us -> 146 us (0.954)
  waiting for transfers between devices: 104 us -> 89.1 us
  matrix products: 18 us -> 21.4 us
  starting transfers between devices: 21.7 us -> 24.2 us
    ppermute x8 -> x12, waiting for transfers between devices: 82.8 us -> 68.8 us  [from_partner(): lax.ppermute(shard, 'row', [(i, i ^ 1 << apart) for i in range(lax.axis_s...]
    ppermute x8 -> x12, starting transfers between devices: 11.8 us -> 14.9 us  [from_partner(): lax.ppermute(shard, 'row', [(i, i ^ 1 << apart) for i in range(lax.axis_s...]
    dot_general x12 -> x18, matrix products: 10.1 us -> 12.2 us  [dot_t(): lax.dot_general(a, b, LEADING, precision=PRECISION, preferred_element_typ...]
    unnamed x10, local copies, waits for them, and re-layouts: 0.03 us -> 1.95 us
    dot_general x12 -> x17, matrix products: 7.95 us -> 9.2 us  [dot(): jnp.dot(a, b, precision=PRECISION, preferred_element_type=jnp.float32)]
    slice x3 -> x2, local copies, waits for them, and re-layouts: 3.58 us -> 2.75 us  [the longest x1 1.68 us: shards(): leaf_reflectors[p]]
  transfers between devices with their start and end apart: 16 -> 20, of which waited for: 12 -> 13; matrix products, arithmetic and copies ran while one was open for 14% -> 16% of each run, Pallas kernels for 0% -> 0%
where the time goes in v4:
time: 146 us; the launch traced here: 145 us
  waiting for transfers between devices  89.1 us (61%)
  starting transfers between devices  24.2 us (17%)
  matrix products  21.4 us (15%)
  local copies, waits for them, and re-layouts  5.7 us (4%)
  other arithmetic  3.21 us (2%)
  between operations  1.88 us (1%)
    ppermute x12, waiting for transfers between devices, from_partner(): lax.ppermute(shard, 'row', [(i, i ^ 1 << apart) for i in range(lax.axis_s...  68.8 us
    ppermute x4, waiting for transfers between devices, exchange(): self.arrived = [lax.ppermute(c, 'col', pairs) for c in self.current]  19.8 us
    ppermute x12, starting transfers between devices, from_partner(): lax.ppermute(shard, 'row', [(i, i ^ 1 << apart) for i in range(lax.axis_s...  14.9 us
    dot_general x18, matrix products, dot_t(): lax.dot_general(a, b, LEADING, precision=PRECISION, preferred_element_typ...  12.2 us
    dot_general x17, matrix products, dot(): jnp.dot(a, b, precision=PRECISION, preferred_element_type=jnp.float32)  9.2 us
    ppermute x4, starting transfers between devices, exchange(): self.arrived = [lax.ppermute(c, 'col', pairs) for c in self.current]  8.19 us
  transfers between devices with their start and end apart: 20, of which 13 were waited for; matrix products, arithmetic and copies ran while one was open for 16% of the time, Pallas kernels for 0%

profile of v4, /device:TPU:0, one launch (start us, length us, event | category | flops | bytes accessed | tf_op | source)
XLA Modules:
  0.0 145.5 jit_solution(10481383100425195262)
XLA Ops:
  0.0 1.1 fusion.120
  1.1 1.7 %fusion.119 = (f32[1,1024,256]{2,1,0:T(8,128)S(1)}, f32[1,1024,256]{2,1,0:T(8,128)S(1)}) fusion(f32[2,1024,256]{2,1,0:T(8,128)} %param.8), kind=kLoop, calls=%fused_computation.177 | loop fusion | bytes 4194304 | tf_op jit(solution)/shard_map/slice | solution.py:155
  5.3 2.9 %collective-permute-start.1 = (f32[640,256]{1,0:T(8,128)S(1)}, f32[640,256]{1,0:T(8,128)S(1)}, u32[]{:S(2)}, u32[]{:S(2)}) collective-permute-start(f32[640,256]{1,0:T(8,128)S(1)} %maximum_select_fusion), channel_id=1, source_target_pairs={{0,2},{1,5},{2,0},{3,7},{4,6},{5,1},{6,4},{7,3},{8,10},{9,13},{10,... | collective-permute-start | bytes 1966088 | tf_op jit(solution)/shard_map/ppermute | solution.py:127
  8.2 8.6 %collective-permute-done.1 = f32[640,256]{1,0:T(8,128)S(1)} collective-permute-done((f32[640,256]{1,0:T(8,128)S(1)}, f32[640,256]{1,0:T(8,128)S(1)}, u32[]{:S(2)}, u32[]{:S(2)}) %collective-permute-start.1) | collective-permute-done | bytes 655392 | tf_op jit(solution)/shard_map/ppermute | solution.py:127
  16.9 2.1 %collective-permute-start.2 = (f32[640,256]{1,0:T(8,128)S(1)}, f32[640,256]{1,0:T(8,128)S(1)}, u32[]{:S(2)}, u32[]{:S(2)}) collective-permute-start(f32[640,256]{1,0:T(8,128)S(1)} %broadcast_select_fusion), channel_id=1, source_target_pairs={{0,4},{1,3},{2,6},{3,1},{4,0},{5,7},{6,2},{7,5},{8,12},{9,11},{10,... | collective-permute-start | bytes 1966088 | tf_op jit(solution)/shard_map/ppermute | solution.py:127
  19.0 8.6 %collective-permute-done.2 = f32[640,256]{1,0:T(8,128)S(1)} collective-permute-done((f32[640,256]{1,0:T(8,128)S(1)}, f32[640,256]{1,0:T(8,128)S(1)}, u32[]{:S(2)}, u32[]{:S(2)}) %collective-permute-start.2) | collective-permute-done | bytes 655392 | tf_op jit(solution)/shard_map/ppermute | solution.py:127
  30.0 1.9 %copy-done = f32[1024,1024]{1,0:T(8,128)S(1)} copy-done((f32[1024,1024]{1,0:T(8,128)S(1)}, f32[1024,1024]{1,0:T(8,128)}, u32[]{:S(2)}) %copy-start) | copy-done | bytes 4194328
  32.0 1.0 fusion.18
  34.1 2.1 %collective-permute-start.8 = (f32[256,256]{1,0:T(8,128)S(1)}, f32[256,256]{1,0:T(8,128)S(1)}, u32[]{:S(2)}, u32[]{:S(2)}) collective-permute-start(f32[256,256]{1,0:T(8,128)S(1)} %convolution_bitcast_fusion.23), channel_id=1, source_target_pairs={{0,8},{8,0},{16,24},{24,16},{1,9},{9,1},{17,25},{25,17},{2,10},{10... | collective-permute-start | bytes 786440 | tf_op jit(solution)/shard_map/ppermute | solution.py:52
  36.2 2.1 %fusion.20 = f32[256,1024]{1,0:T(8,128)S(1)} fusion(f32[1024,1024]{1,0:T(8,128)S(1)} %copy-done, f32[512,256]{1,0:T(8,128)S(1)} %slice.193, f32[512,256]{1,0:T(8,128)S(1)} %slice.192), kind=kOutput, calls=%fused_computation.51 | convolution fusion | flops 1610874880 | bytes 6291456 | tf_op jit(solution)/shard_map/dot_general | solution.py:48
  39.1 1.1 maximum_select_fusion.1
  40.2 1.6 %collective-permute-start.5 = (f32[512,256]{1,0:T(8,128)S(1)}, f32[512,256]{1,0:T(8,128)S(1)}, u32[]{:S(2)}, u32[]{:S(2)}) collective-permute-start(f32[512,256]{1,0:T(8,128)S(1)} %maximum_select_fusion.1), channel_id=1, source_target_pairs={{0,2},{1,5},{2,0},{3,7},{4,6},{5,1},{6,4},{7,3},{8,10},{9,13},{10,... | collective-permute-start | bytes 1572872 | tf_op jit(solution)/shard_map/ppermute | solution.py:127
  43.4 1.5 %slice_subtract_fusion = f32[768,1024]{1,0:T(8,128)S(1)} fusion(f32[1024,1024]{1,0:T(8,128)S(1)} %copy-done, f32[256,1024]{1,0:T(8,128)S(1)} %fusion.92, f32[512,256]{1,0:T(8,128)S(1)} %slice.193, f32[512,256]{1,0:T(8,128)S(1)} %slice.192), kind=kOutput, calls=%fused_computation.1 | convolution fusion | flops 1208942592 | bytes 8388608 | tf_op jit(solution)/shard_map/dot_general | solution.py:44
  45.6 2.7 %collective-permute-start.9 = (f32[256,256]{0,1:T(8,128)S(1)}, f32[256,256]{0,1:T(8,128)S(1)}, u32[]{:S(2)}, u32[]{:S(2)}) collective-permute-start(f32[256,256]{0,1:T(8,128)S(1)} %convolution_bitcast_fusion.21), channel_id=1, source_target_pairs={{0,16},{8,24},{16,0},{24,8},{1,17},{9,25},{17,1},{25,9},{2,18},{10... | collective-permute-start | bytes 786440 | tf_op jit(solution)/shard_map/ppermute | solution.py:52
  48.6 1.6 %collective-permute-start.12 = (f32[256,256]{1,0:T(8,128)S(1)}, f32[256,256]{1,0:T(8,128)S(1)}, u32[]{:S(2)}, u32[]{:S(2)}) collective-permute-start(f32[256,256]{1,0:T(8,128)S(1)} %negate_select_fusion.2), channel_id=1, source_target_pairs={{0,8},{8,0},{16,24},{24,16},{1,9},{9,1},{17,25},{25,17},{2,10},{10... | collective-permute-start | bytes 786440 | tf_op jit(solution)/shard_map/ppermute | solution.py:52
  50.3 1.6 %collective-permute-start.6 = (f32[512,256]{1,0:T(8,128)S(1)}, f32[512,256]{1,0:T(8,128)S(1)}, u32[]{:S(2)}, u32[]{:S(2)}) collective-permute-start(f32[512,256]{1,0:T(8,128)S(1)} %broadcast_select_fusion.4), channel_id=1, source_target_pairs={{0,4},{1,3},{2,6},{3,1},{4,0},{5,7},{6,2},{7,5},{8,12},{9,11},{10,... | collective-permute-start | bytes 1572872 | tf_op jit(solution)/shard_map/ppermute | solution.py:127
  52.9 3.6 %collective-permute-done.10 = f32[256,256]{0,1:T(8,128)S(1)} collective-permute-done((f32[256,256]{0,1:T(8,128)S(1)}, f32[256,256]{0,1:T(8,128)S(1)}, u32[]{:S(2)}, u32[]{:S(2)}) %collective-permute-start.10) | collective-permute-done | bytes 262176 | tf_op jit(solution)/shard_map/ppermute | solution.py:52
  56.9 2.7 %collective-permute-done.6 = f32[512,256]{1,0:T(8,128)S(1)} collective-permute-done((f32[512,256]{1,0:T(8,128)S(1)}, f32[512,256]{1,0:T(8,128)S(1)}, u32[]{:S(2)}, u32[]{:S(2)}) %collective-permute-start.6) | collective-permute-done | bytes 524320 | tf_op jit(solution)/shard_map/ppermute | solution.py:127
  60.1 1.8 %collective-permute-start.11 = (f32[256,256]{0,1:T(8,128)S(1)}, f32[256,256]{0,1:T(8,128)S(1)}, u32[]{:S(2)}, u32[]{:S(2)}) collective-permute-start(f32[256,256]{0,1:T(8,128)S(1)} %convolution_bitcast_fusion.16), channel_id=1, source_target_pairs={{0,16},{8,24},{16,0},{24,8},{1,17},{9,25},{17,1},{25,9},{2,18},{10... | collective-permute-start | bytes 786440 | tf_op jit(solution)/shard_map/ppermute | solution.py:52
  62.0 1.4 collective-permute-done.12
  64.2 2.7 %collective-permute-start.13 = (f32[256,256]{0,1:T(8,128)S(1)}, f32[256,256]{0,1:T(8,128)S(1)}, u32[]{:S(2)}, u32[]{:S(2)}) collective-permute-start(f32[256,256]{0,1:T(8,128)S(1)} %convolution_bitcast_fusion.12), channel_id=1, source_target_pairs={{0,16},{8,24},{16,0},{24,8},{1,17},{9,25},{17,1},{25,9},{2,18},{10... | collective-permute-start | bytes 786440 | tf_op jit(solution)/shard_map/ppermute | solution.py:52
  67.1 1.7 %fusion.24 = f32[256,1024]{1,0:T(8,128)S(1)} fusion(f32[768,1024]{1,0:T(8,128)S(1)} %slice_subtract_fusion, f32[384,256]{1,0:T(8,128)S(1)} %slice.200, f32[384,256]{1,0:T(8,128)S(1)} %slice.199), kind=kOutput, calls=%fused_computation.55 | convolution fusion | flops 1208156160 | bytes 4980736 | tf_op jit(solution)/shard_map/dot_general | solution.py:48
  71.0 1.1 slice_subtract_fusion.1
  72.1 2.3 %collective-permute-done.14 = f32[256,256]{1,0:T(8,128)S(1)} collective-permute-done((f32[256,256]{1,0:T(8,128)S(1)}, f32[256,256]{1,0:T(8,128)S(1)}, u32[]{:S(2)}, u32[]{:S(2)}) %collective-permute-start.14) | collective-permute-done | bytes 262176 | tf_op jit(solution)/shard_map/ppermute | solution.py:52
  76.1 4.5 %collective-permute-done.11 = f32[256,256]{0,1:T(8,128)S(1)} collective-permute-done((f32[256,256]{0,1:T(8,128)S(1)}, f32[256,256]{0,1:T(8,128)S(1)}, u32[]{:S(2)}, u32[]{:S(2)}) %collective-permute-start.11) | collective-permute-done | bytes 262176 | tf_op jit(solution)/shard_map/ppermute | solution.py:52
  81.0 6.2 %collective-permute-done.13 = f32[256,256]{0,1:T(8,128)S(1)} collective-permute-done((f32[256,256]{0,1:T(8,128)S(1)}, f32[256,256]{0,1:T(8,128)S(1)}, u32[]{:S(2)}, u32[]{:S(2)}) %collective-permute-start.13) | collective-permute-done | bytes 262176 | tf_op jit(solution)/shard_map/ppermute | solution.py:52
  87.5 7.8 %collective-permute-done.16 = f32[256,512]{1,0:T(8,128)S(1)} collective-permute-done((f32[256,512]{1,0:T(8,128)S(1)}, f32[256,512]{1,0:T(8,128)S(1)}, u32[]{:S(2)}, u32[]{:S(2)}) %collective-permute-start.16) | collective-permute-done | bytes 524320 | tf_op jit(solution)/shard_map/ppermute | solution.py:52
  97.1 1.6 %collective-permute-start.17 = (f32[256,512]{0,1:T(8,128)S(1)}, f32[256,512]{0,1:T(8,128)S(1)}, u32[]{:S(2)}, u32[]{:S(2)}) collective-permute-start(f32[256,512]{0,1:T(8,128)S(1)} %convolution_bitcast_fusion.5), channel_id=1, source_target_pairs={{0,16},{8,24},{16,0},{24,8},{1,17},{9,25},{17,1},{25,9},{2,18},{10... | collective-permute-start | bytes 1572872 | tf_op jit(solution)/shard_map/ppermute | solution.py:52
  98.8 19.4 %collective-permute-done.18 = f32[256,512]{0,1:T(8,128)S(1)} collective-permute-done((f32[256,512]{0,1:T(8,128)S(1)}, f32[256,512]{0,1:T(8,128)S(1)}, u32[]{:S(2)}, u32[]{:S(2)}) %collective-permute-start.18) | collective-permute-done | bytes 524320 | tf_op jit(solution)/shard_map/ppermute | solution.py:52
  120.3 13.7 %collective-permute-done.17 = f32[256,512]{0,1:T(8,128)S(1)} collective-permute-done((f32[256,512]{0,1:T(8,128)S(1)}, f32[256,512]{0,1:T(8,128)S(1)}, u32[]{:S(2)}, u32[]{:S(2)}) %collective-permute-start.17) | collective-permute-done | bytes 524320 | tf_op jit(solution)/shard_map/ppermute | solution.py:52
  134.4 9.8 %collective-permute-done.19 = f32[256,512]{0,1:T(8,128)S(1)} collective-permute-done((f32[256,512]{0,1:T(8,128)S(1)}, f32[256,512]{0,1:T(8,128)S(1)}, u32[]{:S(2)}, u32[]{:S(2)}) %collective-permute-start.19) | collective-permute-done | bytes 524320 | tf_op jit(solution)/shard_map/ppermute | solution.py:52
  144.2 1.2 fusion.5
  (83 shorter events, 19.8 us)
Async XLA Ops:
  1.1 2.4 %copy-start.4 = (s32[2]{0:T(128)S(1)}, s32[2]{0:T(128)}, u32[]{:S(2)}) copy-start(s32[2]{0:T(128)} %param.7) | copy-start | bytes 28
  3.0 2.2 %collective-permute-start = (f32[640,256]{1,0:T(8,128)S(1)}, f32[640,256]{1,0:T(8,128)S(1)}, u32[]{:S(2)}, u32[]{:S(2)}) collective-permute-start(f32[640,256]{1,0:T(8,128)S(1)} %pad_maximum_fusion.4), channel_id=1, source_target_pairs={{0,1},{1,0},{2,3},{3,2},{4,5},{5,4},{6,7},{7,6},{8,9},{9,8},{10,11... | collective-permute-start | bytes 1966088 | tf_op jit(solution)/shard_map/ppermute | solution.py:56
  5.3 11.5 %collective-permute-start.1 = (f32[640,256]{1,0:T(8,128)S(1)}, f32[640,256]{1,0:T(8,128)S(1)}, u32[]{:S(2)}, u32[]{:S(2)}) collective-permute-start(f32[640,256]{1,0:T(8,128)S(1)} %maximum_select_fusion), channel_id=1, source_target_pairs={{0,2},{1,5},{2,0},{3,7},{4,6},{5,1},{6,4},{7,3},{8,10},{9,13},{10,... | collective-permute-start | bytes 1966088 | tf_op jit(solution)/shard_map/ppermute | solution.py:127
  16.9 10.7 %collective-permute-start.2 = (f32[640,256]{1,0:T(8,128)S(1)}, f32[640,256]{1,0:T(8,128)S(1)}, u32[]{:S(2)}, u32[]{:S(2)}) collective-permute-start(f32[640,256]{1,0:T(8,128)S(1)} %broadcast_select_fusion), channel_id=1, source_target_pairs={{0,4},{1,3},{2,6},{3,1},{4,0},{5,7},{6,2},{7,5},{8,12},{9,11},{10,... | collective-permute-start | bytes 1966088 | tf_op jit(solution)/shard_map/ppermute | solution.py:127
  27.7 2.2 %collective-permute-start.3 = (f32[640,256]{1,0:T(8,128)S(1)}, f32[640,256]{1,0:T(8,128)S(1)}, u32[]{:S(2)}, u32[]{:S(2)}) collective-permute-start(f32[640,256]{1,0:T(8,128)S(1)} %broadcast_select_fusion.1), channel_id=1, source_target_pairs={{0,1},{1,0},{2,3},{3,2},{4,5},{5,4},{6,7},{7,6},{8,9},{9,8},{10,11... | collective-permute-start | bytes 1966088 | tf_op jit(solution)/shard_map/ppermute | solution.py:56
  28.6 10.4 %collective-permute-start.4 = (f32[512,256]{1,0:T(8,128)}, f32[512,256]{1,0:T(8,128)}, u32[]{:S(2)}, u32[]{:S(2)}) collective-permute-start(f32[512,256]{1,0:T(8,128)} %pad_maximum_fusion.5), channel_id=1, source_target_pairs={{0,1},{1,0},{2,3},{3,2},{4,5},{5,4},{6,7},{7,6},{8,9},{9,8},{10,11... | collective-permute-start | bytes 1572872 | tf_op jit(solution)/shard_map/ppermute | solution.py:56
  29.8 2.2 %copy-start = (f32[1024,1024]{1,0:T(8,128)S(1)}, f32[1024,1024]{1,0:T(8,128)}, u32[]{:S(2)}) copy-start(f32[1024,1024]{1,0:T(8,128)} %param.6) | copy-start | bytes 12582916
  29.8 3.9 %copy-start.1 = (f32[2,2,256,256]{3,2,1,0:T(8,128)S(1)}, f32[2,2,256,256]{3,2,1,0:T(8,128)}, u32[]{:S(2)}) copy-start(f32[2,2,256,256]{3,2,1,0:T(8,128)} %param.10) | copy-start | bytes 3145732
  34.1 10.8 %collective-permute-start.8 = (f32[256,256]{1,0:T(8,128)S(1)}, f32[256,256]{1,0:T(8,128)S(1)}, u32[]{:S(2)}, u32[]{:S(2)}) collective-permute-start(f32[256,256]{1,0:T(8,128)S(1)} %convolution_bitcast_fusion.23), channel_id=1, source_target_pairs={{0,8},{8,0},{16,24},{24,16},{1,9},{9,1},{17,25},{25,17},{2,10},{10... | collective-permute-start | bytes 786440 | tf_op jit(solution)/shard_map/ppermute | solution.py:52
  40.2 10.1 %collective-permute-start.5 = (f32[512,256]{1,0:T(8,128)S(1)}, f32[512,256]{1,0:T(8,128)S(1)}, u32[]{:S(2)}, u32[]{:S(2)}) collective-permute-start(f32[512,256]{1,0:T(8,128)S(1)} %maximum_select_fusion.1), channel_id=1, source_target_pairs={{0,2},{1,5},{2,0},{3,7},{4,6},{5,1},{6,4},{7,3},{8,10},{9,13},{10,... | collective-permute-start | bytes 1572872 | tf_op jit(solution)/shard_map/ppermute | solution.py:127
  42.8 2.0 %copy-start.2 = (f32[2,2,256,256]{3,2,1,0:T(8,128)S(1)}, f32[2,2,256,256]{3,2,1,0:T(8,128)}, u32[]{:S(2)}) copy-start(f32[2,2,256,256]{3,2,1,0:T(8,128)} %param.11) | copy-start | bytes 3145732
  42.8 13.7 %collective-permute-start.10 = (f32[256,256]{0,1:T(8,128)S(1)}, f32[256,256]{0,1:T(8,128)S(1)}, u32[]{:S(2)}, u32[]{:S(2)}) collective-permute-start(f32[256,256]{0,1:T(8,128)S(1)} %convolution_bitcast_fusion.18), channel_id=1, source_target_pairs={{0,8},{8,0},{16,24},{24,16},{1,9},{9,1},{17,25},{25,17},{2,10},{10... | collective-permute-start | bytes 786440 | tf_op jit(solution)/shard_map/ppermute | solution.py:52
  45.6 30.2 %collective-permute-start.9 = (f32[256,256]{0,1:T(8,128)S(1)}, f32[256,256]{0,1:T(8,128)S(1)}, u32[]{:S(2)}, u32[]{:S(2)}) collective-permute-start(f32[256,256]{0,1:T(8,128)S(1)} %convolution_bitcast_fusion.21), channel_id=1, source_target_pairs={{0,16},{8,24},{16,0},{24,8},{1,17},{9,25},{17,1},{25,9},{2,18},{10... | collective-permute-start | bytes 786440 | tf_op jit(solution)/shard_map/ppermute | solution.py:52
  48.6 14.7 %collective-permute-start.12 = (f32[256,256]{1,0:T(8,128)S(1)}, f32[256,256]{1,0:T(8,128)S(1)}, u32[]{:S(2)}, u32[]{:S(2)}) collective-permute-start(f32[256,256]{1,0:T(8,128)S(1)} %negate_select_fusion.2), channel_id=1, source_target_pairs={{0,8},{8,0},{16,24},{24,16},{1,9},{9,1},{17,25},{25,17},{2,10},{10... | collective-permute-start | bytes 786440 | tf_op jit(solution)/shard_map/ppermute | solution.py:52
  50.3 9.2 %collective-permute-start.6 = (f32[512,256]{1,0:T(8,128)S(1)}, f32[512,256]{1,0:T(8,128)S(1)}, u32[]{:S(2)}, u32[]{:S(2)}) collective-permute-start(f32[512,256]{1,0:T(8,128)S(1)} %broadcast_select_fusion.4), channel_id=1, source_target_pairs={{0,4},{1,3},{2,6},{3,1},{4,0},{5,7},{6,2},{7,5},{8,12},{9,11},{10,... | collective-permute-start | bytes 1572872 | tf_op jit(solution)/shard_map/ppermute | solution.py:127
  52.3 22.1 %collective-permute-start.14 = (f32[256,256]{1,0:T(8,128)S(1)}, f32[256,256]{1,0:T(8,128)S(1)}, u32[]{:S(2)}, u32[]{:S(2)}) collective-permute-start(f32[256,256]{1,0:T(8,128)S(1)} %negate_select_fusion.4), channel_id=1, source_target_pairs={{0,8},{8,0},{16,24},{24,16},{1,9},{9,1},{17,25},{25,17},{2,10},{10... | collective-permute-start | bytes 786440 | tf_op jit(solution)/shard_map/ppermute | solution.py:52
  59.7 7.3 %collective-permute-start.7 = (f32[512,256]{1,0:T(8,128)S(1)}, f32[512,256]{1,0:T(8,128)S(1)}, u32[]{:S(2)}, u32[]{:S(2)}) collective-permute-start(f32[512,256]{1,0:T(8,128)S(1)} %broadcast_select_fusion.5), channel_id=1, source_target_pairs={{0,1},{1,0},{2,3},{3,2},{4,5},{5,4},{6,7},{7,6},{8,9},{9,8},{10,11... | collective-permute-start | bytes 1572872 | tf_op jit(solution)/shard_map/ppermute | solution.py:56
  60.1 20.5 %collective-permute-start.11 = (f32[256,256]{0,1:T(8,128)S(1)}, f32[256,256]{0,1:T(8,128)S(1)}, u32[]{:S(2)}, u32[]{:S(2)}) collective-permute-start(f32[256,256]{0,1:T(8,128)S(1)} %convolution_bitcast_fusion.16), channel_id=1, source_target_pairs={{0,16},{8,24},{16,0},{24,8},{1,17},{9,25},{17,1},{25,9},{2,18},{10... | collective-permute-start | bytes 786440 | tf_op jit(solution)/shard_map/ppermute | solution.py:52
  64.2 23.0 %collective-permute-start.13 = (f32[256,256]{0,1:T(8,128)S(1)}, f32[256,256]{0,1:T(8,128)S(1)}, u32[]{:S(2)}, u32[]{:S(2)}) collective-permute-start(f32[256,256]{0,1:T(8,128)S(1)} %convolution_bitcast_fusion.12), channel_id=1, source_target_pairs={{0,16},{8,24},{16,0},{24,8},{1,17},{9,25},{17,1},{25,9},{2,18},{10... | collective-permute-start | bytes 786440 | tf_op jit(solution)/shard_map/ppermute | solution.py:52
  70.6 24.7 %collective-permute-start.16 = (f32[256,512]{1,0:T(8,128)S(1)}, f32[256,512]{1,0:T(8,128)S(1)}, u32[]{:S(2)}, u32[]{:S(2)}) collective-permute-start(f32[256,512]{1,0:T(8,128)S(1)} %convolution_bitcast_fusion.7), channel_id=1, source_target_pairs={{0,8},{8,0},{16,24},{24,16},{1,9},{9,1},{17,25},{25,17},{2,10},{10... | collective-permute-start | bytes 1572872 | tf_op jit(solution)/shard_map/ppermute | solution.py:52
  75.7 44.3 %collective-permute-start.15 = (f32[256,256]{0,1:T(8,128)S(1)}, f32[256,256]{0,1:T(8,128)S(1)}, u32[]{:S(2)}, u32[]{:S(2)}) collective-permute-start(f32[256,256]{0,1:T(8,128)S(1)} %convolution_bitcast_fusion.9), channel_id=1, source_target_pairs={{0,16},{8,24},{16,0},{24,8},{1,17},{9,25},{17,1},{25,9},{2,18},{10... | collective-permute-start | bytes 786440 | tf_op jit(solution)/shard_map/ppermute | solution.py:52
  96.0 22.2 %collective-permute-start.18 = (f32[256,512]{0,1:T(8,128)S(1)}, f32[256,512]{0,1:T(8,128)S(1)}, u32[]{:S(2)}, u32[]{:S(2)}) collective-permute-start(f32[256,512]{0,1:T(8,128)S(1)} %negate_select_fusion), channel_id=1, source_target_pairs={{0,8},{8,0},{16,24},{24,16},{1,9},{9,1},{17,25},{25,17},{2,10},{10... | collective-permute-start | bytes 1572872 | tf_op jit(solution)/shard_map/ppermute | solution.py:52
  97.1 36.9 %collective-permute-start.17 = (f32[256,512]{0,1:T(8,128)S(1)}, f32[256,512]{0,1:T(8,128)S(1)}, u32[]{:S(2)}, u32[]{:S(2)}) collective-permute-start(f32[256,512]{0,1:T(8,128)S(1)} %convolution_bitcast_fusion.5), channel_id=1, source_target_pairs={{0,16},{8,24},{16,0},{24,8},{1,17},{9,25},{17,1},{25,9},{2,18},{10... | collective-permute-start | bytes 1572872 | tf_op jit(solution)/shard_map/ppermute | solution.py:52
  119.3 25.0 %collective-permute-start.19 = (f32[256,512]{0,1:T(8,128)S(1)}, f32[256,512]{0,1:T(8,128)S(1)}, u32[]{:S(2)}, u32[]{:S(2)}) collective-permute-start(f32[256,512]{0,1:T(8,128)S(1)} %convolution_bitcast_fusion.1), channel_id=1, source_target_pairs={{0,16},{8,24},{16,0},{24,8},{1,17},{9,25},{17,1},{25,9},{2,18},{10... | collective-permute-start | bytes 1572872 | tf_op jit(solution)/shard_map/ppermute | solution.py:52
  134.4 9.8 %copy-start.3 = (f32[1024,1024]{1,0:T(8,128)}, f32[1024,1024]{1,0:T(8,128)S(1)}, u32[]{:S(2)}) copy-start(f32[1024,1024]{1,0:T(8,128)S(1)} %fusion.2) | copy-start | bytes 12582916

commit v5 on v4

--- a/solution.py
+++ b/solution.py
@@ -6,15 +6,14 @@
 PRECISION = lax.Precision.HIGH
 LEADING = (((0,), (0,)), ((), ()))
 CUTS = ((1, 1, 1, 1), (1, 1))
-STREAMS = 1
-DYNAMIC = True
+STREAMS = 2
 PLAN = (
     ("begin0", ""),
     ("move0.0", ""),
     ("move0.1", ""),
     ("end0", ""),
     ("send0.0", ""),
-    ("leaf0", ""),
+    ("leaf0", "own0.0"),
     ("send0.1", ""),
     ("send0.2", "got0.0"),
     ("send0.3", "got0.0"),
@@ -77,25 +76,18 @@
         self.owner = owner
         self.rows = reflectors.shape[0] - first_row
         self.width = factors.shape[0]
-        middle = first_row + self.rows // 2
         part = (self.rows + self.width) // 2 // streams
         cut = [slice(k * part, (k + 1) * part) for k in range(streams)]
-        if DYNAMIC:
-
-            def half(number):
-                rows = lax.dynamic_slice_in_dim(
-                    reflectors, first_row + number * (self.rows // 2), self.rows // 2, 0
-                )
-                factor = lax.dynamic_slice_in_dim(factors, number * (self.width // 2), self.width // 2, 0)
-                return jnp.concatenate([rows, factor], axis=0)
-
-            mine = half(self.me % 2)
-            other = half(1 - self.me % 2)
-        else:
-            block_0 = jnp.concatenate([reflectors[first_row:middle], factors[: self.width // 2]], axis=0)
-            block_1 = jnp.concatenate([reflectors[middle:], factors[self.width // 2 :]], axis=0)
-            mine = jnp.where(self.first, block_0, block_1)
-            other = jnp.where(self.first, block_1, block_0)
+
+        def half(number):
+            rows = lax.dynamic_slice_in_dim(
+                reflectors, first_row + number * (self.rows // 2), self.rows // 2, 0
+            )
+            factor = lax.dynamic_slice_in_dim(factors, number * (self.width // 2), self.width // 2, 0)
+            return jnp.concatenate([rows, factor], axis=0)
+
+        mine = half(self.me % 2)
+        other = half(1 - self.me % 2)
         self.mine, self.sent = [mine[c] for c in cut], [other[c] for c in cut]
         bits = [1 << k for k in range(1, size.bit_length() - 1)]
         turned = bits[len(bits) // 2 :] + bits[: len(bits) // 2]
@@ -164,8 +156,10 @@
     lower = [slab]
     result = None
 
-    def leaf(panel_no):
+    def leaf(panel_no, held):
         block, factor = blocks[panel_no]
+        if held is not None:
+            block, _ = lax.optimization_barrier((block, held))
         matrix = lower[-1]
         scaled = dot_t(factor, dot_t(block, matrix))
         tops[panel_no] = matrix[:width] - dot(block[:width], scaled)
@@ -225,7 +219,7 @@
             blocks[panel_no] = casts[panel_no].end(held)
             marks[f"arr{panel_no}.2"] = casts[panel_no].arrived[-1]
         elif name == "leaf":
-            leaf(panel_no)
+            leaf(panel_no, held)
         elif name == "send":
             send(panel_no, int(numbers[1]), held)
         elif name == "tree":

time: 146 us -> 144 us (0.986)
  waiting for transfers between devices: 89.1 us -> 83.6 us
    ppermute x4 -> x6, waiting for transfers between devices: 19.8 us -> 12.7 us  [exchange(): self.arrived = [lax.ppermute(c, 'col', pairs) for c in self.current]]
    ppermute x4 -> x6, starting transfers between devices: 8.19 us -> 12.1 us  [exchange(): self.arrived = [lax.ppermute(c, 'col', pairs) for c in self.current]]
    ppermute x12, starting transfers between devices: 14.9 us -> 11.9 us  [from_partner(): lax.ppermute(shard, 'row', [(i, i ^ 1 << apart) for i in range(lax.axis_s...]
    ppermute x12, waiting for transfers between devices: 68.8 us -> 70.9 us  [from_partner(): lax.ppermute(shard, 'row', [(i, i ^ 1 << apart) for i in range(lax.axis_s...]
  transfers between devices with their start and end apart: 20 -> 24, of which waited for: 13 -> 14; matrix products, arithmetic and copies ran while one was open for 16% -> 18% of each run, Pallas kernels for 0% -> 0%
where the time goes in v5:
time: 144 us; the launch traced here: 142 us
  waiting for transfers between devices  83.6 us (58%)
  starting transfers between devices  25.5 us (18%)
  matrix products  21.4 us (15%)
  local copies, waits for them, and re-layouts  6.37 us (4%)
  other arithmetic  3.28 us (2%)
  between operations  1.88 us (1%)
    ppermute x12, waiting for transfers between devices, from_partner(): lax.ppermute(shard, 'row', [(i, i ^ 1 << apart) for i in range(lax.axis_s...  70.9 us
    ppermute x6, waiting for transfers between devices, exchange(): self.arrived = [lax.ppermute(c, 'col', pairs) for c in self.current]  12.7 us
    ppermute x6, starting transfers between devices, exchange(): self.arrived = [lax.ppermute(c, 'col', pairs) for c in self.current]  12.1 us
    dot_general x18, matrix products, dot_t(): lax.dot_general(a, b, LEADING, precision=PRECISION, preferred_element_typ...  12 us
    ppermute x12, starting transfers between devices, from_partner(): lax.ppermute(shard, 'row', [(i, i ^ 1 << apart) for i in range(lax.axis_s...  11.9 us
    dot_general x17, matrix products, dot(): jnp.dot(a, b, precision=PRECISION, preferred_element_type=jnp.float32)  9.4 us
  transfers between devices with their start and end apart: 24, of which 14 were waited for; matrix products, arithmetic and copies ran while one was open for 18% of the time, Pallas kernels for 0%

profile of v5, /device:TPU:0, one launch (start us, length us, event | category | flops | bytes accessed | tf_op | source)
XLA Modules:
  0.0 142.0 jit_solution(11322015135948711169)
XLA Ops:
  0.0 1.1 fusion.117
  1.1 1.7 %fusion.116 = (f32[1,1024,256]{2,1,0:T(8,128)S(1)}, f32[1,1024,256]{2,1,0:T(8,128)S(1)}) fusion(f32[2,1024,256]{2,1,0:T(8,128)} %param.8), kind=kLoop, calls=%fused_computation.182 | loop fusion | bytes 4194304 | tf_op jit(solution)/shard_map/slice | solution.py:147
  5.6 3.0 %collective-permute-start.5 = (f32[320,256]{1,0:T(8,128)S(1)}, f32[320,256]{1,0:T(8,128)}, u32[]{:S(2)}, u32[]{:S(2)}) collective-permute-start(f32[320,256]{1,0:T(8,128)S(1)} %fusion.35), channel_id=1, source_target_pairs={{0,2},{1,5},{2,0},{3,7},{4,6},{5,1},{6,4},{7,3},{8,10},{9,13},{10,... | collective-permute-start | bytes 983048 | tf_op jit(solution)/shard_map/ppermute | solution.py:119
  8.9 4.8 %collective-permute-done.5 = f32[320,256]{1,0:T(8,128)} collective-permute-done((f32[320,256]{1,0:T(8,128)S(1)}, f32[320,256]{1,0:T(8,128)}, u32[]{:S(2)}, u32[]{:S(2)}) %collective-permute-start.5) | collective-permute-done | bytes 327712 | tf_op jit(solution)/shard_map/ppermute | solution.py:119
  13.8 2.1 %collective-permute-start.6 = (f32[320,256]{1,0:T(8,128)S(1)}, f32[320,256]{1,0:T(8,128)S(1)}, u32[]{:S(2)}, u32[]{:S(2)}) collective-permute-start(f32[320,256]{1,0:T(8,128)S(1)} %broadcast_select_fusion.4), channel_id=1, source_target_pairs={{0,4},{1,3},{2,6},{3,1},{4,0},{5,7},{6,2},{7,5},{8,12},{9,11},{10,... | collective-permute-start | bytes 983048 | tf_op jit(solution)/shard_map/ppermute | solution.py:119
  15.9 1.2 collective-permute-done.1
  17.2 2.6 %collective-permute-start.2 = (f32[320,256]{1,0:T(8,128)S(1)}, f32[320,256]{1,0:T(8,128)S(1)}, u32[]{:S(2)}, u32[]{:S(2)}) collective-permute-start(f32[320,256]{1,0:T(8,128)S(1)} %broadcast_select_fusion.5), channel_id=1, source_target_pairs={{0,4},{1,3},{2,6},{3,1},{4,0},{5,7},{6,2},{7,5},{8,12},{9,11},{10,... | collective-permute-start | bytes 983048 | tf_op jit(solution)/shard_map/ppermute | solution.py:119
  19.9 1.1 collective-permute-done.6
  21.3 3.6 %collective-permute-done.2 = f32[320,256]{1,0:T(8,128)S(1)} collective-permute-done((f32[320,256]{1,0:T(8,128)S(1)}, f32[320,256]{1,0:T(8,128)S(1)}, u32[]{:S(2)}, u32[]{:S(2)}) %collective-permute-start.2) | collective-permute-done | bytes 327712 | tf_op jit(solution)/shard_map/ppermute | solution.py:119
  27.3 1.9 %copy-done = f32[1024,1024]{1,0:T(8,128)S(1)} copy-done((f32[1024,1024]{1,0:T(8,128)S(1)}, f32[1024,1024]{1,0:T(8,128)}, u32[]{:S(2)}) %copy-start) | copy-done | bytes 4194328
  31.4 1.7 %collective-permute-start.12 = (f32[256,256]{1,0:T(8,128)S(1)}, f32[256,256]{1,0:T(8,128)S(1)}, u32[]{:S(2)}, u32[]{:S(2)}) collective-permute-start(f32[256,256]{1,0:T(8,128)S(1)} %convolution_bitcast_fusion.23), channel_id=1, source_target_pairs={{0,8},{8,0},{16,24},{24,16},{1,9},{9,1},{17,25},{25,17},{2,10},{10... | collective-permute-start | bytes 786440 | tf_op jit(solution)/shard_map/ppermute | solution.py:51
  33.1 2.1 %fusion.119 = f32[256,1024]{1,0:T(8,128)S(1)} fusion(f32[1024,256]{1,0:T(8,128)S(1)} %fusion.18, f32[1024,1024]{1,0:T(8,128)S(1)} %copy-done), kind=kOutput, calls=%fused_computation.185 | convolution fusion | flops 1610612736 | bytes 6291456 | tf_op jit(solution)/shard_map/dot_general | solution.py:47
  35.9 1.1 maximum_select_fusion
  37.1 2.5 %collective-permute-start.9 = (f32[512,256]{1,0:T(8,128)S(1)}, f32[512,256]{1,0:T(8,128)S(1)}, u32[]{:S(2)}, u32[]{:S(2)}) collective-permute-start(f32[512,256]{1,0:T(8,128)S(1)} %maximum_select_fusion), channel_id=1, source_target_pairs={{0,2},{1,5},{2,0},{3,7},{4,6},{5,1},{6,4},{7,3},{8,10},{9,13},{10,... | collective-permute-start | bytes 1572872 | tf_op jit(solution)/shard_map/ppermute | solution.py:119
  41.2 1.5 %slice_subtract_fusion = f32[768,1024]{1,0:T(8,128)S(1)} fusion(f32[1024,1024]{1,0:T(8,128)S(1)} %copy-done, f32[256,1024]{1,0:T(8,128)S(1)} %fusion.91, f32[1024,256]{1,0:T(8,128)S(1)} %fusion.18), kind=kOutput, calls=%fused_computation.1 | convolution fusion | flops 1208745984 | bytes 8126464 | tf_op jit(solution)/shard_map/dot_general | solution.py:43
  43.4 2.6 %collective-permute-start.13 = (f32[256,256]{0,1:T(8,128)S(1)}, f32[256,256]{0,1:T(8,128)S(1)}, u32[]{:S(2)}, u32[]{:S(2)}) collective-permute-start(f32[256,256]{0,1:T(8,128)S(1)} %convolution_bitcast_fusion.21), channel_id=1, source_target_pairs={{0,16},{8,24},{16,0},{24,8},{1,17},{9,25},{17,1},{25,9},{2,18},{10... | collective-permute-start | bytes 786440 | tf_op jit(solution)/shard_map/ppermute | solution.py:51
  46.4 1.6 %collective-permute-start.16 = (f32[256,256]{1,0:T(8,128)S(1)}, f32[256,256]{1,0:T(8,128)S(1)}, u32[]{:S(2)}, u32[]{:S(2)}) collective-permute-start(f32[256,256]{1,0:T(8,128)S(1)} %negate_select_fusion.2), channel_id=1, source_target_pairs={{0,8},{8,0},{16,24},{24,16},{1,9},{9,1},{17,25},{25,17},{2,10},{10... | collective-permute-start | bytes 786440 | tf_op jit(solution)/shard_map/ppermute | solution.py:51
  48.2 1.6 %collective-permute-start.10 = (f32[512,256]{1,0:T(8,128)S(1)}, f32[512,256]{1,0:T(8,128)S(1)}, u32[]{:S(2)}, u32[]{:S(2)}) collective-permute-start(f32[512,256]{1,0:T(8,128)S(1)} %broadcast_select_fusion), channel_id=1, source_target_pairs={{0,4},{1,3},{2,6},{3,1},{4,0},{5,7},{6,2},{7,5},{8,12},{9,11},{10,... | collective-permute-start | bytes 1572872 | tf_op jit(solution)/shard_map/ppermute | solution.py:119
  50.7 4.4 %collective-permute-done.14 = f32[256,256]{0,1:T(8,128)S(1)} collective-permute-done((f32[256,256]{0,1:T(8,128)S(1)}, f32[256,256]{0,1:T(8,128)S(1)}, u32[]{:S(2)}, u32[]{:S(2)}) %collective-permute-start.14) | collective-permute-done | bytes 262176 | tf_op jit(solution)/shard_map/ppermute | solution.py:51
  55.5 1.9 %collective-permute-done.10 = f32[512,256]{1,0:T(8,128)S(1)} collective-permute-done((f32[512,256]{1,0:T(8,128)S(1)}, f32[512,256]{1,0:T(8,128)S(1)}, u32[]{:S(2)}, u32[]{:S(2)}) %collective-permute-start.10) | collective-permute-done | bytes 524320 | tf_op jit(solution)/shard_map/ppermute | solution.py:119
  58.0 1.3 collective-permute-start.15
  59.3 1.9 %collective-permute-done.16 = f32[256,256]{1,0:T(8,128)S(1)} collective-permute-done((f32[256,256]{1,0:T(8,128)S(1)}, f32[256,256]{1,0:T(8,128)S(1)}, u32[]{:S(2)}, u32[]{:S(2)}) %collective-permute-start.16) | collective-permute-done | bytes 262176 | tf_op jit(solution)/shard_map/ppermute | solution.py:51
  62.1 2.7 %collective-permute-start.17 = (f32[256,256]{0,1:T(8,128)S(1)}, f32[256,256]{0,1:T(8,128)S(1)}, u32[]{:S(2)}, u32[]{:S(2)}) collective-permute-start(f32[256,256]{0,1:T(8,128)S(1)} %convolution_bitcast_fusion.12), channel_id=1, source_target_pairs={{0,16},{8,24},{16,0},{24,8},{1,17},{9,25},{17,1},{25,9},{2,18},{10... | collective-permute-start | bytes 786440 | tf_op jit(solution)/shard_map/ppermute | solution.py:51
  65.0 1.7 %fusion.21 = f32[256,1024]{1,0:T(8,128)S(1)} fusion(f32[768,1024]{1,0:T(8,128)S(1)} %slice_subtract_fusion, f32[384,256]{1,0:T(8,128)S(1)} %slice.226, f32[384,256]{1,0:T(8,128)S(1)} %slice.225), kind=kOutput, calls=%fused_computation.54 | convolution fusion | flops 1208156160 | bytes 4980736 | tf_op jit(solution)/shard_map/dot_general | solution.py:47
  68.5 1.1 slice_subtract_fusion.1
  72.3 6.2 %collective-permute-done.15 = f32[256,256]{0,1:T(8,128)S(1)} collective-permute-done((f32[256,256]{0,1:T(8,128)S(1)}, f32[256,256]{0,1:T(8,128)S(1)}, u32[]{:S(2)}, u32[]{:S(2)}) %collective-permute-start.15) | collective-permute-done | bytes 262176 | tf_op jit(solution)/shard_map/ppermute | solution.py:51
  78.8 6.2 %collective-permute-done.17 = f32[256,256]{0,1:T(8,128)S(1)} collective-permute-done((f32[256,256]{0,1:T(8,128)S(1)}, f32[256,256]{0,1:T(8,128)S(1)}, u32[]{:S(2)}, u32[]{:S(2)}) %collective-permute-start.17) | collective-permute-done | bytes 262176 | tf_op jit(solution)/shard_map/ppermute | solution.py:51
  85.4 8.8 %collective-permute-done.20 = f32[256,512]{1,0:T(8,128)S(1)} collective-permute-done((f32[256,512]{1,0:T(8,128)S(1)}, f32[256,512]{1,0:T(8,128)S(1)}, u32[]{:S(2)}, u32[]{:S(2)}) %collective-permute-start.20) | collective-permute-done | bytes 524320 | tf_op jit(solution)/shard_map/ppermute | solution.py:51
  96.1 18.4 %collective-permute-done.22 = f32[256,512]{0,1:T(8,128)S(1)} collective-permute-done((f32[256,512]{0,1:T(8,128)S(1)}, f32[256,512]{0,1:T(8,128)S(1)}, u32[]{:S(2)}, u32[]{:S(2)}) %collective-permute-start.22) | collective-permute-done | bytes 524320 | tf_op jit(solution)/shard_map/ppermute | solution.py:51
  116.1 14.2 %collective-permute-done.21 = f32[256,512]{0,1:T(8,128)S(1)} collective-permute-done((f32[256,512]{0,1:T(8,128)S(1)}, f32[256,512]{0,1:T(8,128)S(1)}, u32[]{:S(2)}, u32[]{:S(2)}) %collective-permute-start.21) | collective-permute-done | bytes 524320 | tf_op jit(solution)/shard_map/ppermute | solution.py:51
  130.7 10.0 %collective-permute-done.23 = f32[256,512]{0,1:T(8,128)S(1)} collective-permute-done((f32[256,512]{0,1:T(8,128)S(1)}, f32[256,512]{0,1:T(8,128)S(1)}, u32[]{:S(2)}, u32[]{:S(2)}) %collective-permute-start.23) | collective-permute-done | bytes 524320 | tf_op jit(solution)/shard_map/ppermute | solution.py:51
  140.8 1.2 fusion.5
  (95 shorter events, 22.0 us)
Async XLA Ops:
  1.1 3.2 %copy-start.4 = (s32[2]{0:T(128)S(1)}, s32[2]{0:T(128)}, u32[]{:S(2)}) copy-start(s32[2]{0:T(128)} %param.7) | copy-start | bytes 28
  3.0 2.6 %collective-permute-start.4 = (f32[320,256]{1,0:T(8,128)S(1)}, f32[320,256]{1,0:T(8,128)}, u32[]{:S(2)}, u32[]{:S(2)}) collective-permute-start(f32[320,256]{1,0:T(8,128)S(1)} %pad_maximum_fusion.3), channel_id=1, source_target_pairs={{0,1},{1,0},{2,3},{3,2},{4,5},{5,4},{6,7},{7,6},{8,9},{9,8},{10,11... | collective-permute-start | bytes 983048 | tf_op jit(solution)/shard_map/ppermute | solution.py:55
  4.2 4.4 %collective-permute-start = (f32[320,256]{1,0:T(8,128)}, f32[320,256]{1,0:T(8,128)}, u32[]{:S(2)}, u32[]{:S(2)}) collective-permute-start(f32[320,256]{1,0:T(8,128)} %dynamic-slice_bitcast_fusion.4), channel_id=1, source_target_pairs={{0,1},{1,0},{2,3},{3,2},{4,5},{5,4},{6,7},{7,6},{8,9},{9,8},{10,11... | collective-permute-start | bytes 983048 | tf_op jit(solution)/shard_map/ppermute | solution.py:55
  5.6 8.2 %collective-permute-start.5 = (f32[320,256]{1,0:T(8,128)S(1)}, f32[320,256]{1,0:T(8,128)}, u32[]{:S(2)}, u32[]{:S(2)}) collective-permute-start(f32[320,256]{1,0:T(8,128)S(1)} %fusion.35), channel_id=1, source_target_pairs={{0,2},{1,5},{2,0},{3,7},{4,6},{5,1},{6,4},{7,3},{8,10},{9,13},{10,... | collective-permute-start | bytes 983048 | tf_op jit(solution)/shard_map/ppermute | solution.py:119
  8.6 8.5 %collective-permute-start.1 = (f32[320,256]{1,0:T(8,128)S(1)}, f32[320,256]{1,0:T(8,128)S(1)}, u32[]{:S(2)}, u32[]{:S(2)}) collective-permute-start(f32[320,256]{1,0:T(8,128)S(1)} %fusion.36), channel_id=1, source_target_pairs={{0,2},{1,5},{2,0},{3,7},{4,6},{5,1},{6,4},{7,3},{8,10},{9,13},{10,... | collective-permute-start | bytes 983048 | tf_op jit(solution)/shard_map/ppermute | solution.py:119
  13.8 7.2 %collective-permute-start.6 = (f32[320,256]{1,0:T(8,128)S(1)}, f32[320,256]{1,0:T(8,128)S(1)}, u32[]{:S(2)}, u32[]{:S(2)}) collective-permute-start(f32[320,256]{1,0:T(8,128)S(1)} %broadcast_select_fusion.4), channel_id=1, source_target_pairs={{0,4},{1,3},{2,6},{3,1},{4,0},{5,7},{6,2},{7,5},{8,12},{9,11},{10,... | collective-permute-start | bytes 983048 | tf_op jit(solution)/shard_map/ppermute | solution.py:119
  17.2 7.7 %collective-permute-start.2 = (f32[320,256]{1,0:T(8,128)S(1)}, f32[320,256]{1,0:T(8,128)S(1)}, u32[]{:S(2)}, u32[]{:S(2)}) collective-permute-start(f32[320,256]{1,0:T(8,128)S(1)} %broadcast_select_fusion.5), channel_id=1, source_target_pairs={{0,4},{1,3},{2,6},{3,1},{4,0},{5,7},{6,2},{7,5},{8,12},{9,11},{10,... | collective-permute-start | bytes 983048 | tf_op jit(solution)/shard_map/ppermute | solution.py:119
  21.0 6.0 %collective-permute-start.7 = (f32[320,256]{1,0:T(8,128)S(1)}, f32[320,256]{1,0:T(8,128)S(1)}, u32[]{:S(2)}, u32[]{:S(2)}) collective-permute-start(f32[320,256]{1,0:T(8,128)S(1)} %broadcast_select_fusion.6), channel_id=1, source_target_pairs={{0,1},{1,0},{2,3},{3,2},{4,5},{5,4},{6,7},{7,6},{8,9},{9,8},{10,11... | collective-permute-start | bytes 983048 | tf_op jit(solution)/shard_map/ppermute | solution.py:55
  24.9 2.2 %collective-permute-start.3 = (f32[320,256]{1,0:T(8,128)S(1)}, f32[320,256]{1,0:T(8,128)S(1)}, u32[]{:S(2)}, u32[]{:S(2)}) collective-permute-start(f32[320,256]{1,0:T(8,128)S(1)} %broadcast_select_fusion.7), channel_id=1, source_target_pairs={{0,1},{1,0},{2,3},{3,2},{4,5},{5,4},{6,7},{7,6},{8,9},{9,8},{10,11... | collective-permute-start | bytes 983048 | tf_op jit(solution)/shard_map/ppermute | solution.py:55
  25.9 10.0 %collective-permute-start.8 = (f32[512,256]{1,0:T(8,128)}, f32[512,256]{1,0:T(8,128)}, u32[]{:S(2)}, u32[]{:S(2)}) collective-permute-start(f32[512,256]{1,0:T(8,128)} %pad_maximum_fusion.2), channel_id=1, source_target_pairs={{0,1},{1,0},{2,3},{3,2},{4,5},{5,4},{6,7},{7,6},{8,9},{9,8},{10,11... | collective-permute-start | bytes 1572872 | tf_op jit(solution)/shard_map/ppermute | solution.py:55
  27.0 2.2 %copy-start = (f32[1024,1024]{1,0:T(8,128)S(1)}, f32[1024,1024]{1,0:T(8,128)}, u32[]{:S(2)}) copy-start(f32[1024,1024]{1,0:T(8,128)} %param.6) | copy-start | bytes 12582916
  27.1 3.8 %copy-start.1 = (f32[2,2,256,256]{3,2,1,0:T(8,128)S(1)}, f32[2,2,256,256]{3,2,1,0:T(8,128)}, u32[]{:S(2)}) copy-start(f32[2,2,256,256]{3,2,1,0:T(8,128)} %param.10) | copy-start | bytes 3145732
  31.4 11.3 %collective-permute-start.12 = (f32[256,256]{1,0:T(8,128)S(1)}, f32[256,256]{1,0:T(8,128)S(1)}, u32[]{:S(2)}, u32[]{:S(2)}) collective-permute-start(f32[256,256]{1,0:T(8,128)S(1)} %convolution_bitcast_fusion.23), channel_id=1, source_target_pairs={{0,8},{8,0},{16,24},{24,16},{1,9},{9,1},{17,25},{25,17},{2,10},{10... | collective-permute-start | bytes 786440 | tf_op jit(solution)/shard_map/ppermute | solution.py:51
  37.1 11.0 %collective-permute-start.9 = (f32[512,256]{1,0:T(8,128)S(1)}, f32[512,256]{1,0:T(8,128)S(1)}, u32[]{:S(2)}, u32[]{:S(2)}) collective-permute-start(f32[512,256]{1,0:T(8,128)S(1)} %maximum_select_fusion), channel_id=1, source_target_pairs={{0,2},{1,5},{2,0},{3,7},{4,6},{5,1},{6,4},{7,3},{8,10},{9,13},{10,... | collective-permute-start | bytes 1572872 | tf_op jit(solution)/shard_map/ppermute | solution.py:119
  40.6 2.0 %copy-start.2 = (f32[2,2,256,256]{3,2,1,0:T(8,128)S(1)}, f32[2,2,256,256]{3,2,1,0:T(8,128)}, u32[]{:S(2)}) copy-start(f32[2,2,256,256]{3,2,1,0:T(8,128)} %param.11) | copy-start | bytes 3145732
  40.6 14.4 %collective-permute-start.14 = (f32[256,256]{0,1:T(8,128)S(1)}, f32[256,256]{0,1:T(8,128)S(1)}, u32[]{:S(2)}, u32[]{:S(2)}) collective-permute-start(f32[256,256]{0,1:T(8,128)S(1)} %convolution_bitcast_fusion.18), channel_id=1, source_target_pairs={{0,8},{8,0},{16,24},{24,16},{1,9},{9,1},{17,25},{25,17},{2,10},{10... | collective-permute-start | bytes 786440 | tf_op jit(solution)/shard_map/ppermute | solution.py:51
  43.4 28.6 %collective-permute-start.13 = (f32[256,256]{0,1:T(8,128)S(1)}, f32[256,256]{0,1:T(8,128)S(1)}, u32[]{:S(2)}, u32[]{:S(2)}) collective-permute-start(f32[256,256]{0,1:T(8,128)S(1)} %convolution_bitcast_fusion.21), channel_id=1, source_target_pairs={{0,16},{8,24},{16,0},{24,8},{1,17},{9,25},{17,1},{25,9},{2,18},{10... | collective-permute-start | bytes 786440 | tf_op jit(solution)/shard_map/ppermute | solution.py:51
  46.4 14.7 %collective-permute-start.16 = (f32[256,256]{1,0:T(8,128)S(1)}, f32[256,256]{1,0:T(8,128)S(1)}, u32[]{:S(2)}, u32[]{:S(2)}) collective-permute-start(f32[256,256]{1,0:T(8,128)S(1)} %negate_select_fusion.2), channel_id=1, source_target_pairs={{0,8},{8,0},{16,24},{24,16},{1,9},{9,1},{17,25},{25,17},{2,10},{10... | collective-permute-start | bytes 786440 | tf_op jit(solution)/shard_map/ppermute | solution.py:51
  48.2 9.2 %collective-permute-start.10 = (f32[512,256]{1,0:T(8,128)S(1)}, f32[512,256]{1,0:T(8,128)S(1)}, u32[]{:S(2)}, u32[]{:S(2)}) collective-permute-start(f32[512,256]{1,0:T(8,128)S(1)} %broadcast_select_fusion), channel_id=1, source_target_pairs={{0,4},{1,3},{2,6},{3,1},{4,0},{5,7},{6,2},{7,5},{8,12},{9,11},{10,... | collective-permute-start | bytes 1572872 | tf_op jit(solution)/shard_map/ppermute | solution.py:119
  50.1 20.2 %collective-permute-start.18 = (f32[256,256]{1,0:T(8,128)S(1)}, f32[256,256]{1,0:T(8,128)S(1)}, u32[]{:S(2)}, u32[]{:S(2)}) collective-permute-start(f32[256,256]{1,0:T(8,128)S(1)} %negate_select_fusion.4), channel_id=1, source_target_pairs={{0,8},{8,0},{16,24},{24,16},{1,9},{9,1},{17,25},{25,17},{2,10},{10... | collective-permute-start | bytes 786440 | tf_op jit(solution)/shard_map/ppermute | solution.py:51
  57.5 7.3 %collective-permute-start.11 = (f32[512,256]{1,0:T(8,128)S(1)}, f32[512,256]{1,0:T(8,128)S(1)}, u32[]{:S(2)}, u32[]{:S(2)}) collective-permute-start(f32[512,256]{1,0:T(8,128)S(1)} %broadcast_select_fusion.1), channel_id=1, source_target_pairs={{0,1},{1,0},{2,3},{3,2},{4,5},{5,4},{6,7},{7,6},{8,9},{9,8},{10,11... | collective-permute-start | bytes 1572872 | tf_op jit(solution)/shard_map/ppermute | solution.py:55
  58.0 20.5 %collective-permute-start.15 = (f32[256,256]{0,1:T(8,128)S(1)}, f32[256,256]{0,1:T(8,128)S(1)}, u32[]{:S(2)}, u32[]{:S(2)}) collective-permute-start(f32[256,256]{0,1:T(8,128)S(1)} %convolution_bitcast_fusion.16), channel_id=1, source_target_pairs={{0,16},{8,24},{16,0},{24,8},{1,17},{9,25},{17,1},{25,9},{2,18},{10... | collective-permute-start | bytes 786440 | tf_op jit(solution)/shard_map/ppermute | solution.py:51
  62.1 23.0 %collective-permute-start.17 = (f32[256,256]{0,1:T(8,128)S(1)}, f32[256,256]{0,1:T(8,128)S(1)}, u32[]{:S(2)}, u32[]{:S(2)}) collective-permute-start(f32[256,256]{0,1:T(8,128)S(1)} %convolution_bitcast_fusion.12), channel_id=1, source_target_pairs={{0,16},{8,24},{16,0},{24,8},{1,17},{9,25},{17,1},{25,9},{2,18},{10... | collective-permute-start | bytes 786440 | tf_op jit(solution)/shard_map/ppermute | solution.py:51
  68.5 25.7 %collective-permute-start.20 = (f32[256,512]{1,0:T(8,128)S(1)}, f32[256,512]{1,0:T(8,128)S(1)}, u32[]{:S(2)}, u32[]{:S(2)}) collective-permute-start(f32[256,512]{1,0:T(8,128)S(1)} %convolution_bitcast_fusion.7), channel_id=1, source_target_pairs={{0,8},{8,0},{16,24},{24,16},{1,9},{9,1},{17,25},{25,17},{2,10},{10... | collective-permute-start | bytes 1572872 | tf_op jit(solution)/shard_map/ppermute | solution.py:51
  71.6 44.2 %collective-permute-start.19 = (f32[256,256]{0,1:T(8,128)S(1)}, f32[256,256]{0,1:T(8,128)S(1)}, u32[]{:S(2)}, u32[]{:S(2)}) collective-permute-start(f32[256,256]{0,1:T(8,128)S(1)} %convolution_bitcast_fusion.9), channel_id=1, source_target_pairs={{0,16},{8,24},{16,0},{24,8},{1,17},{9,25},{17,1},{25,9},{2,18},{10... | collective-permute-start | bytes 786440 | tf_op jit(solution)/shard_map/ppermute | solution.py:51
  94.8 19.6 %collective-permute-start.22 = (f32[256,512]{0,1:T(8,128)S(1)}, f32[256,512]{0,1:T(8,128)S(1)}, u32[]{:S(2)}, u32[]{:S(2)}) collective-permute-start(f32[256,512]{0,1:T(8,128)S(1)} %negate_select_fusion), channel_id=1, source_target_pairs={{0,8},{8,0},{16,24},{24,16},{1,9},{9,1},{17,25},{25,17},{2,10},{10... | collective-permute-start | bytes 1572872 | tf_op jit(solution)/shard_map/ppermute | solution.py:51
  96.0 34.3 %collective-permute-start.21 = (f32[256,512]{0,1:T(8,128)S(1)}, f32[256,512]{0,1:T(8,128)S(1)}, u32[]{:S(2)}, u32[]{:S(2)}) collective-permute-start(f32[256,512]{0,1:T(8,128)S(1)} %convolution_bitcast_fusion.5), channel_id=1, source_target_pairs={{0,16},{8,24},{16,0},{24,8},{1,17},{9,25},{17,1},{25,9},{2,18},{10... | collective-permute-start | bytes 1572872 | tf_op jit(solution)/shard_map/ppermute | solution.py:51
  115.5 25.3 %collective-permute-start.23 = (f32[256,512]{0,1:T(8,128)S(1)}, f32[256,512]{0,1:T(8,128)S(1)}, u32[]{:S(2)}, u32[]{:S(2)}) collective-permute-start(f32[256,512]{0,1:T(8,128)S(1)} %convolution_bitcast_fusion.1), channel_id=1, source_target_pairs={{0,16},{8,24},{16,0},{24,8},{1,17},{9,25},{17,1},{25,9},{2,18},{10... | collective-permute-start | bytes 1572872 | tf_op jit(solution)/shard_map/ppermute | solution.py:51
  130.7 10.1 %copy-start.3 = (f32[1024,1024]{1,0:T(8,128)}, f32[1024,1024]{1,0:T(8,128)S(1)}, u32[]{:S(2)}) copy-start(f32[1024,1024]{1,0:T(8,128)S(1)} %fusion.2) | copy-start | bytes 12582916

commit v6 on v5

--- a/solution.py
+++ b/solution.py
@@ -168,7 +168,7 @@
     def head(panel_no, chunk):
         block, factor = blocks[panel_no]
         start, stop = edges[panel_no][chunk]
-        part = lower[-1][:, start:stop]
+        part = after(lower[-1][:, start:stop], marks["arr0.0"])
         scaled = dot_t(factor, dot_t(block, part))
         return part[:width] - dot(block[:width], scaled)
 

time: 144 us -> 143 us (level); the launches traced: 142 us -> 144 us
  other arithmetic: 3.28 us -> 5.44 us
  local copies, waits for them, and re-layouts: 6.37 us -> 4.4 us
    ppermute x12, starting transfers between devices: 11.9 us -> 15 us  [from_partner(): lax.ppermute(shard, 'row', [(i, i ^ 1 << apart) for i in range(lax.axis_s...]
    unnamed x10, local copies, waits for them, and re-layouts: 1.95 us -> 0.03 us
    ppermute x6, waiting for transfers between devices: 12.7 us -> 14.4 us  [exchange(): self.arrived = [lax.ppermute(c, 'col', pairs) for c in self.current]]
where the time goes in v6:
time: 143 us; the launch traced here: 144 us
  waiting for transfers between devices  84.4 us (59%)
  starting transfers between devices  26.5 us (19%)
  matrix products  21.1 us (15%)
  other arithmetic  5.44 us (4%)
  local copies, waits for them, and re-layouts  4.4 us (3%)
  between operations  1.96 us (1%)
    ppermute x12, waiting for transfers between devices, from_partner(): lax.ppermute(shard, 'row', [(i, i ^ 1 << apart) for i in range(lax.axis_s...  69.8 us
    ppermute x12, starting transfers between devices, from_partner(): lax.ppermute(shard, 'row', [(i, i ^ 1 << apart) for i in range(lax.axis_s...  15 us
    ppermute x6, waiting for transfers between devices, exchange(): self.arrived = [lax.ppermute(c, 'col', pairs) for c in self.current]  14.4 us
    dot_general x18, matrix products, dot_t(): lax.dot_general(a, b, LEADING, precision=PRECISION, preferred_element_typ...  12 us
    ppermute x6, starting transfers between devices, exchange(): self.arrived = [lax.ppermute(c, 'col', pairs) for c in self.current]  10.8 us
    dot_general x17, matrix products, dot(): jnp.dot(a, b, precision=PRECISION, preferred_element_type=jnp.float32)  9.13 us
  transfers between devices with their start and end apart: 24, of which 14 were waited for; matrix products, arithmetic and copies ran while one was open for 18% of the time, Pallas kernels for 0%

profile of v6, /device:TPU:0, one launch (start us, length us, event | category | flops | bytes accessed | tf_op | source)
XLA Modules:
  0.0 143.8 jit_solution(9723642012708844023)
XLA Ops:
  0.0 1.1 fusion.115
  1.1 1.7 %fusion.114 = (f32[1,1024,256]{2,1,0:T(8,128)S(1)}, f32[1,1024,256]{2,1,0:T(8,128)S(1)}) fusion(f32[2,1024,256]{2,1,0:T(8,128)} %param.8), kind=kLoop, calls=%fused_computation.182 | loop fusion | bytes 4194304 | tf_op jit(solution)/shard_map/slice | solution.py:147
  7.3 3.0 %collective-permute-start.5 = (f32[320,256]{1,0:T(8,128)S(1)}, f32[320,256]{1,0:T(8,128)S(1)}, u32[]{:S(2)}, u32[]{:S(2)}) collective-permute-start(f32[320,256]{1,0:T(8,128)S(1)} %fusion.33), channel_id=1, source_target_pairs={{0,2},{1,5},{2,0},{3,7},{4,6},{5,1},{6,4},{7,3},{8,10},{9,13},{10,... | collective-permute-start | bytes 983048 | tf_op jit(solution)/shard_map/ppermute | solution.py:119
  12.2 3.2 %collective-permute-done.5 = f32[320,256]{1,0:T(8,128)S(1)} collective-permute-done((f32[320,256]{1,0:T(8,128)S(1)}, f32[320,256]{1,0:T(8,128)S(1)}, u32[]{:S(2)}, u32[]{:S(2)}) %collective-permute-start.5) | collective-permute-done | bytes 327712 | tf_op jit(solution)/shard_map/ppermute | solution.py:119
  15.4 2.1 %collective-permute-start.6 = (f32[320,256]{1,0:T(8,128)S(1)}, f32[320,256]{1,0:T(8,128)S(1)}, u32[]{:S(2)}, u32[]{:S(2)}) collective-permute-start(f32[320,256]{1,0:T(8,128)S(1)} %broadcast_select_fusion.4), channel_id=1, source_target_pairs={{0,4},{1,3},{2,6},{3,1},{4,0},{5,7},{6,2},{7,5},{8,12},{9,11},{10,... | collective-permute-start | bytes 983048 | tf_op jit(solution)/shard_map/ppermute | solution.py:119
  17.6 3.6 %collective-permute-done.1 = f32[320,256]{1,0:T(8,128)S(1)} collective-permute-done((f32[320,256]{1,0:T(8,128)S(1)}, f32[320,256]{1,0:T(8,128)S(1)}, u32[]{:S(2)}, u32[]{:S(2)}) %collective-permute-start.1) | collective-permute-done | bytes 327712 | tf_op jit(solution)/shard_map/ppermute | solution.py:119
  21.2 2.4 %collective-permute-start.2 = (f32[320,256]{1,0:T(8,128)S(1)}, f32[320,256]{1,0:T(8,128)S(1)}, u32[]{:S(2)}, u32[]{:S(2)}) collective-permute-start(f32[320,256]{1,0:T(8,128)S(1)} %broadcast_select_fusion.5), channel_id=1, source_target_pairs={{0,4},{1,3},{2,6},{3,1},{4,0},{5,7},{6,2},{7,5},{8,12},{9,11},{10,... | collective-permute-start | bytes 983048 | tf_op jit(solution)/shard_map/ppermute | solution.py:119
  23.8 4.9 %collective-permute-done.2 = f32[320,256]{1,0:T(8,128)S(1)} collective-permute-done((f32[320,256]{1,0:T(8,128)S(1)}, f32[320,256]{1,0:T(8,128)S(1)}, u32[]{:S(2)}, u32[]{:S(2)}) %collective-permute-start.2) | collective-permute-done | bytes 327712 | tf_op jit(solution)/shard_map/ppermute | solution.py:119
  28.8 1.3 negate_select_fusion
  32.7 2.1 %collective-permute-start.12 = (f32[256,256]{1,0:T(8,128)S(1)}, f32[256,256]{1,0:T(8,128)S(1)}, u32[]{:S(2)}, u32[]{:S(2)}) collective-permute-start(f32[256,256]{1,0:T(8,128)S(1)} %convolution_bitcast_fusion.23), channel_id=1, source_target_pairs={{0,8},{8,0},{16,24},{24,16},{1,9},{9,1},{17,25},{25,17},{2,10},{10... | collective-permute-start | bytes 786440 | tf_op jit(solution)/shard_map/ppermute | solution.py:51
  34.8 2.1 %fusion.118 = f32[256,1024]{1,0:T(8,128)S(1)} fusion(f32[1024,256]{1,0:T(8,128)S(1)} %fusion.18, f32[1024,1024]{1,0:T(8,128)S(1)} %copy-done), kind=kOutput, calls=%fused_computation.186 | convolution fusion | flops 1610612736 | bytes 6291456 | tf_op jit(solution)/shard_map/dot_general | solution.py:47
  37.8 1.6 %collective-permute-start.9 = (f32[512,256]{1,0:T(8,128)S(1)}, f32[512,256]{1,0:T(8,128)S(1)}, u32[]{:S(2)}, u32[]{:S(2)}) collective-permute-start(f32[512,256]{1,0:T(8,128)S(1)} %maximum_select_fusion), channel_id=1, source_target_pairs={{0,2},{1,5},{2,0},{3,7},{4,6},{5,1},{6,4},{7,3},{8,10},{9,13},{10,... | collective-permute-start | bytes 1572872 | tf_op jit(solution)/shard_map/ppermute | solution.py:119
  40.9 1.5 %slice_subtract_fusion = f32[768,1024]{1,0:T(8,128)S(1)} fusion(f32[1024,1024]{1,0:T(8,128)S(1)} %copy-done, f32[256,1024]{1,0:T(8,128)S(1)} %fusion.89, f32[1024,256]{1,0:T(8,128)S(1)} %fusion.18), kind=kOutput, calls=%fused_computation.1 | convolution fusion | flops 1208745984 | bytes 8126464 | tf_op jit(solution)/shard_map/dot_general | solution.py:43
  43.1 2.7 %collective-permute-start.13 = (f32[256,256]{0,1:T(8,128)S(1)}, f32[256,256]{0,1:T(8,128)S(1)}, u32[]{:S(2)}, u32[]{:S(2)}) collective-permute-start(f32[256,256]{0,1:T(8,128)S(1)} %convolution_bitcast_fusion.21), channel_id=1, source_target_pairs={{0,16},{8,24},{16,0},{24,8},{1,17},{9,25},{17,1},{25,9},{2,18},{10... | collective-permute-start | bytes 786440 | tf_op jit(solution)/shard_map/ppermute | solution.py:51
  46.2 1.6 %collective-permute-start.16 = (f32[256,256]{1,0:T(8,128)S(1)}, f32[256,256]{1,0:T(8,128)S(1)}, u32[]{:S(2)}, u32[]{:S(2)}) collective-permute-start(f32[256,256]{1,0:T(8,128)S(1)} %negate_select_fusion.3), channel_id=1, source_target_pairs={{0,8},{8,0},{16,24},{24,16},{1,9},{9,1},{17,25},{25,17},{2,10},{10... | collective-permute-start | bytes 786440 | tf_op jit(solution)/shard_map/ppermute | solution.py:51
  47.9 1.6 %collective-permute-start.10 = (f32[512,256]{1,0:T(8,128)S(1)}, f32[512,256]{1,0:T(8,128)S(1)}, u32[]{:S(2)}, u32[]{:S(2)}) collective-permute-start(f32[512,256]{1,0:T(8,128)S(1)} %broadcast_select_fusion), channel_id=1, source_target_pairs={{0,4},{1,3},{2,6},{3,1},{4,0},{5,7},{6,2},{7,5},{8,12},{9,11},{10,... | collective-permute-start | bytes 1572872 | tf_op jit(solution)/shard_map/ppermute | solution.py:119
  50.4 3.6 %collective-permute-done.14 = f32[256,256]{0,1:T(8,128)S(1)} collective-permute-done((f32[256,256]{0,1:T(8,128)S(1)}, f32[256,256]{0,1:T(8,128)S(1)}, u32[]{:S(2)}, u32[]{:S(2)}) %collective-permute-start.14) | collective-permute-done | bytes 262176 | tf_op jit(solution)/shard_map/ppermute | solution.py:51
  54.4 2.7 %collective-permute-done.10 = f32[512,256]{1,0:T(8,128)S(1)} collective-permute-done((f32[512,256]{1,0:T(8,128)S(1)}, f32[512,256]{1,0:T(8,128)S(1)}, u32[]{:S(2)}, u32[]{:S(2)}) %collective-permute-start.10) | collective-permute-done | bytes 524320 | tf_op jit(solution)/shard_map/ppermute | solution.py:119
  57.7 1.9 %collective-permute-start.15 = (f32[256,256]{0,1:T(8,128)S(1)}, f32[256,256]{0,1:T(8,128)S(1)}, u32[]{:S(2)}, u32[]{:S(2)}) collective-permute-start(f32[256,256]{0,1:T(8,128)S(1)} %convolution_bitcast_fusion.16), channel_id=1, source_target_pairs={{0,16},{8,24},{16,0},{24,8},{1,17},{9,25},{17,1},{25,9},{2,18},{10... | collective-permute-start | bytes 786440 | tf_op jit(solution)/shard_map/ppermute | solution.py:51
  59.5 1.4 collective-permute-done.16
  61.6 2.7 %collective-permute-start.17 = (f32[256,256]{0,1:T(8,128)S(1)}, f32[256,256]{0,1:T(8,128)S(1)}, u32[]{:S(2)}, u32[]{:S(2)}) collective-permute-start(f32[256,256]{0,1:T(8,128)S(1)} %convolution_bitcast_fusion.12), channel_id=1, source_target_pairs={{0,16},{8,24},{16,0},{24,8},{1,17},{9,25},{17,1},{25,9},{2,18},{10... | collective-permute-start | bytes 786440 | tf_op jit(solution)/shard_map/ppermute | solution.py:51
  64.4 1.7 %fusion.19 = f32[256,1024]{1,0:T(8,128)S(1)} fusion(f32[768,1024]{1,0:T(8,128)S(1)} %slice_subtract_fusion, f32[384,256]{1,0:T(8,128)S(1)} %slice.231, f32[384,256]{1,0:T(8,128)S(1)} %slice.230), kind=kOutput, calls=%fused_computation.53 | convolution fusion | flops 1208156160 | bytes 4980736 | tf_op jit(solution)/shard_map/dot_general | solution.py:47
  68.4 1.1 slice_subtract_fusion.1
  69.5 2.7 %collective-permute-done.18 = f32[256,256]{1,0:T(8,128)S(1)} collective-permute-done((f32[256,256]{1,0:T(8,128)S(1)}, f32[256,256]{1,0:T(8,128)S(1)}, u32[]{:S(2)}, u32[]{:S(2)}) %collective-permute-start.18) | collective-permute-done | bytes 262176 | tf_op jit(solution)/shard_map/ppermute | solution.py:51
  73.9 4.3 %collective-permute-done.15 = f32[256,256]{0,1:T(8,128)S(1)} collective-permute-done((f32[256,256]{0,1:T(8,128)S(1)}, f32[256,256]{0,1:T(8,128)S(1)}, u32[]{:S(2)}, u32[]{:S(2)}) %collective-permute-start.15) | collective-permute-done | bytes 262176 | tf_op jit(solution)/shard_map/ppermute | solution.py:51
  78.5 6.2 %collective-permute-done.17 = f32[256,256]{0,1:T(8,128)S(1)} collective-permute-done((f32[256,256]{0,1:T(8,128)S(1)}, f32[256,256]{0,1:T(8,128)S(1)}, u32[]{:S(2)}, u32[]{:S(2)}) %collective-permute-start.17) | collective-permute-done | bytes 262176 | tf_op jit(solution)/shard_map/ppermute | solution.py:51
  85.1 8.3 %collective-permute-done.20 = f32[256,512]{1,0:T(8,128)S(1)} collective-permute-done((f32[256,512]{1,0:T(8,128)S(1)}, f32[256,512]{1,0:T(8,128)S(1)}, u32[]{:S(2)}, u32[]{:S(2)}) %collective-permute-start.20) | collective-permute-done | bytes 524320 | tf_op jit(solution)/shard_map/ppermute | solution.py:51
  95.1 1.9 %collective-permute-start.21 = (f32[256,512]{0,1:T(8,128)S(1)}, f32[256,512]{0,1:T(8,128)S(1)}, u32[]{:S(2)}, u32[]{:S(2)}) collective-permute-start(f32[256,512]{0,1:T(8,128)S(1)} %convolution_bitcast_fusion.5), channel_id=1, source_target_pairs={{0,16},{8,24},{16,0},{24,8},{1,17},{9,25},{17,1},{25,9},{2,18},{10... | collective-permute-start | bytes 1572872 | tf_op jit(solution)/shard_map/ppermute | solution.py:51
  97.0 19.0 %collective-permute-done.22 = f32[256,512]{0,1:T(8,128)S(1)} collective-permute-done((f32[256,512]{0,1:T(8,128)S(1)}, f32[256,512]{0,1:T(8,128)S(1)}, u32[]{:S(2)}, u32[]{:S(2)}) %collective-permute-start.22) | collective-permute-done | bytes 524320 | tf_op jit(solution)/shard_map/ppermute | solution.py:51
  117.9 15.0 %collective-permute-done.21 = f32[256,512]{0,1:T(8,128)S(1)} collective-permute-done((f32[256,512]{0,1:T(8,128)S(1)}, f32[256,512]{0,1:T(8,128)S(1)}, u32[]{:S(2)}, u32[]{:S(2)}) %collective-permute-start.21) | collective-permute-done | bytes 524320 | tf_op jit(solution)/shard_map/ppermute | solution.py:51
  133.3 9.3 %collective-permute-done.23 = f32[256,512]{0,1:T(8,128)S(1)} collective-permute-done((f32[256,512]{0,1:T(8,128)S(1)}, f32[256,512]{0,1:T(8,128)S(1)}, u32[]{:S(2)}, u32[]{:S(2)}) %collective-permute-start.23) | collective-permute-done | bytes 524320 | tf_op jit(solution)/shard_map/ppermute | solution.py:51
  142.6 1.2 fusion.5
  (97 shorter events, 22.5 us)
Async XLA Ops:
  1.1 3.9 %copy-start.4 = (s32[2]{0:T(128)S(1)}, s32[2]{0:T(128)}, u32[]{:S(2)}) copy-start(s32[2]{0:T(128)} %param.7) | copy-start | bytes 28
  3.7 2.6 %collective-permute-start.4 = (f32[320,256]{1,0:T(8,128)}, f32[320,256]{1,0:T(8,128)}, u32[]{:S(2)}, u32[]{:S(2)}) collective-permute-start(f32[320,256]{1,0:T(8,128)} %pad_maximum_fusion.3), channel_id=1, source_target_pairs={{0,1},{1,0},{2,3},{3,2},{4,5},{5,4},{6,7},{7,6},{8,9},{9,8},{10,11... | collective-permute-start | bytes 983048 | tf_op jit(solution)/shard_map/ppermute | solution.py:55
  4.9 5.5 %collective-permute-start = (f32[320,256]{1,0:T(8,128)}, f32[320,256]{1,0:T(8,128)}, u32[]{:S(2)}, u32[]{:S(2)}) collective-permute-start(f32[320,256]{1,0:T(8,128)} %dynamic-slice_bitcast_fusion.4), channel_id=1, source_target_pairs={{0,1},{1,0},{2,3},{3,2},{4,5},{5,4},{6,7},{7,6},{8,9},{9,8},{10,11... | collective-permute-start | bytes 983048 | tf_op jit(solution)/shard_map/ppermute | solution.py:55
  7.3 8.1 %collective-permute-start.5 = (f32[320,256]{1,0:T(8,128)S(1)}, f32[320,256]{1,0:T(8,128)S(1)}, u32[]{:S(2)}, u32[]{:S(2)}) collective-permute-start(f32[320,256]{1,0:T(8,128)S(1)} %fusion.33), channel_id=1, source_target_pairs={{0,2},{1,5},{2,0},{3,7},{4,6},{5,1},{6,4},{7,3},{8,10},{9,13},{10,... | collective-permute-start | bytes 983048 | tf_op jit(solution)/shard_map/ppermute | solution.py:119
  11.4 9.8 %collective-permute-start.1 = (f32[320,256]{1,0:T(8,128)S(1)}, f32[320,256]{1,0:T(8,128)S(1)}, u32[]{:S(2)}, u32[]{:S(2)}) collective-permute-start(f32[320,256]{1,0:T(8,128)S(1)} %fusion.34), channel_id=1, source_target_pairs={{0,2},{1,5},{2,0},{3,7},{4,6},{5,1},{6,4},{7,3},{8,10},{9,13},{10,... | collective-permute-start | bytes 983048 | tf_op jit(solution)/shard_map/ppermute | solution.py:119
  11.5 26.2 %collective-permute-start.8 = (f32[512,256]{1,0:T(8,128)S(1)}, f32[512,256]{1,0:T(8,128)S(1)}, u32[]{:S(2)}, u32[]{:S(2)}) collective-permute-start(f32[512,256]{1,0:T(8,128)S(1)} %pad_maximum_fusion.2), channel_id=1, source_target_pairs={{0,1},{1,0},{2,3},{3,2},{4,5},{5,4},{6,7},{7,6},{8,9},{9,8},{10,11... | collective-permute-start | bytes 1572872 | tf_op jit(solution)/shard_map/ppermute | solution.py:55
  15.4 8.2 %collective-permute-start.6 = (f32[320,256]{1,0:T(8,128)S(1)}, f32[320,256]{1,0:T(8,128)S(1)}, u32[]{:S(2)}, u32[]{:S(2)}) collective-permute-start(f32[320,256]{1,0:T(8,128)S(1)} %broadcast_select_fusion.4), channel_id=1, source_target_pairs={{0,4},{1,3},{2,6},{3,1},{4,0},{5,7},{6,2},{7,5},{8,12},{9,11},{10,... | collective-permute-start | bytes 983048 | tf_op jit(solution)/shard_map/ppermute | solution.py:119
  21.2 7.5 %collective-permute-start.2 = (f32[320,256]{1,0:T(8,128)S(1)}, f32[320,256]{1,0:T(8,128)S(1)}, u32[]{:S(2)}, u32[]{:S(2)}) collective-permute-start(f32[320,256]{1,0:T(8,128)S(1)} %broadcast_select_fusion.5), channel_id=1, source_target_pairs={{0,4},{1,3},{2,6},{3,1},{4,0},{5,7},{6,2},{7,5},{8,12},{9,11},{10,... | collective-permute-start | bytes 983048 | tf_op jit(solution)/shard_map/ppermute | solution.py:119
  23.7 6.4 %collective-permute-start.7 = (f32[320,256]{1,0:T(8,128)S(1)}, f32[320,256]{1,0:T(8,128)S(1)}, u32[]{:S(2)}, u32[]{:S(2)}) collective-permute-start(f32[320,256]{1,0:T(8,128)S(1)} %broadcast_select_fusion.6), channel_id=1, source_target_pairs={{0,1},{1,0},{2,3},{3,2},{4,5},{5,4},{6,7},{7,6},{8,9},{9,8},{10,11... | collective-permute-start | bytes 983048 | tf_op jit(solution)/shard_map/ppermute | solution.py:55
  28.7 1.7 %collective-permute-start.3 = (f32[320,256]{1,0:T(8,128)S(1)}, f32[320,256]{1,0:T(8,128)S(1)}, u32[]{:S(2)}, u32[]{:S(2)}) collective-permute-start(f32[320,256]{1,0:T(8,128)S(1)} %broadcast_select_fusion.7), channel_id=1, source_target_pairs={{0,1},{1,0},{2,3},{3,2},{4,5},{5,4},{6,7},{7,6},{8,9},{9,8},{10,11... | collective-permute-start | bytes 983048 | tf_op jit(solution)/shard_map/ppermute | solution.py:55
  30.2 2.1 %copy-start.1 = (f32[2,2,256,256]{3,2,1,0:T(8,128)S(1)}, f32[2,2,256,256]{3,2,1,0:T(8,128)}, u32[]{:S(2)}) copy-start(f32[2,2,256,256]{3,2,1,0:T(8,128)} %param.10) | copy-start | bytes 3145732
  30.2 4.6 %copy-start = (f32[1024,1024]{1,0:T(8,128)S(1)}, f32[1024,1024]{1,0:T(8,128)}, u32[]{:S(2)}) copy-start(f32[1024,1024]{1,0:T(8,128)} %param.6) | copy-start | bytes 12582916
  32.7 9.7 %collective-permute-start.12 = (f32[256,256]{1,0:T(8,128)S(1)}, f32[256,256]{1,0:T(8,128)S(1)}, u32[]{:S(2)}, u32[]{:S(2)}) collective-permute-start(f32[256,256]{1,0:T(8,128)S(1)} %convolution_bitcast_fusion.23), channel_id=1, source_target_pairs={{0,8},{8,0},{16,24},{24,16},{1,9},{9,1},{17,25},{25,17},{2,10},{10... | collective-permute-start | bytes 786440 | tf_op jit(solution)/shard_map/ppermute | solution.py:51
  37.8 10.0 %collective-permute-start.9 = (f32[512,256]{1,0:T(8,128)S(1)}, f32[512,256]{1,0:T(8,128)S(1)}, u32[]{:S(2)}, u32[]{:S(2)}) collective-permute-start(f32[512,256]{1,0:T(8,128)S(1)} %maximum_select_fusion), channel_id=1, source_target_pairs={{0,2},{1,5},{2,0},{3,7},{4,6},{5,1},{6,4},{7,3},{8,10},{9,13},{10,... | collective-permute-start | bytes 1572872 | tf_op jit(solution)/shard_map/ppermute | solution.py:119
  40.4 2.0 %copy-start.2 = (f32[2,2,256,256]{3,2,1,0:T(8,128)S(1)}, f32[2,2,256,256]{3,2,1,0:T(8,128)}, u32[]{:S(2)}) copy-start(f32[2,2,256,256]{3,2,1,0:T(8,128)} %param.11) | copy-start | bytes 3145732
  40.4 13.6 %collective-permute-start.14 = (f32[256,256]{0,1:T(8,128)S(1)}, f32[256,256]{0,1:T(8,128)S(1)}, u32[]{:S(2)}, u32[]{:S(2)}) collective-permute-start(f32[256,256]{0,1:T(8,128)S(1)} %convolution_bitcast_fusion.18), channel_id=1, source_target_pairs={{0,8},{8,0},{16,24},{24,16},{1,9},{9,1},{17,25},{25,17},{2,10},{10... | collective-permute-start | bytes 786440 | tf_op jit(solution)/shard_map/ppermute | solution.py:51
  43.1 30.5 %collective-permute-start.13 = (f32[256,256]{0,1:T(8,128)S(1)}, f32[256,256]{0,1:T(8,128)S(1)}, u32[]{:S(2)}, u32[]{:S(2)}) collective-permute-start(f32[256,256]{0,1:T(8,128)S(1)} %convolution_bitcast_fusion.21), channel_id=1, source_target_pairs={{0,16},{8,24},{16,0},{24,8},{1,17},{9,25},{17,1},{25,9},{2,18},{10... | collective-permute-start | bytes 786440 | tf_op jit(solution)/shard_map/ppermute | solution.py:51
  46.2 14.7 %collective-permute-start.16 = (f32[256,256]{1,0:T(8,128)S(1)}, f32[256,256]{1,0:T(8,128)S(1)}, u32[]{:S(2)}, u32[]{:S(2)}) collective-permute-start(f32[256,256]{1,0:T(8,128)S(1)} %negate_select_fusion.3), channel_id=1, source_target_pairs={{0,8},{8,0},{16,24},{24,16},{1,9},{9,1},{17,25},{25,17},{2,10},{10... | collective-permute-start | bytes 786440 | tf_op jit(solution)/shard_map/ppermute | solution.py:51
  47.9 9.2 %collective-permute-start.10 = (f32[512,256]{1,0:T(8,128)S(1)}, f32[512,256]{1,0:T(8,128)S(1)}, u32[]{:S(2)}, u32[]{:S(2)}) collective-permute-start(f32[512,256]{1,0:T(8,128)S(1)} %broadcast_select_fusion), channel_id=1, source_target_pairs={{0,4},{1,3},{2,6},{3,1},{4,0},{5,7},{6,2},{7,5},{8,12},{9,11},{10,... | collective-permute-start | bytes 1572872 | tf_op jit(solution)/shard_map/ppermute | solution.py:119
  49.9 22.3 %collective-permute-start.18 = (f32[256,256]{1,0:T(8,128)S(1)}, f32[256,256]{1,0:T(8,128)S(1)}, u32[]{:S(2)}, u32[]{:S(2)}) collective-permute-start(f32[256,256]{1,0:T(8,128)S(1)} %negate_select_fusion.5), channel_id=1, source_target_pairs={{0,8},{8,0},{16,24},{24,16},{1,9},{9,1},{17,25},{25,17},{2,10},{10... | collective-permute-start | bytes 786440 | tf_op jit(solution)/shard_map/ppermute | solution.py:51
  57.2 7.1 %collective-permute-start.11 = (f32[512,256]{1,0:T(8,128)S(1)}, f32[512,256]{1,0:T(8,128)S(1)}, u32[]{:S(2)}, u32[]{:S(2)}) collective-permute-start(f32[512,256]{1,0:T(8,128)S(1)} %broadcast_select_fusion.1), channel_id=1, source_target_pairs={{0,1},{1,0},{2,3},{3,2},{4,5},{5,4},{6,7},{7,6},{8,9},{9,8},{10,11... | collective-permute-start | bytes 1572872 | tf_op jit(solution)/shard_map/ppermute | solution.py:55
  57.7 20.5 %collective-permute-start.15 = (f32[256,256]{0,1:T(8,128)S(1)}, f32[256,256]{0,1:T(8,128)S(1)}, u32[]{:S(2)}, u32[]{:S(2)}) collective-permute-start(f32[256,256]{0,1:T(8,128)S(1)} %convolution_bitcast_fusion.16), channel_id=1, source_target_pairs={{0,16},{8,24},{16,0},{24,8},{1,17},{9,25},{17,1},{25,9},{2,18},{10... | collective-permute-start | bytes 786440 | tf_op jit(solution)/shard_map/ppermute | solution.py:51
  61.6 23.2 %collective-permute-start.17 = (f32[256,256]{0,1:T(8,128)S(1)}, f32[256,256]{0,1:T(8,128)S(1)}, u32[]{:S(2)}, u32[]{:S(2)}) collective-permute-start(f32[256,256]{0,1:T(8,128)S(1)} %convolution_bitcast_fusion.12), channel_id=1, source_target_pairs={{0,16},{8,24},{16,0},{24,8},{1,17},{9,25},{17,1},{25,9},{2,18},{10... | collective-permute-start | bytes 786440 | tf_op jit(solution)/shard_map/ppermute | solution.py:51
  67.9 25.5 %collective-permute-start.20 = (f32[256,512]{1,0:T(8,128)S(1)}, f32[256,512]{1,0:T(8,128)S(1)}, u32[]{:S(2)}, u32[]{:S(2)}) collective-permute-start(f32[256,512]{1,0:T(8,128)S(1)} %convolution_bitcast_fusion.7), channel_id=1, source_target_pairs={{0,8},{8,0},{16,24},{24,16},{1,9},{9,1},{17,25},{25,17},{2,10},{10... | collective-permute-start | bytes 1572872 | tf_op jit(solution)/shard_map/ppermute | solution.py:51
  73.5 44.0 %collective-permute-start.19 = (f32[256,256]{0,1:T(8,128)S(1)}, f32[256,256]{0,1:T(8,128)S(1)}, u32[]{:S(2)}, u32[]{:S(2)}) collective-permute-start(f32[256,256]{0,1:T(8,128)S(1)} %convolution_bitcast_fusion.9), channel_id=1, source_target_pairs={{0,16},{8,24},{16,0},{24,8},{1,17},{9,25},{17,1},{25,9},{2,18},{10... | collective-permute-start | bytes 786440 | tf_op jit(solution)/shard_map/ppermute | solution.py:51
  94.0 22.0 %collective-permute-start.22 = (f32[256,512]{0,1:T(8,128)S(1)}, f32[256,512]{0,1:T(8,128)S(1)}, u32[]{:S(2)}, u32[]{:S(2)}) collective-permute-start(f32[256,512]{0,1:T(8,128)S(1)} %negate_select_fusion.1), channel_id=1, source_target_pairs={{0,8},{8,0},{16,24},{24,16},{1,9},{9,1},{17,25},{25,17},{2,10},{10... | collective-permute-start | bytes 1572872 | tf_op jit(solution)/shard_map/ppermute | solution.py:51
  95.1 37.7 %collective-permute-start.21 = (f32[256,512]{0,1:T(8,128)S(1)}, f32[256,512]{0,1:T(8,128)S(1)}, u32[]{:S(2)}, u32[]{:S(2)}) collective-permute-start(f32[256,512]{0,1:T(8,128)S(1)} %convolution_bitcast_fusion.5), channel_id=1, source_target_pairs={{0,16},{8,24},{16,0},{24,8},{1,17},{9,25},{17,1},{25,9},{2,18},{10... | collective-permute-start | bytes 1572872 | tf_op jit(solution)/shard_map/ppermute | solution.py:51
  117.0 25.6 %collective-permute-start.23 = (f32[256,512]{0,1:T(8,128)S(1)}, f32[256,512]{0,1:T(8,128)S(1)}, u32[]{:S(2)}, u32[]{:S(2)}) collective-permute-start(f32[256,512]{0,1:T(8,128)S(1)} %convolution_bitcast_fusion.1), channel_id=1, source_target_pairs={{0,16},{8,24},{16,0},{24,8},{1,17},{9,25},{17,1},{25,9},{2,18},{10... | collective-permute-start | bytes 1572872 | tf_op jit(solution)/shard_map/ppermute | solution.py:51
  133.3 9.3 %copy-start.3 = (f32[1024,1024]{1,0:T(8,128)}, f32[1024,1024]{1,0:T(8,128)S(1)}, u32[]{:S(2)}) copy-start(f32[1024,1024]{1,0:T(8,128)S(1)} %fusion.2) | copy-start | bytes 12582916

commit v7 on v6

--- a/solution.py
+++ b/solution.py
@@ -17,7 +17,7 @@
     ("send0.1", ""),
     ("send0.2", "got0.0"),
     ("send0.3", "got0.0"),
-    ("begin1", ""),
+    ("begin1", "arr0.0"),
     ("move1.0", "own0.0"),
     ("move1.1", ""),
     ("end1", ""),
@@ -78,16 +78,11 @@
         self.width = factors.shape[0]
         part = (self.rows + self.width) // 2 // streams
         cut = [slice(k * part, (k + 1) * part) for k in range(streams)]
-
-        def half(number):
-            rows = lax.dynamic_slice_in_dim(
-                reflectors, first_row + number * (self.rows // 2), self.rows // 2, 0
-            )
-            factor = lax.dynamic_slice_in_dim(factors, number * (self.width // 2), self.width // 2, 0)
-            return jnp.concatenate([rows, factor], axis=0)
-
-        mine = half(self.me % 2)
-        other = half(1 - self.me % 2)
+        middle = first_row + self.rows // 2
+        block_0 = jnp.concatenate([reflectors[first_row:middle], factors[: self.width // 2]], axis=0)
+        block_1 = jnp.concatenate([reflectors[middle:], factors[self.width // 2 :]], axis=0)
+        mine = jnp.where(self.first, block_0, block_1)
+        other = jnp.where(self.first, block_1, block_0)
         self.mine, self.sent = [mine[c] for c in cut], [other[c] for c in cut]
         bits = [1 << k for k in range(1, size.bit_length() - 1)]
         turned = bits[len(bits) // 2 :] + bits[: len(bits) // 2]

time: 143 us -> 140 us (0.979)
  other arithmetic: 5.44 us -> 2.88 us
  waiting for transfers between devices: 84.4 us -> 82.4 us
    ppermute x6, waiting for transfers between devices: 14.4 us -> 11.9 us  [exchange(): self.arrived = [lax.ppermute(c, 'col', pairs) for c in self.current]]
    select_n x9 -> x8, other arithmetic: 2.41 us -> 0.49 us  [select(): result.append(jnp.where(keep, current, arrived))]
    slice x2 -> x3, local copies, waits for them, and re-layouts: 2.75 us -> 3.58 us  [the longest x2 2.44 us: __init__(): reflectors[first_row:middle]]
  transfers between devices with their start and end apart: 24 -> 24, of which waited for: 14 -> 15; matrix products, arithmetic and copies ran while one was open for 18% -> 18% of each run, Pallas kernels for 0% -> 0%
where the time goes in v7:
time: 140 us
  waiting for transfers between devices  82.4 us (59%)
  starting transfers between devices  27 us (19%)
  matrix products  21.3 us (15%)
  local copies, waits for them, and re-layouts  4.33 us (3%)
  other arithmetic  2.88 us (2%)
  between operations  1.89 us (1%)
    ppermute x12, waiting for transfers between devices, from_partner(): lax.ppermute(shard, 'row', [(i, i ^ 1 << apart) for i in range(lax.axis_s...  69.2 us
    ppermute x12, starting transfers between devices, from_partner(): lax.ppermute(shard, 'row', [(i, i ^ 1 << apart) for i in range(lax.axis_s...  14.9 us
    dot_general x18, matrix products, dot_t(): lax.dot_general(a, b, LEADING, precision=PRECISION, preferred_element_typ...  12 us
    ppermute x6, waiting for transfers between devices, exchange(): self.arrived = [lax.ppermute(c, 'col', pairs) for c in self.current]  11.9 us
    ppermute x6, starting transfers between devices, exchange(): self.arrived = [lax.ppermute(c, 'col', pairs) for c in self.current]  10.7 us
    dot_general x17, matrix products, dot(): jnp.dot(a, b, precision=PRECISION, preferred_element_type=jnp.float32)  9.33 us
  transfers between devices with their start and end apart: 24, of which 15 were waited for; matrix products, arithmetic and copies ran while one was open for 18% of the time, Pallas kernels for 0%

profile of v7, /device:TPU:0, one launch (start us, length us, event | category | flops | bytes accessed | tf_op | source)
XLA Modules:
  0.0 139.7 jit_solution(10327769018067330271)
XLA Ops:
  0.0 1.1 slice_bitcast_fusion.5
  1.1 1.3 slice_bitcast_fusion.1
  4.9 2.9 %collective-permute-start.5 = (f32[320,256]{1,0:T(8,128)S(1)}, f32[320,256]{1,0:T(8,128)S(1)}, u32[]{:S(2)}, u32[]{:S(2)}) collective-permute-start(f32[320,256]{1,0:T(8,128)S(1)} %get-tuple-element.20), channel_id=1, source_target_pairs={{0,2},{1,5},{2,0},{3,7},{4,6},{5,1},{6,4},{7,3},{8,10},{9,13},{10,... | collective-permute-start | bytes 983048 | tf_op jit(solution)/shard_map/ppermute | solution.py:114
  7.9 1.2 slice_bitcast_fusion.3
  9.8 3.1 %collective-permute-done.5 = f32[320,256]{1,0:T(8,128)S(1)} collective-permute-done((f32[320,256]{1,0:T(8,128)S(1)}, f32[320,256]{1,0:T(8,128)S(1)}, u32[]{:S(2)}, u32[]{:S(2)}) %collective-permute-start.5) | collective-permute-done | bytes 327712 | tf_op jit(solution)/shard_map/ppermute | solution.py:114
  12.9 2.1 %collective-permute-start.6 = (f32[320,256]{1,0:T(8,128)S(1)}, f32[320,256]{1,0:T(8,128)S(1)}, u32[]{:S(2)}, u32[]{:S(2)}) collective-permute-start(f32[320,256]{1,0:T(8,128)S(1)} %broadcast_select_fusion.4), channel_id=1, source_target_pairs={{0,4},{1,3},{2,6},{3,1},{4,0},{5,7},{6,2},{7,5},{8,12},{9,11},{10,... | collective-permute-start | bytes 983048 | tf_op jit(solution)/shard_map/ppermute | solution.py:114
  15.1 2.5 %collective-permute-done.1 = f32[320,256]{1,0:T(8,128)S(1)} collective-permute-done((f32[320,256]{1,0:T(8,128)S(1)}, f32[320,256]{1,0:T(8,128)S(1)}, u32[]{:S(2)}, u32[]{:S(2)}) %collective-permute-start.1) | collective-permute-done | bytes 327712 | tf_op jit(solution)/shard_map/ppermute | solution.py:114
  17.6 2.4 %collective-permute-start.2 = (f32[320,256]{1,0:T(8,128)S(1)}, f32[320,256]{1,0:T(8,128)S(1)}, u32[]{:S(2)}, u32[]{:S(2)}) collective-permute-start(f32[320,256]{1,0:T(8,128)S(1)} %broadcast_select_fusion.5), channel_id=1, source_target_pairs={{0,4},{1,3},{2,6},{3,1},{4,0},{5,7},{6,2},{7,5},{8,12},{9,11},{10,... | collective-permute-start | bytes 983048 | tf_op jit(solution)/shard_map/ppermute | solution.py:114
  20.0 1.3 negate_select_fusion
  21.5 3.6 %collective-permute-done.2 = f32[320,256]{1,0:T(8,128)S(1)} collective-permute-done((f32[320,256]{1,0:T(8,128)S(1)}, f32[320,256]{1,0:T(8,128)S(1)}, u32[]{:S(2)}, u32[]{:S(2)}) %collective-permute-start.2) | collective-permute-done | bytes 327712 | tf_op jit(solution)/shard_map/ppermute | solution.py:114
  29.1 2.1 %collective-permute-start.12 = (f32[256,256]{1,0:T(8,128)S(1)}, f32[256,256]{1,0:T(8,128)S(1)}, u32[]{:S(2)}, u32[]{:S(2)}) collective-permute-start(f32[256,256]{1,0:T(8,128)S(1)} %convolution_bitcast_fusion.23), channel_id=1, source_target_pairs={{0,8},{8,0},{16,24},{24,16},{1,9},{9,1},{17,25},{25,17},{2,10},{10... | collective-permute-start | bytes 786440 | tf_op jit(solution)/shard_map/ppermute | solution.py:51
  31.2 2.1 %fusion.117 = f32[256,1024]{1,0:T(8,128)S(1)} fusion(f32[1024,256]{1,0:T(8,128)S(1)} %fusion.18, f32[1024,1024]{1,0:T(8,128)S(1)} %copy-done), kind=kOutput, calls=%fused_computation.187 | convolution fusion | flops 1610612736 | bytes 6291456 | tf_op jit(solution)/shard_map/dot_general | solution.py:47
  34.2 1.6 %collective-permute-start.9 = (f32[512,256]{1,0:T(8,128)S(1)}, f32[512,256]{1,0:T(8,128)S(1)}, u32[]{:S(2)}, u32[]{:S(2)}) collective-permute-start(f32[512,256]{1,0:T(8,128)S(1)} %select_select_fusion), channel_id=1, source_target_pairs={{0,2},{1,5},{2,0},{3,7},{4,6},{5,1},{6,4},{7,3},{8,10},{9,13},{10,... | collective-permute-start | bytes 1572872 | tf_op jit(solution)/shard_map/ppermute | solution.py:114
  37.3 1.5 %slice_subtract_fusion = f32[768,1024]{1,0:T(8,128)S(1)} fusion(f32[1024,1024]{1,0:T(8,128)S(1)} %copy-done, f32[256,1024]{1,0:T(8,128)S(1)} %fusion.89, f32[1024,256]{1,0:T(8,128)S(1)} %fusion.18), kind=kOutput, calls=%fused_computation.1 | convolution fusion | flops 1208745984 | bytes 8126464 | tf_op jit(solution)/shard_map/dot_general | solution.py:43
  39.5 2.7 %collective-permute-start.13 = (f32[256,256]{0,1:T(8,128)S(1)}, f32[256,256]{0,1:T(8,128)S(1)}, u32[]{:S(2)}, u32[]{:S(2)}) collective-permute-start(f32[256,256]{0,1:T(8,128)S(1)} %convolution_bitcast_fusion.21), channel_id=1, source_target_pairs={{0,16},{8,24},{16,0},{24,8},{1,17},{9,25},{17,1},{25,9},{2,18},{10... | collective-permute-start | bytes 786440 | tf_op jit(solution)/shard_map/ppermute | solution.py:51
  42.6 1.6 %collective-permute-start.16 = (f32[256,256]{1,0:T(8,128)S(1)}, f32[256,256]{1,0:T(8,128)S(1)}, u32[]{:S(2)}, u32[]{:S(2)}) collective-permute-start(f32[256,256]{1,0:T(8,128)S(1)} %negate_select_fusion.4), channel_id=1, source_target_pairs={{0,8},{8,0},{16,24},{24,16},{1,9},{9,1},{17,25},{25,17},{2,10},{10... | collective-permute-start | bytes 786440 | tf_op jit(solution)/shard_map/ppermute | solution.py:51
  44.3 1.6 %collective-permute-start.10 = (f32[512,256]{1,0:T(8,128)S(1)}, f32[512,256]{1,0:T(8,128)S(1)}, u32[]{:S(2)}, u32[]{:S(2)}) collective-permute-start(f32[512,256]{1,0:T(8,128)S(1)} %broadcast_select_fusion), channel_id=1, source_target_pairs={{0,4},{1,3},{2,6},{3,1},{4,0},{5,7},{6,2},{7,5},{8,12},{9,11},{10,... | collective-permute-start | bytes 1572872 | tf_op jit(solution)/shard_map/ppermute | solution.py:114
  46.8 3.6 %collective-permute-done.14 = f32[256,256]{0,1:T(8,128)S(1)} collective-permute-done((f32[256,256]{0,1:T(8,128)S(1)}, f32[256,256]{0,1:T(8,128)S(1)}, u32[]{:S(2)}, u32[]{:S(2)}) %collective-permute-start.14) | collective-permute-done | bytes 262176 | tf_op jit(solution)/shard_map/ppermute | solution.py:51
  50.9 2.7 %collective-permute-done.10 = f32[512,256]{1,0:T(8,128)S(1)} collective-permute-done((f32[512,256]{1,0:T(8,128)S(1)}, f32[512,256]{1,0:T(8,128)S(1)}, u32[]{:S(2)}, u32[]{:S(2)}) %collective-permute-start.10) | collective-permute-done | bytes 524320 | tf_op jit(solution)/shard_map/ppermute | solution.py:114
  54.1 1.9 %collective-permute-start.15 = (f32[256,256]{0,1:T(8,128)S(1)}, f32[256,256]{0,1:T(8,128)S(1)}, u32[]{:S(2)}, u32[]{:S(2)}) collective-permute-start(f32[256,256]{0,1:T(8,128)S(1)} %convolution_bitcast_fusion.16), channel_id=1, source_target_pairs={{0,16},{8,24},{16,0},{24,8},{1,17},{9,25},{17,1},{25,9},{2,18},{10... | collective-permute-start | bytes 786440 | tf_op jit(solution)/shard_map/ppermute | solution.py:51
  56.0 1.4 collective-permute-done.16
  58.2 2.7 %collective-permute-start.17 = (f32[256,256]{0,1:T(8,128)S(1)}, f32[256,256]{0,1:T(8,128)S(1)}, u32[]{:S(2)}, u32[]{:S(2)}) collective-permute-start(f32[256,256]{0,1:T(8,128)S(1)} %convolution_bitcast_fusion.12), channel_id=1, source_target_pairs={{0,16},{8,24},{16,0},{24,8},{1,17},{9,25},{17,1},{25,9},{2,18},{10... | collective-permute-start | bytes 786440 | tf_op jit(solution)/shard_map/ppermute | solution.py:51
  61.1 1.7 %fusion.19 = f32[256,1024]{1,0:T(8,128)S(1)} fusion(f32[768,1024]{1,0:T(8,128)S(1)} %slice_subtract_fusion, f32[384,256]{1,0:T(8,128)S(1)} %slice.288, f32[384,256]{1,0:T(8,128)S(1)} %slice.287), kind=kOutput, calls=%fused_computation.53 | convolution fusion | flops 1208156160 | bytes 4980736 | tf_op jit(solution)/shard_map/dot_general | solution.py:47
  66.1 2.4 %collective-permute-done.18 = f32[256,256]{1,0:T(8,128)S(1)} collective-permute-done((f32[256,256]{1,0:T(8,128)S(1)}, f32[256,256]{1,0:T(8,128)S(1)}, u32[]{:S(2)}, u32[]{:S(2)}) %collective-permute-start.18) | collective-permute-done | bytes 262176 | tf_op jit(solution)/shard_map/ppermute | solution.py:51
  70.2 4.4 %collective-permute-done.15 = f32[256,256]{0,1:T(8,128)S(1)} collective-permute-done((f32[256,256]{0,1:T(8,128)S(1)}, f32[256,256]{0,1:T(8,128)S(1)}, u32[]{:S(2)}, u32[]{:S(2)}) %collective-permute-start.15) | collective-permute-done | bytes 262176 | tf_op jit(solution)/shard_map/ppermute | solution.py:51
  74.9 6.2 %collective-permute-done.17 = f32[256,256]{0,1:T(8,128)S(1)} collective-permute-done((f32[256,256]{0,1:T(8,128)S(1)}, f32[256,256]{0,1:T(8,128)S(1)}, u32[]{:S(2)}, u32[]{:S(2)}) %collective-permute-start.17) | collective-permute-done | bytes 262176 | tf_op jit(solution)/shard_map/ppermute | solution.py:51
  81.5 8.0 %collective-permute-done.20 = f32[256,512]{1,0:T(8,128)S(1)} collective-permute-done((f32[256,512]{1,0:T(8,128)S(1)}, f32[256,512]{1,0:T(8,128)S(1)}, u32[]{:S(2)}, u32[]{:S(2)}) %collective-permute-start.20) | collective-permute-done | bytes 524320 | tf_op jit(solution)/shard_map/ppermute | solution.py:51
  91.3 1.7 %collective-permute-start.21 = (f32[256,512]{0,1:T(8,128)S(1)}, f32[256,512]{0,1:T(8,128)S(1)}, u32[]{:S(2)}, u32[]{:S(2)}) collective-permute-start(f32[256,512]{0,1:T(8,128)S(1)} %convolution_bitcast_fusion.5), channel_id=1, source_target_pairs={{0,16},{8,24},{16,0},{24,8},{1,17},{9,25},{17,1},{25,9},{2,18},{10... | collective-permute-start | bytes 1572872 | tf_op jit(solution)/shard_map/ppermute | solution.py:51
  93.0 19.3 %collective-permute-done.22 = f32[256,512]{0,1:T(8,128)S(1)} collective-permute-done((f32[256,512]{0,1:T(8,128)S(1)}, f32[256,512]{0,1:T(8,128)S(1)}, u32[]{:S(2)}, u32[]{:S(2)}) %collective-permute-start.22) | collective-permute-done | bytes 524320 | tf_op jit(solution)/shard_map/ppermute | solution.py:51
  114.3 14.1 %collective-permute-done.21 = f32[256,512]{0,1:T(8,128)S(1)} collective-permute-done((f32[256,512]{0,1:T(8,128)S(1)}, f32[256,512]{0,1:T(8,128)S(1)}, u32[]{:S(2)}, u32[]{:S(2)}) %collective-permute-start.21) | collective-permute-done | bytes 524320 | tf_op jit(solution)/shard_map/ppermute | solution.py:51
  128.9 9.6 %collective-permute-done.23 = f32[256,512]{0,1:T(8,128)S(1)} collective-permute-done((f32[256,512]{0,1:T(8,128)S(1)}, f32[256,512]{0,1:T(8,128)S(1)}, u32[]{:S(2)}, u32[]{:S(2)}) %collective-permute-start.23) | collective-permute-done | bytes 524320 | tf_op jit(solution)/shard_map/ppermute | solution.py:51
  138.5 1.2 fusion.5
  (94 shorter events, 22.1 us)
Async XLA Ops:
  0.0 3.2 %copy-start.4 = (s32[2]{0:T(128)S(1)}, s32[2]{0:T(128)}, u32[]{:S(2)}) copy-start(s32[2]{0:T(128)} %param.7) | copy-start | bytes 28
  2.6 1.8 %collective-permute-start = (f32[320,256]{1,0:T(8,128)S(1)}, f32[320,256]{1,0:T(8,128)S(1)}, u32[]{:S(2)}, u32[]{:S(2)}) collective-permute-start(f32[320,256]{1,0:T(8,128)S(1)} %get-tuple-element.21), channel_id=1, source_target_pairs={{0,1},{1,0},{2,3},{3,2},{4,5},{5,4},{6,7},{7,6},{8,9},{9,8},{10,11... | collective-permute-start | bytes 983048 | tf_op jit(solution)/shard_map/ppermute | solution.py:55
  3.1 1.7 %collective-permute-start.4 = (f32[320,256]{1,0:T(8,128)S(1)}, f32[320,256]{1,0:T(8,128)S(1)}, u32[]{:S(2)}, u32[]{:S(2)}) collective-permute-start(f32[320,256]{1,0:T(8,128)S(1)} %get-tuple-element.22), channel_id=1, source_target_pairs={{0,1},{1,0},{2,3},{3,2},{4,5},{5,4},{6,7},{7,6},{8,9},{9,8},{10,11... | collective-permute-start | bytes 983048 | tf_op jit(solution)/shard_map/ppermute | solution.py:55
  4.9 8.0 %collective-permute-start.5 = (f32[320,256]{1,0:T(8,128)S(1)}, f32[320,256]{1,0:T(8,128)S(1)}, u32[]{:S(2)}, u32[]{:S(2)}) collective-permute-start(f32[320,256]{1,0:T(8,128)S(1)} %get-tuple-element.20), channel_id=1, source_target_pairs={{0,2},{1,5},{2,0},{3,7},{4,6},{5,1},{6,4},{7,3},{8,10},{9,13},{10,... | collective-permute-start | bytes 983048 | tf_op jit(solution)/shard_map/ppermute | solution.py:114
  7.8 9.7 %collective-permute-start.1 = (f32[320,256]{1,0:T(8,128)S(1)}, f32[320,256]{1,0:T(8,128)S(1)}, u32[]{:S(2)}, u32[]{:S(2)}) collective-permute-start(f32[320,256]{1,0:T(8,128)S(1)} %get-tuple-element.19), channel_id=1, source_target_pairs={{0,2},{1,5},{2,0},{3,7},{4,6},{5,1},{6,4},{7,3},{8,10},{9,13},{10,... | collective-permute-start | bytes 983048 | tf_op jit(solution)/shard_map/ppermute | solution.py:114
  12.9 8.4 %collective-permute-start.6 = (f32[320,256]{1,0:T(8,128)S(1)}, f32[320,256]{1,0:T(8,128)S(1)}, u32[]{:S(2)}, u32[]{:S(2)}) collective-permute-start(f32[320,256]{1,0:T(8,128)S(1)} %broadcast_select_fusion.4), channel_id=1, source_target_pairs={{0,4},{1,3},{2,6},{3,1},{4,0},{5,7},{6,2},{7,5},{8,12},{9,11},{10,... | collective-permute-start | bytes 983048 | tf_op jit(solution)/shard_map/ppermute | solution.py:114
  17.6 7.5 %collective-permute-start.2 = (f32[320,256]{1,0:T(8,128)S(1)}, f32[320,256]{1,0:T(8,128)S(1)}, u32[]{:S(2)}, u32[]{:S(2)}) collective-permute-start(f32[320,256]{1,0:T(8,128)S(1)} %broadcast_select_fusion.5), channel_id=1, source_target_pairs={{0,4},{1,3},{2,6},{3,1},{4,0},{5,7},{6,2},{7,5},{8,12},{9,11},{10,... | collective-permute-start | bytes 983048 | tf_op jit(solution)/shard_map/ppermute | solution.py:114
  21.4 4.4 %collective-permute-start.7 = (f32[320,256]{1,0:T(8,128)S(1)}, f32[320,256]{1,0:T(8,128)S(1)}, u32[]{:S(2)}, u32[]{:S(2)}) collective-permute-start(f32[320,256]{1,0:T(8,128)S(1)} %broadcast_select_fusion.6), channel_id=1, source_target_pairs={{0,1},{1,0},{2,3},{3,2},{4,5},{5,4},{6,7},{7,6},{8,9},{9,8},{10,11... | collective-permute-start | bytes 983048 | tf_op jit(solution)/shard_map/ppermute | solution.py:55
  25.1 1.7 %collective-permute-start.3 = (f32[320,256]{1,0:T(8,128)S(1)}, f32[320,256]{1,0:T(8,128)S(1)}, u32[]{:S(2)}, u32[]{:S(2)}) collective-permute-start(f32[320,256]{1,0:T(8,128)S(1)} %broadcast_select_fusion.7), channel_id=1, source_target_pairs={{0,1},{1,0},{2,3},{3,2},{4,5},{5,4},{6,7},{7,6},{8,9},{9,8},{10,11... | collective-permute-start | bytes 983048 | tf_op jit(solution)/shard_map/ppermute | solution.py:55
  25.3 8.8 %collective-permute-start.8 = (f32[512,256]{1,0:T(8,128)S(1)}, f32[512,256]{1,0:T(8,128)S(1)}, u32[]{:S(2)}, u32[]{:S(2)}) collective-permute-start(f32[512,256]{1,0:T(8,128)S(1)} %negate_select_fusion.2), channel_id=1, source_target_pairs={{0,1},{1,0},{2,3},{3,2},{4,5},{5,4},{6,7},{7,6},{8,9},{9,8},{10,11... | collective-permute-start | bytes 1572872 | tf_op jit(solution)/shard_map/ppermute | solution.py:55
  25.9 2.8 %copy-start.1 = (f32[2,2,256,256]{3,2,1,0:T(8,128)S(1)}, f32[2,2,256,256]{3,2,1,0:T(8,128)}, u32[]{:S(2)}) copy-start(f32[2,2,256,256]{3,2,1,0:T(8,128)} %param.10) | copy-start | bytes 3145732
  25.9 5.3 %copy-start = (f32[1024,1024]{1,0:T(8,128)S(1)}, f32[1024,1024]{1,0:T(8,128)}, u32[]{:S(2)}) copy-start(f32[1024,1024]{1,0:T(8,128)} %param.6) | copy-start | bytes 12582916
  29.1 9.8 %collective-permute-start.12 = (f32[256,256]{1,0:T(8,128)S(1)}, f32[256,256]{1,0:T(8,128)S(1)}, u32[]{:S(2)}, u32[]{:S(2)}) collective-permute-start(f32[256,256]{1,0:T(8,128)S(1)} %convolution_bitcast_fusion.23), channel_id=1, source_target_pairs={{0,8},{8,0},{16,24},{24,16},{1,9},{9,1},{17,25},{25,17},{2,10},{10... | collective-permute-start | bytes 786440 | tf_op jit(solution)/shard_map/ppermute | solution.py:51
  34.2 10.0 %collective-permute-start.9 = (f32[512,256]{1,0:T(8,128)S(1)}, f32[512,256]{1,0:T(8,128)S(1)}, u32[]{:S(2)}, u32[]{:S(2)}) collective-permute-start(f32[512,256]{1,0:T(8,128)S(1)} %select_select_fusion), channel_id=1, source_target_pairs={{0,2},{1,5},{2,0},{3,7},{4,6},{5,1},{6,4},{7,3},{8,10},{9,13},{10,... | collective-permute-start | bytes 1572872 | tf_op jit(solution)/shard_map/ppermute | solution.py:114
  36.8 2.0 %copy-start.2 = (f32[2,2,256,256]{3,2,1,0:T(8,128)S(1)}, f32[2,2,256,256]{3,2,1,0:T(8,128)}, u32[]{:S(2)}) copy-start(f32[2,2,256,256]{3,2,1,0:T(8,128)} %param.11) | copy-start | bytes 3145732
  36.8 13.7 %collective-permute-start.14 = (f32[256,256]{0,1:T(8,128)S(1)}, f32[256,256]{0,1:T(8,128)S(1)}, u32[]{:S(2)}, u32[]{:S(2)}) collective-permute-start(f32[256,256]{0,1:T(8,128)S(1)} %convolution_bitcast_fusion.18), channel_id=1, source_target_pairs={{0,8},{8,0},{16,24},{24,16},{1,9},{9,1},{17,25},{25,17},{2,10},{10... | collective-permute-start | bytes 786440 | tf_op jit(solution)/shard_map/ppermute | solution.py:51
  39.5 30.3 %collective-permute-start.13 = (f32[256,256]{0,1:T(8,128)S(1)}, f32[256,256]{0,1:T(8,128)S(1)}, u32[]{:S(2)}, u32[]{:S(2)}) collective-permute-start(f32[256,256]{0,1:T(8,128)S(1)} %convolution_bitcast_fusion.21), channel_id=1, source_target_pairs={{0,16},{8,24},{16,0},{24,8},{1,17},{9,25},{17,1},{25,9},{2,18},{10... | collective-permute-start | bytes 786440 | tf_op jit(solution)/shard_map/ppermute | solution.py:51
  42.6 14.8 %collective-permute-start.16 = (f32[256,256]{1,0:T(8,128)S(1)}, f32[256,256]{1,0:T(8,128)S(1)}, u32[]{:S(2)}, u32[]{:S(2)}) collective-permute-start(f32[256,256]{1,0:T(8,128)S(1)} %negate_select_fusion.4), channel_id=1, source_target_pairs={{0,8},{8,0},{16,24},{24,16},{1,9},{9,1},{17,25},{25,17},{2,10},{10... | collective-permute-start | bytes 786440 | tf_op jit(solution)/shard_map/ppermute | solution.py:51
  44.3 9.2 %collective-permute-start.10 = (f32[512,256]{1,0:T(8,128)S(1)}, f32[512,256]{1,0:T(8,128)S(1)}, u32[]{:S(2)}, u32[]{:S(2)}) collective-permute-start(f32[512,256]{1,0:T(8,128)S(1)} %broadcast_select_fusion), channel_id=1, source_target_pairs={{0,4},{1,3},{2,6},{3,1},{4,0},{5,7},{6,2},{7,5},{8,12},{9,11},{10,... | collective-permute-start | bytes 1572872 | tf_op jit(solution)/shard_map/ppermute | solution.py:114
  46.3 22.2 %collective-permute-start.18 = (f32[256,256]{1,0:T(8,128)S(1)}, f32[256,256]{1,0:T(8,128)S(1)}, u32[]{:S(2)}, u32[]{:S(2)}) collective-permute-start(f32[256,256]{1,0:T(8,128)S(1)} %negate_select_fusion.6), channel_id=1, source_target_pairs={{0,8},{8,0},{16,24},{24,16},{1,9},{9,1},{17,25},{25,17},{2,10},{10... | collective-permute-start | bytes 786440 | tf_op jit(solution)/shard_map/ppermute | solution.py:51
  53.6 7.3 %collective-permute-start.11 = (f32[512,256]{1,0:T(8,128)S(1)}, f32[512,256]{1,0:T(8,128)S(1)}, u32[]{:S(2)}, u32[]{:S(2)}) collective-permute-start(f32[512,256]{1,0:T(8,128)S(1)} %broadcast_select_fusion.1), channel_id=1, source_target_pairs={{0,1},{1,0},{2,3},{3,2},{4,5},{5,4},{6,7},{7,6},{8,9},{9,8},{10,11... | collective-permute-start | bytes 1572872 | tf_op jit(solution)/shard_map/ppermute | solution.py:55
  54.1 20.5 %collective-permute-start.15 = (f32[256,256]{0,1:T(8,128)S(1)}, f32[256,256]{0,1:T(8,128)S(1)}, u32[]{:S(2)}, u32[]{:S(2)}) collective-permute-start(f32[256,256]{0,1:T(8,128)S(1)} %convolution_bitcast_fusion.16), channel_id=1, source_target_pairs={{0,16},{8,24},{16,0},{24,8},{1,17},{9,25},{17,1},{25,9},{2,18},{10... | collective-permute-start | bytes 786440 | tf_op jit(solution)/shard_map/ppermute | solution.py:51
  58.2 23.0 %collective-permute-start.17 = (f32[256,256]{0,1:T(8,128)S(1)}, f32[256,256]{0,1:T(8,128)S(1)}, u32[]{:S(2)}, u32[]{:S(2)}) collective-permute-start(f32[256,256]{0,1:T(8,128)S(1)} %convolution_bitcast_fusion.12), channel_id=1, source_target_pairs={{0,16},{8,24},{16,0},{24,8},{1,17},{9,25},{17,1},{25,9},{2,18},{10... | collective-permute-start | bytes 786440 | tf_op jit(solution)/shard_map/ppermute | solution.py:51
  64.6 24.9 %collective-permute-start.20 = (f32[256,512]{1,0:T(8,128)S(1)}, f32[256,512]{1,0:T(8,128)S(1)}, u32[]{:S(2)}, u32[]{:S(2)}) collective-permute-start(f32[256,512]{1,0:T(8,128)S(1)} %convolution_bitcast_fusion.7), channel_id=1, source_target_pairs={{0,8},{8,0},{16,24},{24,16},{1,9},{9,1},{17,25},{25,17},{2,10},{10... | collective-permute-start | bytes 1572872 | tf_op jit(solution)/shard_map/ppermute | solution.py:51
  69.8 44.2 %collective-permute-start.19 = (f32[256,256]{0,1:T(8,128)S(1)}, f32[256,256]{0,1:T(8,128)S(1)}, u32[]{:S(2)}, u32[]{:S(2)}) collective-permute-start(f32[256,256]{0,1:T(8,128)S(1)} %convolution_bitcast_fusion.9), channel_id=1, source_target_pairs={{0,16},{8,24},{16,0},{24,8},{1,17},{9,25},{17,1},{25,9},{2,18},{10... | collective-permute-start | bytes 786440 | tf_op jit(solution)/shard_map/ppermute | solution.py:51
  90.2 22.1 %collective-permute-start.22 = (f32[256,512]{0,1:T(8,128)S(1)}, f32[256,512]{0,1:T(8,128)S(1)}, u32[]{:S(2)}, u32[]{:S(2)}) collective-permute-start(f32[256,512]{0,1:T(8,128)S(1)} %negate_select_fusion.1), channel_id=1, source_target_pairs={{0,8},{8,0},{16,24},{24,16},{1,9},{9,1},{17,25},{25,17},{2,10},{10... | collective-permute-start | bytes 1572872 | tf_op jit(solution)/shard_map/ppermute | solution.py:51
  91.3 37.2 %collective-permute-start.21 = (f32[256,512]{0,1:T(8,128)S(1)}, f32[256,512]{0,1:T(8,128)S(1)}, u32[]{:S(2)}, u32[]{:S(2)}) collective-permute-start(f32[256,512]{0,1:T(8,128)S(1)} %convolution_bitcast_fusion.5), channel_id=1, source_target_pairs={{0,16},{8,24},{16,0},{24,8},{1,17},{9,25},{17,1},{25,9},{2,18},{10... | collective-permute-start | bytes 1572872 | tf_op jit(solution)/shard_map/ppermute | solution.py:51
  113.4 25.2 %collective-permute-start.23 = (f32[256,512]{0,1:T(8,128)S(1)}, f32[256,512]{0,1:T(8,128)S(1)}, u32[]{:S(2)}, u32[]{:S(2)}) collective-permute-start(f32[256,512]{0,1:T(8,128)S(1)} %convolution_bitcast_fusion.1), channel_id=1, source_target_pairs={{0,16},{8,24},{16,0},{24,8},{1,17},{9,25},{17,1},{25,9},{2,18},{10... | collective-permute-start | bytes 1572872 | tf_op jit(solution)/shard_map/ppermute | solution.py:51
  128.9 9.7 %copy-start.3 = (f32[1024,1024]{1,0:T(8,128)}, f32[1024,1024]{1,0:T(8,128)S(1)}, u32[]{:S(2)}) copy-start(f32[1024,1024]{1,0:T(8,128)S(1)} %fusion.2) | copy-start | bytes 12582916

commit v8 on v7

--- a/solution.py
+++ b/solution.py
@@ -19,12 +19,12 @@
     ("send0.3", "got0.0"),
     ("begin1", "arr0.0"),
     ("move1.0", "own0.0"),
-    ("move1.1", ""),
+    ("tree0.0", ""),
+    ("move1.1", "up0.0"),
     ("end1", ""),
     ("leaf1", ""),
     ("send1.0", ""),
     ("send1.1", "got1.0"),
-    ("tree0.0", ""),
     ("tree0.1", "own0.3"),
     ("tree0.2", ""),
     ("tree0.3", "own1.0"),

time: 140 us -> 140 us (level)
  no operation moved by 1% of the time
where the time goes in v8:
time: 140 us
  waiting for transfers between devices  82.3 us (59%)
  starting transfers between devices  27 us (19%)
  matrix products  21.3 us (15%)
  local copies, waits for them, and re-layouts  4.34 us (3%)
  other arithmetic  2.91 us (2%)
  between operations  1.95 us (1%)
    ppermute x12, waiting for transfers between devices, from_partner(): lax.ppermute(shard, 'row', [(i, i ^ 1 << apart) for i in range(lax.axis_s...  69.2 us
    ppermute x12, starting transfers between devices, from_partner(): lax.ppermute(shard, 'row', [(i, i ^ 1 << apart) for i in range(lax.axis_s...  14.9 us
    dot_general x18, matrix products, dot_t(): lax.dot_general(a, b, LEADING, precision=PRECISION, preferred_element_typ...  12 us
    ppermute x6, waiting for transfers between devices, exchange(): self.arrived = [lax.ppermute(c, 'col', pairs) for c in self.current]  11.9 us
    ppermute x6, starting transfers between devices, exchange(): self.arrived = [lax.ppermute(c, 'col', pairs) for c in self.current]  10.7 us
    dot_general x17, matrix products, dot(): jnp.dot(a, b, precision=PRECISION, preferred_element_type=jnp.float32)  9.29 us
  transfers between devices with their start and end apart: 24, of which 15 were waited for; matrix products, arithmetic and copies ran while one was open for 18% of the time, Pallas kernels for 0%

profile of v8, /device:TPU:0, one launch (start us, length us, event | category | flops | bytes accessed | tf_op | source)
XLA Modules:
  0.0 139.7 jit_solution(18250921483475515679)
XLA Ops:
  0.0 1.1 slice_bitcast_fusion.5
  1.1 1.3 slice_bitcast_fusion.1
  4.9 2.9 %collective-permute-start.5 = (f32[320,256]{1,0:T(8,128)S(1)}, f32[320,256]{1,0:T(8,128)S(1)}, u32[]{:S(2)}, u32[]{:S(2)}) collective-permute-start(f32[320,256]{1,0:T(8,128)S(1)} %get-tuple-element.20), channel_id=1, source_target_pairs={{0,2},{1,5},{2,0},{3,7},{4,6},{5,1},{6,4},{7,3},{8,10},{9,13},{10,... | collective-permute-start | bytes 983048 | tf_op jit(solution)/shard_map/ppermute | solution.py:114
  7.9 1.2 slice_bitcast_fusion.3
  9.8 3.1 %collective-permute-done.5 = f32[320,256]{1,0:T(8,128)S(1)} collective-permute-done((f32[320,256]{1,0:T(8,128)S(1)}, f32[320,256]{1,0:T(8,128)S(1)}, u32[]{:S(2)}, u32[]{:S(2)}) %collective-permute-start.5) | collective-permute-done | bytes 327712 | tf_op jit(solution)/shard_map/ppermute | solution.py:114
  12.9 2.1 %collective-permute-start.6 = (f32[320,256]{1,0:T(8,128)S(1)}, f32[320,256]{1,0:T(8,128)S(1)}, u32[]{:S(2)}, u32[]{:S(2)}) collective-permute-start(f32[320,256]{1,0:T(8,128)S(1)} %broadcast_select_fusion.4), channel_id=1, source_target_pairs={{0,4},{1,3},{2,6},{3,1},{4,0},{5,7},{6,2},{7,5},{8,12},{9,11},{10,... | collective-permute-start | bytes 983048 | tf_op jit(solution)/shard_map/ppermute | solution.py:114
  15.1 2.5 %collective-permute-done.1 = f32[320,256]{1,0:T(8,128)S(1)} collective-permute-done((f32[320,256]{1,0:T(8,128)S(1)}, f32[320,256]{1,0:T(8,128)S(1)}, u32[]{:S(2)}, u32[]{:S(2)}) %collective-permute-start.1) | collective-permute-done | bytes 327712 | tf_op jit(solution)/shard_map/ppermute | solution.py:114
  17.6 2.4 %collective-permute-start.2 = (f32[320,256]{1,0:T(8,128)S(1)}, f32[320,256]{1,0:T(8,128)S(1)}, u32[]{:S(2)}, u32[]{:S(2)}) collective-permute-start(f32[320,256]{1,0:T(8,128)S(1)} %broadcast_select_fusion.5), channel_id=1, source_target_pairs={{0,4},{1,3},{2,6},{3,1},{4,0},{5,7},{6,2},{7,5},{8,12},{9,11},{10,... | collective-permute-start | bytes 983048 | tf_op jit(solution)/shard_map/ppermute | solution.py:114
  20.0 1.3 negate_select_fusion
  21.5 3.6 %collective-permute-done.2 = f32[320,256]{1,0:T(8,128)S(1)} collective-permute-done((f32[320,256]{1,0:T(8,128)S(1)}, f32[320,256]{1,0:T(8,128)S(1)}, u32[]{:S(2)}, u32[]{:S(2)}) %collective-permute-start.2) | collective-permute-done | bytes 327712 | tf_op jit(solution)/shard_map/ppermute | solution.py:114
  29.1 2.1 %collective-permute-start.8 = (f32[256,256]{1,0:T(8,128)S(1)}, f32[256,256]{1,0:T(8,128)S(1)}, u32[]{:S(2)}, u32[]{:S(2)}) collective-permute-start(f32[256,256]{1,0:T(8,128)S(1)} %convolution_bitcast_fusion.23), channel_id=1, source_target_pairs={{0,8},{8,0},{16,24},{24,16},{1,9},{9,1},{17,25},{25,17},{2,10},{10... | collective-permute-start | bytes 786440 | tf_op jit(solution)/shard_map/ppermute | solution.py:51
  31.2 2.1 %fusion.117 = f32[256,1024]{1,0:T(8,128)S(1)} fusion(f32[1024,256]{1,0:T(8,128)S(1)} %fusion.18, f32[1024,1024]{1,0:T(8,128)S(1)} %copy-done), kind=kOutput, calls=%fused_computation.188 | convolution fusion | flops 1610612736 | bytes 6291456 | tf_op jit(solution)/shard_map/dot_general | solution.py:47
  34.2 1.6 %collective-permute-start.10 = (f32[512,256]{1,0:T(8,128)S(1)}, f32[512,256]{1,0:T(8,128)S(1)}, u32[]{:S(2)}, u32[]{:S(2)}) collective-permute-start(f32[512,256]{1,0:T(8,128)S(1)} %select_select_fusion), channel_id=1, source_target_pairs={{0,2},{1,5},{2,0},{3,7},{4,6},{5,1},{6,4},{7,3},{8,10},{9,13},{10,... | collective-permute-start | bytes 1572872 | tf_op jit(solution)/shard_map/ppermute | solution.py:114
  37.3 1.5 %slice_subtract_fusion = f32[768,1024]{1,0:T(8,128)S(1)} fusion(f32[1024,1024]{1,0:T(8,128)S(1)} %copy-done, f32[256,1024]{1,0:T(8,128)S(1)} %fusion.89, f32[1024,256]{1,0:T(8,128)S(1)} %fusion.18), kind=kOutput, calls=%fused_computation.1 | convolution fusion | flops 1208745984 | bytes 8126464 | tf_op jit(solution)/shard_map/dot_general | solution.py:43
  39.5 2.6 %collective-permute-start.13 = (f32[256,256]{1,0:T(8,128)S(1)}, f32[256,256]{1,0:T(8,128)S(1)}, u32[]{:S(2)}, u32[]{:S(2)}) collective-permute-start(f32[256,256]{1,0:T(8,128)S(1)} %convolution_bitcast_fusion.21), channel_id=1, source_target_pairs={{0,16},{8,24},{16,0},{24,8},{1,17},{9,25},{17,1},{25,9},{2,18},{10... | collective-permute-start | bytes 786440 | tf_op jit(solution)/shard_map/ppermute | solution.py:51
  42.6 1.6 %collective-permute-start.16 = (f32[256,256]{1,0:T(8,128)S(1)}, f32[256,256]{1,0:T(8,128)S(1)}, u32[]{:S(2)}, u32[]{:S(2)}) collective-permute-start(f32[256,256]{1,0:T(8,128)S(1)} %negate_select_fusion.4), channel_id=1, source_target_pairs={{0,8},{8,0},{16,24},{24,16},{1,9},{9,1},{17,25},{25,17},{2,10},{10... | collective-permute-start | bytes 786440 | tf_op jit(solution)/shard_map/ppermute | solution.py:51
  44.3 1.6 %collective-permute-start.11 = (f32[512,256]{1,0:T(8,128)S(1)}, f32[512,256]{1,0:T(8,128)S(1)}, u32[]{:S(2)}, u32[]{:S(2)}) collective-permute-start(f32[512,256]{1,0:T(8,128)S(1)} %broadcast_select_fusion), channel_id=1, source_target_pairs={{0,4},{1,3},{2,6},{3,1},{4,0},{5,7},{6,2},{7,5},{8,12},{9,11},{10,... | collective-permute-start | bytes 1572872 | tf_op jit(solution)/shard_map/ppermute | solution.py:114
  46.9 3.6 %collective-permute-done.14 = f32[256,256]{0,1:T(8,128)S(1)} collective-permute-done((f32[256,256]{0,1:T(8,128)S(1)}, f32[256,256]{0,1:T(8,128)S(1)}, u32[]{:S(2)}, u32[]{:S(2)}) %collective-permute-start.14) | collective-permute-done | bytes 262176 | tf_op jit(solution)/shard_map/ppermute | solution.py:51
  50.9 2.7 %collective-permute-done.11 = f32[512,256]{1,0:T(8,128)S(1)} collective-permute-done((f32[512,256]{1,0:T(8,128)S(1)}, f32[512,256]{1,0:T(8,128)S(1)}, u32[]{:S(2)}, u32[]{:S(2)}) %collective-permute-start.11) | collective-permute-done | bytes 524320 | tf_op jit(solution)/shard_map/ppermute | solution.py:114
  54.1 1.8 %collective-permute-start.15 = (f32[256,256]{0,1:T(8,128)S(1)}, f32[256,256]{0,1:T(8,128)S(1)}, u32[]{:S(2)}, u32[]{:S(2)}) collective-permute-start(f32[256,256]{0,1:T(8,128)S(1)} %convolution_bitcast_fusion.16), channel_id=1, source_target_pairs={{0,16},{8,24},{16,0},{24,8},{1,17},{9,25},{17,1},{25,9},{2,18},{10... | collective-permute-start | bytes 786440 | tf_op jit(solution)/shard_map/ppermute | solution.py:51
  56.0 1.4 collective-permute-done.16
  58.2 2.7 %collective-permute-start.17 = (f32[256,256]{0,1:T(8,128)S(1)}, f32[256,256]{0,1:T(8,128)S(1)}, u32[]{:S(2)}, u32[]{:S(2)}) collective-permute-start(f32[256,256]{0,1:T(8,128)S(1)} %convolution_bitcast_fusion.12), channel_id=1, source_target_pairs={{0,16},{8,24},{16,0},{24,8},{1,17},{9,25},{17,1},{25,9},{2,18},{10... | collective-permute-start | bytes 786440 | tf_op jit(solution)/shard_map/ppermute | solution.py:51
  61.1 1.7 %fusion.19 = f32[256,1024]{1,0:T(8,128)S(1)} fusion(f32[768,1024]{1,0:T(8,128)S(1)} %slice_subtract_fusion, f32[384,256]{1,0:T(8,128)S(1)} %slice.293, f32[384,256]{1,0:T(8,128)S(1)} %slice.292), kind=kOutput, calls=%fused_computation.53 | convolution fusion | flops 1208156160 | bytes 4980736 | tf_op jit(solution)/shard_map/dot_general | solution.py:47
  66.1 2.3 %collective-permute-done.18 = f32[256,256]{1,0:T(8,128)S(1)} collective-permute-done((f32[256,256]{1,0:T(8,128)S(1)}, f32[256,256]{1,0:T(8,128)S(1)}, u32[]{:S(2)}, u32[]{:S(2)}) %collective-permute-start.18) | collective-permute-done | bytes 262176 | tf_op jit(solution)/shard_map/ppermute | solution.py:51
  70.1 4.5 %collective-permute-done.15 = f32[256,256]{0,1:T(8,128)S(1)} collective-permute-done((f32[256,256]{0,1:T(8,128)S(1)}, f32[256,256]{0,1:T(8,128)S(1)}, u32[]{:S(2)}, u32[]{:S(2)}) %collective-permute-start.15) | collective-permute-done | bytes 262176 | tf_op jit(solution)/shard_map/ppermute | solution.py:51
  75.0 6.2 %collective-permute-done.17 = f32[256,256]{0,1:T(8,128)S(1)} collective-permute-done((f32[256,256]{0,1:T(8,128)S(1)}, f32[256,256]{0,1:T(8,128)S(1)}, u32[]{:S(2)}, u32[]{:S(2)}) %collective-permute-start.17) | collective-permute-done | bytes 262176 | tf_op jit(solution)/shard_map/ppermute | solution.py:51
  81.5 8.0 %collective-permute-done.20 = f32[256,512]{1,0:T(8,128)S(1)} collective-permute-done((f32[256,512]{1,0:T(8,128)S(1)}, f32[256,512]{1,0:T(8,128)S(1)}, u32[]{:S(2)}, u32[]{:S(2)}) %collective-permute-start.20) | collective-permute-done | bytes 524320 | tf_op jit(solution)/shard_map/ppermute | solution.py:51
  91.3 1.7 %collective-permute-start.21 = (f32[256,512]{0,1:T(8,128)S(1)}, f32[256,512]{0,1:T(8,128)S(1)}, u32[]{:S(2)}, u32[]{:S(2)}) collective-permute-start(f32[256,512]{0,1:T(8,128)S(1)} %convolution_bitcast_fusion.5), channel_id=1, source_target_pairs={{0,16},{8,24},{16,0},{24,8},{1,17},{9,25},{17,1},{25,9},{2,18},{10... | collective-permute-start | bytes 1572872 | tf_op jit(solution)/shard_map/ppermute | solution.py:51
  93.0 19.3 %collective-permute-done.22 = f32[256,512]{0,1:T(8,128)S(1)} collective-permute-done((f32[256,512]{0,1:T(8,128)S(1)}, f32[256,512]{0,1:T(8,128)S(1)}, u32[]{:S(2)}, u32[]{:S(2)}) %collective-permute-start.22) | collective-permute-done | bytes 524320 | tf_op jit(solution)/shard_map/ppermute | solution.py:51
  114.3 14.1 %collective-permute-done.21 = f32[256,512]{0,1:T(8,128)S(1)} collective-permute-done((f32[256,512]{0,1:T(8,128)S(1)}, f32[256,512]{0,1:T(8,128)S(1)}, u32[]{:S(2)}, u32[]{:S(2)}) %collective-permute-start.21) | collective-permute-done | bytes 524320 | tf_op jit(solution)/shard_map/ppermute | solution.py:51
  128.8 9.7 %collective-permute-done.23 = f32[256,512]{0,1:T(8,128)S(1)} collective-permute-done((f32[256,512]{0,1:T(8,128)S(1)}, f32[256,512]{0,1:T(8,128)S(1)}, u32[]{:S(2)}, u32[]{:S(2)}) %collective-permute-start.23) | collective-permute-done | bytes 524320 | tf_op jit(solution)/shard_map/ppermute | solution.py:51
  138.5 1.2 fusion.5
  (95 shorter events, 22.0 us)
Async XLA Ops:
  0.0 3.2 %copy-start.4 = (s32[2]{0:T(128)S(1)}, s32[2]{0:T(128)}, u32[]{:S(2)}) copy-start(s32[2]{0:T(128)} %param.7) | copy-start | bytes 28
  2.6 1.9 %collective-permute-start = (f32[320,256]{1,0:T(8,128)S(1)}, f32[320,256]{1,0:T(8,128)S(1)}, u32[]{:S(2)}, u32[]{:S(2)}) collective-permute-start(f32[320,256]{1,0:T(8,128)S(1)} %get-tuple-element.21), channel_id=1, source_target_pairs={{0,1},{1,0},{2,3},{3,2},{4,5},{5,4},{6,7},{7,6},{8,9},{9,8},{10,11... | collective-permute-start | bytes 983048 | tf_op jit(solution)/shard_map/ppermute | solution.py:55
  3.1 1.7 %collective-permute-start.4 = (f32[320,256]{1,0:T(8,128)S(1)}, f32[320,256]{1,0:T(8,128)S(1)}, u32[]{:S(2)}, u32[]{:S(2)}) collective-permute-start(f32[320,256]{1,0:T(8,128)S(1)} %get-tuple-element.22), channel_id=1, source_target_pairs={{0,1},{1,0},{2,3},{3,2},{4,5},{5,4},{6,7},{7,6},{8,9},{9,8},{10,11... | collective-permute-start | bytes 983048 | tf_op jit(solution)/shard_map/ppermute | solution.py:55
  4.9 8.0 %collective-permute-start.5 = (f32[320,256]{1,0:T(8,128)S(1)}, f32[320,256]{1,0:T(8,128)S(1)}, u32[]{:S(2)}, u32[]{:S(2)}) collective-permute-start(f32[320,256]{1,0:T(8,128)S(1)} %get-tuple-element.20), channel_id=1, source_target_pairs={{0,2},{1,5},{2,0},{3,7},{4,6},{5,1},{6,4},{7,3},{8,10},{9,13},{10,... | collective-permute-start | bytes 983048 | tf_op jit(solution)/shard_map/ppermute | solution.py:114
  7.8 9.7 %collective-permute-start.1 = (f32[320,256]{1,0:T(8,128)S(1)}, f32[320,256]{1,0:T(8,128)S(1)}, u32[]{:S(2)}, u32[]{:S(2)}) collective-permute-start(f32[320,256]{1,0:T(8,128)S(1)} %get-tuple-element.19), channel_id=1, source_target_pairs={{0,2},{1,5},{2,0},{3,7},{4,6},{5,1},{6,4},{7,3},{8,10},{9,13},{10,... | collective-permute-start | bytes 983048 | tf_op jit(solution)/shard_map/ppermute | solution.py:114
  12.9 8.4 %collective-permute-start.6 = (f32[320,256]{1,0:T(8,128)S(1)}, f32[320,256]{1,0:T(8,128)S(1)}, u32[]{:S(2)}, u32[]{:S(2)}) collective-permute-start(f32[320,256]{1,0:T(8,128)S(1)} %broadcast_select_fusion.4), channel_id=1, source_target_pairs={{0,4},{1,3},{2,6},{3,1},{4,0},{5,7},{6,2},{7,5},{8,12},{9,11},{10,... | collective-permute-start | bytes 983048 | tf_op jit(solution)/shard_map/ppermute | solution.py:114
  17.6 7.5 %collective-permute-start.2 = (f32[320,256]{1,0:T(8,128)S(1)}, f32[320,256]{1,0:T(8,128)S(1)}, u32[]{:S(2)}, u32[]{:S(2)}) collective-permute-start(f32[320,256]{1,0:T(8,128)S(1)} %broadcast_select_fusion.5), channel_id=1, source_target_pairs={{0,4},{1,3},{2,6},{3,1},{4,0},{5,7},{6,2},{7,5},{8,12},{9,11},{10,... | collective-permute-start | bytes 983048 | tf_op jit(solution)/shard_map/ppermute | solution.py:114
  21.4 4.4 %collective-permute-start.7 = (f32[320,256]{1,0:T(8,128)S(1)}, f32[320,256]{1,0:T(8,128)S(1)}, u32[]{:S(2)}, u32[]{:S(2)}) collective-permute-start(f32[320,256]{1,0:T(8,128)S(1)} %broadcast_select_fusion.6), channel_id=1, source_target_pairs={{0,1},{1,0},{2,3},{3,2},{4,5},{5,4},{6,7},{7,6},{8,9},{9,8},{10,11... | collective-permute-start | bytes 983048 | tf_op jit(solution)/shard_map/ppermute | solution.py:55
  25.1 1.7 %collective-permute-start.3 = (f32[320,256]{1,0:T(8,128)S(1)}, f32[320,256]{1,0:T(8,128)S(1)}, u32[]{:S(2)}, u32[]{:S(2)}) collective-permute-start(f32[320,256]{1,0:T(8,128)S(1)} %broadcast_select_fusion.7), channel_id=1, source_target_pairs={{0,1},{1,0},{2,3},{3,2},{4,5},{5,4},{6,7},{7,6},{8,9},{9,8},{10,11... | collective-permute-start | bytes 983048 | tf_op jit(solution)/shard_map/ppermute | solution.py:55
  25.3 8.8 %collective-permute-start.9 = (f32[512,256]{1,0:T(8,128)S(1)}, f32[512,256]{1,0:T(8,128)S(1)}, u32[]{:S(2)}, u32[]{:S(2)}) collective-permute-start(f32[512,256]{1,0:T(8,128)S(1)} %negate_select_fusion.2), channel_id=1, source_target_pairs={{0,1},{1,0},{2,3},{3,2},{4,5},{5,4},{6,7},{7,6},{8,9},{9,8},{10,11... | collective-permute-start | bytes 1572872 | tf_op jit(solution)/shard_map/ppermute | solution.py:55
  25.9 2.8 %copy-start.1 = (f32[2,2,256,256]{3,2,1,0:T(8,128)S(1)}, f32[2,2,256,256]{3,2,1,0:T(8,128)}, u32[]{:S(2)}) copy-start(f32[2,2,256,256]{3,2,1,0:T(8,128)} %param.10) | copy-start | bytes 3145732
  25.9 5.3 %copy-start = (f32[1024,1024]{1,0:T(8,128)S(1)}, f32[1024,1024]{1,0:T(8,128)}, u32[]{:S(2)}) copy-start(f32[1024,1024]{1,0:T(8,128)} %param.6) | copy-start | bytes 12582916
  29.1 9.8 %collective-permute-start.8 = (f32[256,256]{1,0:T(8,128)S(1)}, f32[256,256]{1,0:T(8,128)S(1)}, u32[]{:S(2)}, u32[]{:S(2)}) collective-permute-start(f32[256,256]{1,0:T(8,128)S(1)} %convolution_bitcast_fusion.23), channel_id=1, source_target_pairs={{0,8},{8,0},{16,24},{24,16},{1,9},{9,1},{17,25},{25,17},{2,10},{10... | collective-permute-start | bytes 786440 | tf_op jit(solution)/shard_map/ppermute | solution.py:51
  34.2 10.1 %collective-permute-start.10 = (f32[512,256]{1,0:T(8,128)S(1)}, f32[512,256]{1,0:T(8,128)S(1)}, u32[]{:S(2)}, u32[]{:S(2)}) collective-permute-start(f32[512,256]{1,0:T(8,128)S(1)} %select_select_fusion), channel_id=1, source_target_pairs={{0,2},{1,5},{2,0},{3,7},{4,6},{5,1},{6,4},{7,3},{8,10},{9,13},{10,... | collective-permute-start | bytes 1572872 | tf_op jit(solution)/shard_map/ppermute | solution.py:114
  36.8 2.0 %copy-start.2 = (f32[2,2,256,256]{3,2,1,0:T(8,128)S(1)}, f32[2,2,256,256]{3,2,1,0:T(8,128)}, u32[]{:S(2)}) copy-start(f32[2,2,256,256]{3,2,1,0:T(8,128)} %param.11) | copy-start | bytes 3145732
  36.8 13.7 %collective-permute-start.14 = (f32[256,256]{0,1:T(8,128)S(1)}, f32[256,256]{0,1:T(8,128)S(1)}, u32[]{:S(2)}, u32[]{:S(2)}) collective-permute-start(f32[256,256]{0,1:T(8,128)S(1)} %convolution_bitcast_fusion.18), channel_id=1, source_target_pairs={{0,8},{8,0},{16,24},{24,16},{1,9},{9,1},{17,25},{25,17},{2,10},{10... | collective-permute-start | bytes 786440 | tf_op jit(solution)/shard_map/ppermute | solution.py:51
  39.5 30.3 %collective-permute-start.13 = (f32[256,256]{1,0:T(8,128)S(1)}, f32[256,256]{1,0:T(8,128)S(1)}, u32[]{:S(2)}, u32[]{:S(2)}) collective-permute-start(f32[256,256]{1,0:T(8,128)S(1)} %convolution_bitcast_fusion.21), channel_id=1, source_target_pairs={{0,16},{8,24},{16,0},{24,8},{1,17},{9,25},{17,1},{25,9},{2,18},{10... | collective-permute-start | bytes 786440 | tf_op jit(solution)/shard_map/ppermute | solution.py:51
  42.6 14.8 %collective-permute-start.16 = (f32[256,256]{1,0:T(8,128)S(1)}, f32[256,256]{1,0:T(8,128)S(1)}, u32[]{:S(2)}, u32[]{:S(2)}) collective-permute-start(f32[256,256]{1,0:T(8,128)S(1)} %negate_select_fusion.4), channel_id=1, source_target_pairs={{0,8},{8,0},{16,24},{24,16},{1,9},{9,1},{17,25},{25,17},{2,10},{10... | collective-permute-start | bytes 786440 | tf_op jit(solution)/shard_map/ppermute | solution.py:51
  44.3 9.2 %collective-permute-start.11 = (f32[512,256]{1,0:T(8,128)S(1)}, f32[512,256]{1,0:T(8,128)S(1)}, u32[]{:S(2)}, u32[]{:S(2)}) collective-permute-start(f32[512,256]{1,0:T(8,128)S(1)} %broadcast_select_fusion), channel_id=1, source_target_pairs={{0,4},{1,3},{2,6},{3,1},{4,0},{5,7},{6,2},{7,5},{8,12},{9,11},{10,... | collective-permute-start | bytes 1572872 | tf_op jit(solution)/shard_map/ppermute | solution.py:114
  46.3 22.1 %collective-permute-start.18 = (f32[256,256]{1,0:T(8,128)S(1)}, f32[256,256]{1,0:T(8,128)S(1)}, u32[]{:S(2)}, u32[]{:S(2)}) collective-permute-start(f32[256,256]{1,0:T(8,128)S(1)} %negate_select_fusion.6), channel_id=1, source_target_pairs={{0,8},{8,0},{16,24},{24,16},{1,9},{9,1},{17,25},{25,17},{2,10},{10... | collective-permute-start | bytes 786440 | tf_op jit(solution)/shard_map/ppermute | solution.py:51
  53.7 7.3 %collective-permute-start.12 = (f32[512,256]{1,0:T(8,128)S(1)}, f32[512,256]{1,0:T(8,128)S(1)}, u32[]{:S(2)}, u32[]{:S(2)}) collective-permute-start(f32[512,256]{1,0:T(8,128)S(1)} %broadcast_select_fusion.1), channel_id=1, source_target_pairs={{0,1},{1,0},{2,3},{3,2},{4,5},{5,4},{6,7},{7,6},{8,9},{9,8},{10,11... | collective-permute-start | bytes 1572872 | tf_op jit(solution)/shard_map/ppermute | solution.py:55
  54.1 20.5 %collective-permute-start.15 = (f32[256,256]{0,1:T(8,128)S(1)}, f32[256,256]{0,1:T(8,128)S(1)}, u32[]{:S(2)}, u32[]{:S(2)}) collective-permute-start(f32[256,256]{0,1:T(8,128)S(1)} %convolution_bitcast_fusion.16), channel_id=1, source_target_pairs={{0,16},{8,24},{16,0},{24,8},{1,17},{9,25},{17,1},{25,9},{2,18},{10... | collective-permute-start | bytes 786440 | tf_op jit(solution)/shard_map/ppermute | solution.py:51
  58.2 23.0 %collective-permute-start.17 = (f32[256,256]{0,1:T(8,128)S(1)}, f32[256,256]{0,1:T(8,128)S(1)}, u32[]{:S(2)}, u32[]{:S(2)}) collective-permute-start(f32[256,256]{0,1:T(8,128)S(1)} %convolution_bitcast_fusion.12), channel_id=1, source_target_pairs={{0,16},{8,24},{16,0},{24,8},{1,17},{9,25},{17,1},{25,9},{2,18},{10... | collective-permute-start | bytes 786440 | tf_op jit(solution)/shard_map/ppermute | solution.py:51
  64.6 24.9 %collective-permute-start.20 = (f32[256,512]{1,0:T(8,128)S(1)}, f32[256,512]{1,0:T(8,128)S(1)}, u32[]{:S(2)}, u32[]{:S(2)}) collective-permute-start(f32[256,512]{1,0:T(8,128)S(1)} %convolution_bitcast_fusion.7), channel_id=1, source_target_pairs={{0,8},{8,0},{16,24},{24,16},{1,9},{9,1},{17,25},{25,17},{2,10},{10... | collective-permute-start | bytes 1572872 | tf_op jit(solution)/shard_map/ppermute | solution.py:51
  69.7 44.2 %collective-permute-start.19 = (f32[256,256]{0,1:T(8,128)S(1)}, f32[256,256]{0,1:T(8,128)S(1)}, u32[]{:S(2)}, u32[]{:S(2)}) collective-permute-start(f32[256,256]{0,1:T(8,128)S(1)} %convolution_bitcast_fusion.9), channel_id=1, source_target_pairs={{0,16},{8,24},{16,0},{24,8},{1,17},{9,25},{17,1},{25,9},{2,18},{10... | collective-permute-start | bytes 786440 | tf_op jit(solution)/shard_map/ppermute | solution.py:51
  90.2 22.2 %collective-permute-start.22 = (f32[256,512]{0,1:T(8,128)S(1)}, f32[256,512]{0,1:T(8,128)S(1)}, u32[]{:S(2)}, u32[]{:S(2)}) collective-permute-start(f32[256,512]{0,1:T(8,128)S(1)} %negate_select_fusion.1), channel_id=1, source_target_pairs={{0,8},{8,0},{16,24},{24,16},{1,9},{9,1},{17,25},{25,17},{2,10},{10... | collective-permute-start | bytes 1572872 | tf_op jit(solution)/shard_map/ppermute | solution.py:51
  91.3 37.1 %collective-permute-start.21 = (f32[256,512]{0,1:T(8,128)S(1)}, f32[256,512]{0,1:T(8,128)S(1)}, u32[]{:S(2)}, u32[]{:S(2)}) collective-permute-start(f32[256,512]{0,1:T(8,128)S(1)} %convolution_bitcast_fusion.5), channel_id=1, source_target_pairs={{0,16},{8,24},{16,0},{24,8},{1,17},{9,25},{17,1},{25,9},{2,18},{10... | collective-permute-start | bytes 1572872 | tf_op jit(solution)/shard_map/ppermute | solution.py:51
  113.4 25.2 %collective-permute-start.23 = (f32[256,512]{0,1:T(8,128)S(1)}, f32[256,512]{0,1:T(8,128)S(1)}, u32[]{:S(2)}, u32[]{:S(2)}) collective-permute-start(f32[256,512]{0,1:T(8,128)S(1)} %convolution_bitcast_fusion.1), channel_id=1, source_target_pairs={{0,16},{8,24},{16,0},{24,8},{1,17},{9,25},{17,1},{25,9},{2,18},{10... | collective-permute-start | bytes 1572872 | tf_op jit(solution)/shard_map/ppermute | solution.py:51
  128.8 9.7 %copy-start.3 = (f32[1024,1024]{1,0:T(8,128)}, f32[1024,1024]{1,0:T(8,128)S(1)}, u32[]{:S(2)}) copy-start(f32[1024,1024]{1,0:T(8,128)S(1)} %fusion.2) | copy-start | bytes 12582916

commit v9 on v7

--- a/solution.py
+++ b/solution.py
@@ -16,7 +16,7 @@
     ("leaf0", "own0.0"),
     ("send0.1", ""),
     ("send0.2", "got0.0"),
-    ("send0.3", "got0.0"),
+    ("send0.3", "got0.1"),
     ("begin1", "arr0.0"),
     ("move1.0", "own0.0"),
     ("move1.1", ""),
@@ -25,7 +25,7 @@
     ("send1.0", ""),
     ("send1.1", "got1.0"),
     ("tree0.0", ""),
-    ("tree0.1", "own0.3"),
+    ("tree0.1", "own0.2"),
     ("tree0.2", ""),
     ("tree0.3", "own1.0"),
     ("tree1.0", ""),

time: 140 us -> 140 us (level)
  starting transfers between devices: 27 us -> 23 us
  waiting for transfers between devices: 82.4 us -> 86 us
    ppermute x12, waiting for transfers between devices: 69.2 us -> 73.5 us  [from_partner(): lax.ppermute(shard, 'row', [(i, i ^ 1 << apart) for i in range(lax.axis_s...]
    ppermute x12, starting transfers between devices: 14.9 us -> 11 us  [from_partner(): lax.ppermute(shard, 'row', [(i, i ^ 1 << apart) for i in range(lax.axis_s...]
  transfers between devices with their start and end apart: 24 -> 24, of which waited for: 15 -> 14; matrix products, arithmetic and copies ran while one was open for 18% -> 18% of each run, Pallas kernels for 0% -> 0%
where the time goes in v9:
time: 140 us
  waiting for transfers between devices  86 us (61%)
  starting transfers between devices  23 us (16%)
  matrix products  21.4 us (15%)
  local copies, waits for them, and re-layouts  4.34 us (3%)
  other arithmetic  3 us (2%)
  between operations  2.01 us (1%)
    ppermute x12, waiting for transfers between devices, from_partner(): lax.ppermute(shard, 'row', [(i, i ^ 1 << apart) for i in range(lax.axis_s...  73.5 us
    dot_general x18, matrix products, dot_t(): lax.dot_general(a, b, LEADING, precision=PRECISION, preferred_element_typ...  12 us
    ppermute x6, waiting for transfers between devices, exchange(): self.arrived = [lax.ppermute(c, 'col', pairs) for c in self.current]  11.3 us
    ppermute x12, starting transfers between devices, from_partner(): lax.ppermute(shard, 'row', [(i, i ^ 1 << apart) for i in range(lax.axis_s...  11 us
    ppermute x6, starting transfers between devices, exchange(): self.arrived = [lax.ppermute(c, 'col', pairs) for c in self.current]  10.7 us
    dot_general x17, matrix products, dot(): jnp.dot(a, b, precision=PRECISION, preferred_element_type=jnp.float32)  9.46 us
  transfers between devices with their start and end apart: 24, of which 14 were waited for; matrix products, arithmetic and copies ran while one was open for 18% of the time, Pallas kernels for 0%

profile of v9, /device:TPU:0, one launch (start us, length us, event | category | flops | bytes accessed | tf_op | source)
XLA Modules:
  0.0 139.9 jit_solution(6950898870410498348)
XLA Ops:
  0.0 1.1 slice_bitcast_fusion.5
  1.1 1.3 slice_bitcast_fusion.1
  4.9 2.9 %collective-permute-start.5 = (f32[320,256]{1,0:T(8,128)S(1)}, f32[320,256]{1,0:T(8,128)S(1)}, u32[]{:S(2)}, u32[]{:S(2)}) collective-permute-start(f32[320,256]{1,0:T(8,128)S(1)} %get-tuple-element.20), channel_id=1, source_target_pairs={{0,2},{1,5},{2,0},{3,7},{4,6},{5,1},{6,4},{7,3},{8,10},{9,13},{10,... | collective-permute-start | bytes 983048 | tf_op jit(solution)/shard_map/ppermute | solution.py:114
  7.9 1.2 slice_bitcast_fusion.3
  9.8 3.1 %collective-permute-done.5 = f32[320,256]{1,0:T(8,128)S(1)} collective-permute-done((f32[320,256]{1,0:T(8,128)S(1)}, f32[320,256]{1,0:T(8,128)S(1)}, u32[]{:S(2)}, u32[]{:S(2)}) %collective-permute-start.5) | collective-permute-done | bytes 327712 | tf_op jit(solution)/shard_map/ppermute | solution.py:114
  12.9 2.1 %collective-permute-start.6 = (f32[320,256]{1,0:T(8,128)S(1)}, f32[320,256]{1,0:T(8,128)S(1)}, u32[]{:S(2)}, u32[]{:S(2)}) collective-permute-start(f32[320,256]{1,0:T(8,128)S(1)} %broadcast_select_fusion.4), channel_id=1, source_target_pairs={{0,4},{1,3},{2,6},{3,1},{4,0},{5,7},{6,2},{7,5},{8,12},{9,11},{10,... | collective-permute-start | bytes 983048 | tf_op jit(solution)/shard_map/ppermute | solution.py:114
  15.1 2.5 %collective-permute-done.1 = f32[320,256]{1,0:T(8,128)S(1)} collective-permute-done((f32[320,256]{1,0:T(8,128)S(1)}, f32[320,256]{1,0:T(8,128)S(1)}, u32[]{:S(2)}, u32[]{:S(2)}) %collective-permute-start.1) | collective-permute-done | bytes 327712 | tf_op jit(solution)/shard_map/ppermute | solution.py:114
  17.6 2.4 %collective-permute-start.2 = (f32[320,256]{1,0:T(8,128)S(1)}, f32[320,256]{1,0:T(8,128)S(1)}, u32[]{:S(2)}, u32[]{:S(2)}) collective-permute-start(f32[320,256]{1,0:T(8,128)S(1)} %broadcast_select_fusion.5), channel_id=1, source_target_pairs={{0,4},{1,3},{2,6},{3,1},{4,0},{5,7},{6,2},{7,5},{8,12},{9,11},{10,... | collective-permute-start | bytes 983048 | tf_op jit(solution)/shard_map/ppermute | solution.py:114
  20.0 1.3 negate_select_fusion
  21.5 3.6 %collective-permute-done.2 = f32[320,256]{1,0:T(8,128)S(1)} collective-permute-done((f32[320,256]{1,0:T(8,128)S(1)}, f32[320,256]{1,0:T(8,128)S(1)}, u32[]{:S(2)}, u32[]{:S(2)}) %collective-permute-start.2) | collective-permute-done | bytes 327712 | tf_op jit(solution)/shard_map/ppermute | solution.py:114
  25.9 0.9 collective-permute-done.3
  26.9 1.0 fusion.117
  29.1 2.1 %collective-permute-start.12 = (f32[256,256]{1,0:T(8,128)S(1)}, f32[256,256]{1,0:T(8,128)S(1)}, u32[]{:S(2)}, u32[]{:S(2)}) collective-permute-start(f32[256,256]{1,0:T(8,128)S(1)} %convolution_bitcast_fusion.23), channel_id=1, source_target_pairs={{0,8},{8,0},{16,24},{24,16},{1,9},{9,1},{17,25},{25,17},{2,10},{10... | collective-permute-start | bytes 786440 | tf_op jit(solution)/shard_map/ppermute | solution.py:51
  31.2 2.1 %fusion.118 = f32[256,1024]{1,0:T(8,128)S(1)} fusion(f32[1024,256]{1,0:T(8,128)S(1)} %fusion.18, f32[1024,1024]{1,0:T(8,128)S(1)} %copy-done), kind=kOutput, calls=%fused_computation.189 | convolution fusion | flops 1610612736 | bytes 6291456 | tf_op jit(solution)/shard_map/dot_general | solution.py:47
  34.2 1.6 %collective-permute-start.9 = (f32[512,256]{1,0:T(8,128)S(1)}, f32[512,256]{1,0:T(8,128)S(1)}, u32[]{:S(2)}, u32[]{:S(2)}) collective-permute-start(f32[512,256]{1,0:T(8,128)S(1)} %select_select_fusion), channel_id=1, source_target_pairs={{0,2},{1,5},{2,0},{3,7},{4,6},{5,1},{6,4},{7,3},{8,10},{9,13},{10,... | collective-permute-start | bytes 1572872 | tf_op jit(solution)/shard_map/ppermute | solution.py:114
  37.3 1.5 %slice_subtract_fusion = f32[768,1024]{1,0:T(8,128)S(1)} fusion(f32[1024,1024]{1,0:T(8,128)S(1)} %copy-done, f32[256,1024]{1,0:T(8,128)S(1)} %fusion.89, f32[1024,256]{1,0:T(8,128)S(1)} %fusion.18), kind=kOutput, calls=%fused_computation.1 | convolution fusion | flops 1208745984 | bytes 8126464 | tf_op jit(solution)/shard_map/dot_general | solution.py:43
  39.5 2.7 %collective-permute-start.13 = (f32[256,256]{0,1:T(8,128)S(1)}, f32[256,256]{0,1:T(8,128)S(1)}, u32[]{:S(2)}, u32[]{:S(2)}) collective-permute-start(f32[256,256]{0,1:T(8,128)S(1)} %convolution_bitcast_fusion.21), channel_id=1, source_target_pairs={{0,16},{8,24},{16,0},{24,8},{1,17},{9,25},{17,1},{25,9},{2,18},{10... | collective-permute-start | bytes 786440 | tf_op jit(solution)/shard_map/ppermute | solution.py:51
  42.6 1.6 %collective-permute-start.16 = (f32[256,256]{1,0:T(8,128)S(1)}, f32[256,256]{1,0:T(8,128)S(1)}, u32[]{:S(2)}, u32[]{:S(2)}) collective-permute-start(f32[256,256]{1,0:T(8,128)S(1)} %negate_select_fusion.6), channel_id=1, source_target_pairs={{0,8},{8,0},{16,24},{24,16},{1,9},{9,1},{17,25},{25,17},{2,10},{10... | collective-permute-start | bytes 786440 | tf_op jit(solution)/shard_map/ppermute | solution.py:51
  44.4 1.6 %collective-permute-start.10 = (f32[512,256]{1,0:T(8,128)S(1)}, f32[512,256]{1,0:T(8,128)S(1)}, u32[]{:S(2)}, u32[]{:S(2)}) collective-permute-start(f32[512,256]{1,0:T(8,128)S(1)} %broadcast_select_fusion), channel_id=1, source_target_pairs={{0,4},{1,3},{2,6},{3,1},{4,0},{5,7},{6,2},{7,5},{8,12},{9,11},{10,... | collective-permute-start | bytes 1572872 | tf_op jit(solution)/shard_map/ppermute | solution.py:114
  45.9 4.5 %collective-permute-done.14 = f32[256,256]{0,1:T(8,128)S(1)} collective-permute-done((f32[256,256]{0,1:T(8,128)S(1)}, f32[256,256]{0,1:T(8,128)S(1)}, u32[]{:S(2)}, u32[]{:S(2)}) %collective-permute-start.14) | collective-permute-done | bytes 262176 | tf_op jit(solution)/shard_map/ppermute | solution.py:51
  51.5 2.1 %collective-permute-done.10 = f32[512,256]{1,0:T(8,128)S(1)} collective-permute-done((f32[512,256]{1,0:T(8,128)S(1)}, f32[512,256]{1,0:T(8,128)S(1)}, u32[]{:S(2)}, u32[]{:S(2)}) %collective-permute-start.10) | collective-permute-done | bytes 524320 | tf_op jit(solution)/shard_map/ppermute | solution.py:114
  54.7 7.1 %collective-permute-done.16 = f32[256,256]{1,0:T(8,128)S(1)} collective-permute-done((f32[256,256]{1,0:T(8,128)S(1)}, f32[256,256]{1,0:T(8,128)S(1)}, u32[]{:S(2)}, u32[]{:S(2)}) %collective-permute-start.16) | collective-permute-done | bytes 262176 | tf_op jit(solution)/shard_map/ppermute | solution.py:51
  62.9 1.7 %fusion.19 = f32[256,1024]{1,0:T(8,128)S(1)} fusion(f32[768,1024]{1,0:T(8,128)S(1)} %slice_subtract_fusion, f32[384,256]{1,0:T(8,128)S(1)} %slice.291, f32[384,256]{1,0:T(8,128)S(1)} %slice.290), kind=kOutput, calls=%fused_computation.53 | convolution fusion | flops 1208156160 | bytes 4980736 | tf_op jit(solution)/shard_map/dot_general | solution.py:47
  66.4 1.1 slice_subtract_fusion.1
  67.5 5.5 %collective-permute-done.18 = f32[256,256]{0,1:T(8,128)S(1)} collective-permute-done((f32[256,256]{0,1:T(8,128)S(1)}, f32[256,256]{0,1:T(8,128)S(1)}, u32[]{:S(2)}, u32[]{:S(2)}) %collective-permute-start.18) | collective-permute-done | bytes 262176 | tf_op jit(solution)/shard_map/ppermute | solution.py:51
  75.1 2.0 %collective-permute-done.17 = f32[256,256]{0,1:T(8,128)S(1)} collective-permute-done((f32[256,256]{0,1:T(8,128)S(1)}, f32[256,256]{0,1:T(8,128)S(1)}, u32[]{:S(2)}, u32[]{:S(2)}) %collective-permute-start.17) | collective-permute-done | bytes 262176 | tf_op jit(solution)/shard_map/ppermute | solution.py:51
  77.5 12.2 %collective-permute-done.20 = f32[256,512]{1,0:T(8,128)S(1)} collective-permute-done((f32[256,512]{1,0:T(8,128)S(1)}, f32[256,512]{1,0:T(8,128)S(1)}, u32[]{:S(2)}, u32[]{:S(2)}) %collective-permute-start.20) | collective-permute-done | bytes 524320 | tf_op jit(solution)/shard_map/ppermute | solution.py:51
  91.4 3.1 %collective-permute-start.21 = (f32[256,512]{0,1:T(8,128)S(1)}, f32[256,512]{0,1:T(8,128)S(1)}, u32[]{:S(2)}, u32[]{:S(2)}) collective-permute-start(f32[256,512]{0,1:T(8,128)S(1)} %convolution_bitcast_fusion.5), channel_id=1, source_target_pairs={{0,16},{8,24},{16,0},{24,8},{1,17},{9,25},{17,1},{25,9},{2,18},{10... | collective-permute-start | bytes 1572872 | tf_op jit(solution)/shard_map/ppermute | solution.py:51
  94.5 18.2 %collective-permute-done.22 = f32[256,512]{0,1:T(8,128)S(1)} collective-permute-done((f32[256,512]{0,1:T(8,128)S(1)}, f32[256,512]{0,1:T(8,128)S(1)}, u32[]{:S(2)}, u32[]{:S(2)}) %collective-permute-start.22) | collective-permute-done | bytes 524320 | tf_op jit(solution)/shard_map/ppermute | solution.py:51
  114.2 14.6 %collective-permute-done.21 = f32[256,512]{0,1:T(8,128)S(1)} collective-permute-done((f32[256,512]{0,1:T(8,128)S(1)}, f32[256,512]{0,1:T(8,128)S(1)}, u32[]{:S(2)}, u32[]{:S(2)}) %collective-permute-start.21) | collective-permute-done | bytes 524320 | tf_op jit(solution)/shard_map/ppermute | solution.py:51
  129.2 9.5 %collective-permute-done.23 = f32[256,512]{0,1:T(8,128)S(1)} collective-permute-done((f32[256,512]{0,1:T(8,128)S(1)}, f32[256,512]{0,1:T(8,128)S(1)}, u32[]{:S(2)}, u32[]{:S(2)}) %collective-permute-start.23) | collective-permute-done | bytes 524320 | tf_op jit(solution)/shard_map/ppermute | solution.py:51
  138.6 1.2 fusion.5
  (95 shorter events, 18.5 us)
Async XLA Ops:
  0.0 3.2 %copy-start.4 = (s32[2]{0:T(128)S(1)}, s32[2]{0:T(128)}, u32[]{:S(2)}) copy-start(s32[2]{0:T(128)} %param.7) | copy-start | bytes 28
  2.6 1.9 %collective-permute-start = (f32[320,256]{1,0:T(8,128)S(1)}, f32[320,256]{1,0:T(8,128)S(1)}, u32[]{:S(2)}, u32[]{:S(2)}) collective-permute-start(f32[320,256]{1,0:T(8,128)S(1)} %get-tuple-element.21), channel_id=1, source_target_pairs={{0,1},{1,0},{2,3},{3,2},{4,5},{5,4},{6,7},{7,6},{8,9},{9,8},{10,11... | collective-permute-start | bytes 983048 | tf_op jit(solution)/shard_map/ppermute | solution.py:55
  3.1 1.7 %collective-permute-start.4 = (f32[320,256]{1,0:T(8,128)S(1)}, f32[320,256]{1,0:T(8,128)S(1)}, u32[]{:S(2)}, u32[]{:S(2)}) collective-permute-start(f32[320,256]{1,0:T(8,128)S(1)} %get-tuple-element.22), channel_id=1, source_target_pairs={{0,1},{1,0},{2,3},{3,2},{4,5},{5,4},{6,7},{7,6},{8,9},{9,8},{10,11... | collective-permute-start | bytes 983048 | tf_op jit(solution)/shard_map/ppermute | solution.py:55
  4.9 8.0 %collective-permute-start.5 = (f32[320,256]{1,0:T(8,128)S(1)}, f32[320,256]{1,0:T(8,128)S(1)}, u32[]{:S(2)}, u32[]{:S(2)}) collective-permute-start(f32[320,256]{1,0:T(8,128)S(1)} %get-tuple-element.20), channel_id=1, source_target_pairs={{0,2},{1,5},{2,0},{3,7},{4,6},{5,1},{6,4},{7,3},{8,10},{9,13},{10,... | collective-permute-start | bytes 983048 | tf_op jit(solution)/shard_map/ppermute | solution.py:114
  7.8 9.7 %collective-permute-start.1 = (f32[320,256]{1,0:T(8,128)S(1)}, f32[320,256]{1,0:T(8,128)S(1)}, u32[]{:S(2)}, u32[]{:S(2)}) collective-permute-start(f32[320,256]{1,0:T(8,128)S(1)} %get-tuple-element.19), channel_id=1, source_target_pairs={{0,2},{1,5},{2,0},{3,7},{4,6},{5,1},{6,4},{7,3},{8,10},{9,13},{10,... | collective-permute-start | bytes 983048 | tf_op jit(solution)/shard_map/ppermute | solution.py:114
  12.9 8.4 %collective-permute-start.6 = (f32[320,256]{1,0:T(8,128)S(1)}, f32[320,256]{1,0:T(8,128)S(1)}, u32[]{:S(2)}, u32[]{:S(2)}) collective-permute-start(f32[320,256]{1,0:T(8,128)S(1)} %broadcast_select_fusion.4), channel_id=1, source_target_pairs={{0,4},{1,3},{2,6},{3,1},{4,0},{5,7},{6,2},{7,5},{8,12},{9,11},{10,... | collective-permute-start | bytes 983048 | tf_op jit(solution)/shard_map/ppermute | solution.py:114
  17.6 7.5 %collective-permute-start.2 = (f32[320,256]{1,0:T(8,128)S(1)}, f32[320,256]{1,0:T(8,128)S(1)}, u32[]{:S(2)}, u32[]{:S(2)}) collective-permute-start(f32[320,256]{1,0:T(8,128)S(1)} %broadcast_select_fusion.5), channel_id=1, source_target_pairs={{0,4},{1,3},{2,6},{3,1},{4,0},{5,7},{6,2},{7,5},{8,12},{9,11},{10,... | collective-permute-start | bytes 983048 | tf_op jit(solution)/shard_map/ppermute | solution.py:114
  21.4 4.4 %collective-permute-start.7 = (f32[320,256]{1,0:T(8,128)S(1)}, f32[320,256]{1,0:T(8,128)S(1)}, u32[]{:S(2)}, u32[]{:S(2)}) collective-permute-start(f32[320,256]{1,0:T(8,128)S(1)} %broadcast_select_fusion.6), channel_id=1, source_target_pairs={{0,1},{1,0},{2,3},{3,2},{4,5},{5,4},{6,7},{7,6},{8,9},{9,8},{10,11... | collective-permute-start | bytes 983048 | tf_op jit(solution)/shard_map/ppermute | solution.py:55
  25.1 1.7 %collective-permute-start.3 = (f32[320,256]{1,0:T(8,128)S(1)}, f32[320,256]{1,0:T(8,128)S(1)}, u32[]{:S(2)}, u32[]{:S(2)}) collective-permute-start(f32[320,256]{1,0:T(8,128)S(1)} %broadcast_select_fusion.7), channel_id=1, source_target_pairs={{0,1},{1,0},{2,3},{3,2},{4,5},{5,4},{6,7},{7,6},{8,9},{9,8},{10,11... | collective-permute-start | bytes 983048 | tf_op jit(solution)/shard_map/ppermute | solution.py:55
  25.3 8.8 %collective-permute-start.8 = (f32[512,256]{1,0:T(8,128)S(1)}, f32[512,256]{1,0:T(8,128)S(1)}, u32[]{:S(2)}, u32[]{:S(2)}) collective-permute-start(f32[512,256]{1,0:T(8,128)S(1)} %negate_select_fusion.2), channel_id=1, source_target_pairs={{0,1},{1,0},{2,3},{3,2},{4,5},{5,4},{6,7},{7,6},{8,9},{9,8},{10,11... | collective-permute-start | bytes 1572872 | tf_op jit(solution)/shard_map/ppermute | solution.py:55
  25.9 2.8 %copy-start.1 = (f32[2,2,256,256]{3,2,1,0:T(8,128)S(1)}, f32[2,2,256,256]{3,2,1,0:T(8,128)}, u32[]{:S(2)}) copy-start(f32[2,2,256,256]{3,2,1,0:T(8,128)} %param.10) | copy-start | bytes 3145732
  25.9 5.3 %copy-start = (f32[1024,1024]{1,0:T(8,128)S(1)}, f32[1024,1024]{1,0:T(8,128)}, u32[]{:S(2)}) copy-start(f32[1024,1024]{1,0:T(8,128)} %param.6) | copy-start | bytes 12582916
  29.1 9.8 %collective-permute-start.12 = (f32[256,256]{1,0:T(8,128)S(1)}, f32[256,256]{1,0:T(8,128)S(1)}, u32[]{:S(2)}, u32[]{:S(2)}) collective-permute-start(f32[256,256]{1,0:T(8,128)S(1)} %convolution_bitcast_fusion.23), channel_id=1, source_target_pairs={{0,8},{8,0},{16,24},{24,16},{1,9},{9,1},{17,25},{25,17},{2,10},{10... | collective-permute-start | bytes 786440 | tf_op jit(solution)/shard_map/ppermute | solution.py:51
  34.2 10.1 %collective-permute-start.9 = (f32[512,256]{1,0:T(8,128)S(1)}, f32[512,256]{1,0:T(8,128)S(1)}, u32[]{:S(2)}, u32[]{:S(2)}) collective-permute-start(f32[512,256]{1,0:T(8,128)S(1)} %select_select_fusion), channel_id=1, source_target_pairs={{0,2},{1,5},{2,0},{3,7},{4,6},{5,1},{6,4},{7,3},{8,10},{9,13},{10,... | collective-permute-start | bytes 1572872 | tf_op jit(solution)/shard_map/ppermute | solution.py:114
  36.8 2.0 %copy-start.2 = (f32[2,2,256,256]{3,2,1,0:T(8,128)S(1)}, f32[2,2,256,256]{3,2,1,0:T(8,128)}, u32[]{:S(2)}) copy-start(f32[2,2,256,256]{3,2,1,0:T(8,128)} %param.11) | copy-start | bytes 3145732
  36.8 13.7 %collective-permute-start.14 = (f32[256,256]{0,1:T(8,128)S(1)}, f32[256,256]{0,1:T(8,128)S(1)}, u32[]{:S(2)}, u32[]{:S(2)}) collective-permute-start(f32[256,256]{0,1:T(8,128)S(1)} %convolution_bitcast_fusion.18), channel_id=1, source_target_pairs={{0,8},{8,0},{16,24},{24,16},{1,9},{9,1},{17,25},{25,17},{2,10},{10... | collective-permute-start | bytes 786440 | tf_op jit(solution)/shard_map/ppermute | solution.py:51
  39.5 34.9 %collective-permute-start.13 = (f32[256,256]{0,1:T(8,128)S(1)}, f32[256,256]{0,1:T(8,128)S(1)}, u32[]{:S(2)}, u32[]{:S(2)}) collective-permute-start(f32[256,256]{0,1:T(8,128)S(1)} %convolution_bitcast_fusion.21), channel_id=1, source_target_pairs={{0,16},{8,24},{16,0},{24,8},{1,17},{9,25},{17,1},{25,9},{2,18},{10... | collective-permute-start | bytes 786440 | tf_op jit(solution)/shard_map/ppermute | solution.py:51
  42.6 19.1 %collective-permute-start.16 = (f32[256,256]{1,0:T(8,128)S(1)}, f32[256,256]{1,0:T(8,128)S(1)}, u32[]{:S(2)}, u32[]{:S(2)}) collective-permute-start(f32[256,256]{1,0:T(8,128)S(1)} %negate_select_fusion.6), channel_id=1, source_target_pairs={{0,8},{8,0},{16,24},{24,16},{1,9},{9,1},{17,25},{25,17},{2,10},{10... | collective-permute-start | bytes 786440 | tf_op jit(solution)/shard_map/ppermute | solution.py:51
  44.4 9.2 %collective-permute-start.10 = (f32[512,256]{1,0:T(8,128)S(1)}, f32[512,256]{1,0:T(8,128)S(1)}, u32[]{:S(2)}, u32[]{:S(2)}) collective-permute-start(f32[512,256]{1,0:T(8,128)S(1)} %broadcast_select_fusion), channel_id=1, source_target_pairs={{0,4},{1,3},{2,6},{3,1},{4,0},{5,7},{6,2},{7,5},{8,12},{9,11},{10,... | collective-permute-start | bytes 1572872 | tf_op jit(solution)/shard_map/ppermute | solution.py:114
  51.3 23.5 %collective-permute-start.15 = (f32[256,256]{0,1:T(8,128)S(1)}, f32[256,256]{0,1:T(8,128)S(1)}, u32[]{:S(2)}, u32[]{:S(2)}) collective-permute-start(f32[256,256]{0,1:T(8,128)S(1)} %convolution_bitcast_fusion.16), channel_id=1, source_target_pairs={{0,16},{8,24},{16,0},{24,8},{1,17},{9,25},{17,1},{25,9},{2,18},{10... | collective-permute-start | bytes 786440 | tf_op jit(solution)/shard_map/ppermute | solution.py:51
  53.7 9.0 %collective-permute-start.11 = (f32[512,256]{1,0:T(8,128)S(1)}, f32[512,256]{1,0:T(8,128)S(1)}, u32[]{:S(2)}, u32[]{:S(2)}) collective-permute-start(f32[512,256]{1,0:T(8,128)S(1)} %broadcast_select_fusion.1), channel_id=1, source_target_pairs={{0,1},{1,0},{2,3},{3,2},{4,5},{5,4},{6,7},{7,6},{8,9},{9,8},{10,11... | collective-permute-start | bytes 1572872 | tf_op jit(solution)/shard_map/ppermute | solution.py:55
  54.1 18.8 %collective-permute-start.18 = (f32[256,256]{0,1:T(8,128)S(1)}, f32[256,256]{0,1:T(8,128)S(1)}, u32[]{:S(2)}, u32[]{:S(2)}) collective-permute-start(f32[256,256]{0,1:T(8,128)S(1)} %negate_select_fusion.4), channel_id=1, source_target_pairs={{0,8},{8,0},{16,24},{24,16},{1,9},{9,1},{17,25},{25,17},{2,10},{10... | collective-permute-start | bytes 786440 | tf_op jit(solution)/shard_map/ppermute | solution.py:51
  62.6 14.6 %collective-permute-start.17 = (f32[256,256]{0,1:T(8,128)S(1)}, f32[256,256]{0,1:T(8,128)S(1)}, u32[]{:S(2)}, u32[]{:S(2)}) collective-permute-start(f32[256,256]{0,1:T(8,128)S(1)} %convolution_bitcast_fusion.13), channel_id=1, source_target_pairs={{0,16},{8,24},{16,0},{24,8},{1,17},{9,25},{17,1},{25,9},{2,18},{10... | collective-permute-start | bytes 786440 | tf_op jit(solution)/shard_map/ppermute | solution.py:51
  66.4 23.3 %collective-permute-start.20 = (f32[256,512]{1,0:T(8,128)S(1)}, f32[256,512]{1,0:T(8,128)S(1)}, u32[]{:S(2)}, u32[]{:S(2)}) collective-permute-start(f32[256,512]{1,0:T(8,128)S(1)} %convolution_bitcast_fusion.7), channel_id=1, source_target_pairs={{0,8},{8,0},{16,24},{24,16},{1,9},{9,1},{17,25},{25,17},{2,10},{10... | collective-permute-start | bytes 1572872 | tf_op jit(solution)/shard_map/ppermute | solution.py:51
  74.4 39.5 %collective-permute-start.19 = (f32[256,256]{0,1:T(8,128)S(1)}, f32[256,256]{0,1:T(8,128)S(1)}, u32[]{:S(2)}, u32[]{:S(2)}) collective-permute-start(f32[256,256]{0,1:T(8,128)S(1)} %convolution_bitcast_fusion.9), channel_id=1, source_target_pairs={{0,16},{8,24},{16,0},{24,8},{1,17},{9,25},{17,1},{25,9},{2,18},{10... | collective-permute-start | bytes 786440 | tf_op jit(solution)/shard_map/ppermute | solution.py:51
  90.3 22.4 %collective-permute-start.22 = (f32[256,512]{0,1:T(8,128)S(1)}, f32[256,512]{0,1:T(8,128)S(1)}, u32[]{:S(2)}, u32[]{:S(2)}) collective-permute-start(f32[256,512]{0,1:T(8,128)S(1)} %negate_select_fusion.1), channel_id=1, source_target_pairs={{0,8},{8,0},{16,24},{24,16},{1,9},{9,1},{17,25},{25,17},{2,10},{10... | collective-permute-start | bytes 1572872 | tf_op jit(solution)/shard_map/ppermute | solution.py:51
  91.4 37.3 %collective-permute-start.21 = (f32[256,512]{0,1:T(8,128)S(1)}, f32[256,512]{0,1:T(8,128)S(1)}, u32[]{:S(2)}, u32[]{:S(2)}) collective-permute-start(f32[256,512]{0,1:T(8,128)S(1)} %convolution_bitcast_fusion.5), channel_id=1, source_target_pairs={{0,16},{8,24},{16,0},{24,8},{1,17},{9,25},{17,1},{25,9},{2,18},{10... | collective-permute-start | bytes 1572872 | tf_op jit(solution)/shard_map/ppermute | solution.py:51
  113.7 24.9 %collective-permute-start.23 = (f32[256,512]{0,1:T(8,128)S(1)}, f32[256,512]{0,1:T(8,128)S(1)}, u32[]{:S(2)}, u32[]{:S(2)}) collective-permute-start(f32[256,512]{0,1:T(8,128)S(1)} %convolution_bitcast_fusion.1), channel_id=1, source_target_pairs={{0,16},{8,24},{16,0},{24,8},{1,17},{9,25},{17,1},{25,9},{2,18},{10... | collective-permute-start | bytes 1572872 | tf_op jit(solution)/shard_map/ppermute | solution.py:51
  129.2 9.5 %copy-start.3 = (f32[1024,1024]{1,0:T(8,128)}, f32[1024,1024]{1,0:T(8,128)S(1)}, u32[]{:S(2)}) copy-start(f32[1024,1024]{1,0:T(8,128)S(1)} %fusion.2) | copy-start | bytes 12582916
